TPU v7x, 256 devices: a whole 4x4x8 slice. The times are simulated.
256 devices in a mesh: section: 8 (over x, core), dp: 32 (over y, z).
Axes of the slice: x: 4, y: 4, z: 8, core: 2. Of those that a mesh axis runs over, the one named last changes fastest.
Arguments:
- section_inputs: bfloat16 [8, 8, 1024, 8192], P('section', None, 'dp'), may hold values from -6 to 6
- adapter_down: bfloat16 [8, 8192, 128], P('section'), may hold values from -0.0625 to 0.0625
- adapter_up: bfloat16 [8, 8192, 128], P('section'), may hold values from -0.5 to 0.5
- representation: bfloat16 [8, 1024, 8192], P('section', 'dp'), may hold values from -6 to 6
- head_weights: bfloat16 [8192, 128], P('dp'), may hold values from -1 to 1
- head_targets: bfloat16 [8, 1024, 128], P('section', 'dp'), may hold values from -40 to 40
- head_task: int32 [8, 1], replicated, may hold values from 0 to 5
Outputs:
- down_grads: float32 [8, 8192, 128], P('section', 'dp')
- up_grads: float32 [8, 8192, 128], P('section', 'dp')
- task_weights: float32 [6], replicated
Inputs may be any that keep to these rules, and one draw needn't show every extreme that they name: `head_task`: each head belongs to one task, and every task has at least one head.
All inputs are finite; a program needn't handle non-finite values.
Results may differ from a plain program's by a relative error of at most 0.022.
Values may be sent and summed in bfloat16 or wider, within the bound.
No kernel may reach another device: no remote copies, remote signals or barrier semaphores. Data moves between devices by JAX's collectives and lax.ppermute only.
A program may use at most 64 MiB of HBM per device.

v0:
```python
import jax
import jax.numpy as jnp
from jax import lax
from jax.sharding import PartitionSpec as P

HEAD_OUT = 16
TASKS = 6
STEPS = 20


STEP_RATE = 3.0


def from_behind(value, axis, steps):
    count = lax.axis_size(axis)
    first, last = (max(0, -steps), min(count, count - steps))
    return lax.ppermute(value, axis, [(source, source + steps) for source in range(first, last)])


def swish_slope(preact):
    logistic = jax.nn.sigmoid(preact)
    return logistic * (1.0 + preact * (1.0 - logistic))


def section_back(inputs, down_map, up_map, cotangent):
    preact = jnp.dot(inputs, down_map, preferred_element_type=jnp.float32)
    active = jax.nn.silu(preact).astype(jnp.bfloat16)
    branch = jnp.dot(cotangent, up_map, preferred_element_type=jnp.float32)
    inner = (branch * swish_slope(preact)).astype(jnp.bfloat16)
    back = lax.dot_general(
        inner, down_map, (((1,), (1,)), ((), ())), preferred_element_type=jnp.float32
    )
    passed = (cotangent.astype(jnp.float32) + back).astype(jnp.bfloat16)
    return (active, inner, passed)


def store_row(buffer, value, index, valid):
    previous = lax.dynamic_index_in_dim(buffer, index, 0, keepdims=False)
    chosen = jnp.where(valid, value, previous)
    return lax.dynamic_update_index_in_dim(buffer, chosen, index, 0)


def descend(gram_matrix):
    trace_sum = jnp.trace(gram_matrix) + 1e-06
    start = jnp.full((TASKS,), 1.0 / TASKS, dtype=jnp.float32)

    def advance(counter, weights):
        descent = jnp.dot(gram_matrix, weights, precision=lax.Precision.HIGHEST) / trace_sum
        weights = weights * jnp.exp(-STEP_RATE * descent)
        return weights / jnp.sum(weights)

    return lax.fori_loop(0, STEPS, advance, start)


def body(
    section_inputs, adapter_down, adapter_up, representation, head_weights, head_targets, head_task
):
    sections = lax.axis_size("section")
    my_section = lax.axis_index("section")
    micro_count = section_inputs.shape[1]
    tok_rows = section_inputs.shape[2]
    dim_model = section_inputs.shape[3]
    rank_width = adapter_down.shape[2]
    saved = section_inputs[0]
    down_map = adapter_down[0]
    up_map = adapter_up[0]
    weights = lax.all_gather(head_weights, "dp", axis=0, tiled=True)
    predicted = jnp.dot(representation[0], weights, preferred_element_type=jnp.float32)
    residual = (predicted - head_targets[0].astype(jnp.float32)).astype(jnp.bfloat16)
    column_task = jnp.repeat(head_task[:, 0], HEAD_OUT)
    onehot = (column_task[None, :] == jnp.arange(TASKS, dtype=jnp.int32)[:, None]).astype(
        jnp.float32
    )
    masked = residual[None, :, :] * onehot.astype(jnp.bfloat16)[:, None, :]
    task_grads = jnp.einsum("atc,dc->atd", masked, weights, preferred_element_type=jnp.float32)
    partial_gram = jnp.einsum(
        "atd,btd->ab", task_grads, task_grads, precision=lax.Precision.HIGHEST
    )
    gram_matrix = lax.psum(partial_gram, ("section", "dp"))
    mixing = descend(gram_matrix)
    column_weight = jnp.dot(mixing, onehot, precision=lax.Precision.HIGHEST)
    weighted = (residual.astype(jnp.float32) * column_weight[None, :]).astype(jnp.bfloat16)
    own_grad = jnp.einsum(
        "tc,dc->td", weighted, weights, preferred_element_type=jnp.float32
    ).astype(jnp.bfloat16)
    cotangents = lax.all_gather(own_grad[None], "section", axis=0, tiled=True)

    def tick(counter, carry):
        incoming, grad_rows, active_rows, inner_rows = carry
        micro_index = counter - (sections - 1 - my_section)
        valid = (micro_index >= 0) & (micro_index < micro_count)
        clipped = jnp.clip(micro_index, 0, micro_count - 1)
        from_heads = lax.dynamic_index_in_dim(cotangents, clipped, 0, keepdims=False)
        current = jnp.where(my_section == sections - 1, from_heads, incoming)
        inputs = lax.dynamic_index_in_dim(saved, clipped, 0, keepdims=False)
        active, inner, passed = section_back(inputs, down_map, up_map, current)
        grad_rows = store_row(grad_rows, current, clipped, valid)
        active_rows = store_row(active_rows, active, clipped, valid)
        inner_rows = store_row(inner_rows, inner, clipped, valid)
        incoming = from_behind(passed, "section", -1)
        return (incoming, grad_rows, active_rows, inner_rows)

    start_carry = (
        jnp.zeros((tok_rows, dim_model), jnp.bfloat16),
        jnp.zeros((micro_count, tok_rows, dim_model), jnp.bfloat16),
        jnp.zeros((micro_count, tok_rows, rank_width), jnp.bfloat16),
        jnp.zeros((micro_count, tok_rows, rank_width), jnp.bfloat16),
    )
    finished = lax.fori_loop(0, micro_count + sections - 1, tick, start_carry)
    grad_rows = finished[1]
    active_rows = finished[2]
    inner_rows = finished[3]
    part_down = jnp.einsum("mtd,mtr->dr", saved, inner_rows, preferred_element_type=jnp.float32)
    part_up = jnp.einsum("mtd,mtr->dr", grad_rows, active_rows, preferred_element_type=jnp.float32)
    shares = lax.psum_scatter(
        jnp.concatenate([part_down, part_up], axis=1).astype(jnp.bfloat16),
        "dp",
        scatter_dimension=0,
        tiled=True,
    ).astype(jnp.float32)
    grad_down = shares[:, :rank_width]
    grad_up = shares[:, rank_width:]
    return (grad_down[None], grad_up[None], mixing)


def solution(mesh):
    in_specs = (
        P("section", None, "dp", None),
        P("section", None, None),
        P("section", None, None),
        P("section", "dp", None),
        P("dp", None),
        P("section", "dp", None),
        P(),
    )
    out_specs = (P("section", "dp", None), P("section", "dp", None), P())
    return jax.shard_map(body, mesh=mesh, in_specs=in_specs, out_specs=out_specs, check_vma=False)
```

profile of v0, /device:TPU:4, one launch (start us, length us, event | category | flops | bytes accessed | tf_op | source)
XLA Modules:
  0.0 765.6 jit_solution(4357182135453760184)
XLA Ops:
  8.8 82.9 %all-gather.4.cloned.1.call-done = bf16[8192,128]{1,0:T(8,128)(2,1)} async-done(((bf16[256,128]{1,0:T(8,128)(2,1)}), bf16[8192,128]{1,0:T(8,128)(2,1)}) %all-gather.4.cloned.1.call-update) | async-done | bytes 2097168 | tf_op jit(solution)/shard_map/all_gather | solution.py:67
  96.3 24.6 %fusion.22 = f32[6,6]{1,0:T(8,128)S(1)} fusion(f32[6,32,8192]{2,1,0:T(8,128)S(1)} %fusion.19), kind=kOutput, calls=%fused_computation.43 | convolution fusion | flops 113246208 | bytes 6291600 | tf_op jit(solution)/shard_map/atd,btd->ab/dot_general | solution.py:76
  120.9 72.7 %psum.7 = f32[6,6]{1,0:T(8,128)S(1)} all-reduce(f32[6,6]{1,0:T(8,128)S(1)} %fusion.22), channel_id=1, replica_groups=mesh['section'=8,'dp'=32] {'section','dp'}, use_global_device_ids=true, to_apply=%region_0.0 | all-reduce | flops 36 | bytes 288 | tf_op jit(solution)/shard_map/psum | solution.py:79
  194.8 28.4 %while.33 = (s32[]{:T(128)}, f32[6]{0:T(128)S(1)}, f32[6,6]{1,0:T(8,128)S(1)}, f32[]{:T(128)}, s32[]{:T(128)}, /*index=5*/s32[]{:T(128)}) while((s32[]{:T(128)}, f32[6]{0:T(128)S(1)}, f32[6,6]{1,0:T(8,128)S(1)}, f32[]{:T(128)}, s32[]{:T(128)}, /*index=5*/s32[]{:T(128)}) %tuple.73), condition=%wide.region_4.5_spmd.clone, body=%wide.region_2.4_spmd.clone.sunk | while | flops 476 | bytes 331 | solution.py:52
  226.9 29.7 %all-gather.6.cloned.1.call-done = bf16[256,8192]{1,0:T(8,128)(2,1)} async-done(((bf16[32,8192]{1,0:T(8,128)(2,1)}), bf16[256,8192]{1,0:T(8,128)(2,1)}) %all-gather.6.cloned.1.call-update) | async-done | bytes 4194320 | tf_op jit(solution)/shard_map/all_gather | solution.py:86
  259.2 263.7 %while.32 = (s32[]{:T(128)}, bf16[32,8192]{1,0:T(8,128)(2,1)S(1)}, bf16[8,32,8192]{2,1,0:T(8,128)(2,1)}, bf16[8,32,128]{2,1,0:T(8,128)(2,1)S(1)}, bf16[8,32,128]...) while((s32[]{:T(128)}, bf16[32,8192]{1,0:T(8,128)(2,1)S(1)}, ...), condition=%wide.region_6.7_spmd, body=%wide.region_5.6_spmd.sunk | while | flops 202702848 | bytes 22661404 | solution.py:109
  268.7 7.0 collective-permute-done
  286.3 7.0 collective-permute-done
  304.0 7.0 collective-permute-done
  321.6 7.0 collective-permute-done
  339.3 7.0 collective-permute-done
  356.9 7.0 collective-permute-done
  370.8 3.7 collective-permute-start
  374.6 7.0 collective-permute-done
  392.2 7.0 collective-permute-done
  406.1 3.7 collective-permute-start
  409.8 7.0 collective-permute-done
  427.5 7.0 collective-permute-done
  445.1 7.0 collective-permute-done
  462.8 7.0 collective-permute-done
  480.5 7.0 collective-permute-done
  498.2 7.0 collective-permute-done
  515.9 7.0 collective-permute-done
  529.5 227.1 %reduce-scatter.2.cloned.1.call-done = bf16[256,256]{0,1:T(8,128)(2,1)} async-done(((bf16[8192,256]{0,1:T(8,128)(2,1)}), bf16[256,256]{0,1:T(8,128)(2,1)}) %reduce-scatter.2.cloned.1.call-update) | async-done | bytes 131088 | tf_op jit(solution)/shard_map/reduce_scatter | solution.py:115
  (207 shorter events, 200.8 us)
Async XLA Ops:
  7.2 84.5 %copy-start = (bf16[1,32,8192]{2,1,0:T(8,128)(2,1)S(1)}, bf16[1,32,8192]{2,1,0:T(8,128)(2,1)}, u32[]{:S(2)}) copy-start(bf16[1,32,8192]{2,1,0:T(8,128)(2,1)} %param.14) | copy-start | bytes 1572868
  7.2 84.5 %all-gather.4.cloned.1.call-start = ((), (), s32[]{:S(2)}) async-start(), calls=%async_computation.1 | async-start | bytes 2162688 | tf_op jit(solution)/shard_map/all_gather | solution.py:67
  7.9 248.7 %all-gather.6.cloned.1.call-start = ((), (), s32[]{:S(2)}) async-start(), calls=%async_computation.3 | async-start | bytes 4718592 | tf_op jit(solution)/shard_map/all_gather | solution.py:86
  120.9 138.3 %copy-start.1 = (bf16[1,8192,128]{2,1,0:T(8,128)(2,1)S(1)}, bf16[1,8192,128]{2,1,0:T(8,128)(2,1)}, u32[]{:S(2)}) copy-start(bf16[1,8192,128]{2,1,0:T(8,128)(2,1)} %param.12) | copy-start | bytes 6291460
  223.2 35.9 %copy-start.4 = (f32[6]{0:T(128)}, f32[6]{0:T(128)S(1)}, u32[]{:S(2)}) copy-start(f32[6]{0:T(128)S(1)} %get-tuple-element.286) | copy-start | bytes 76
  226.6 530.0 %reduce-scatter.2.cloned.1.call-start = ((), (), s32[]{:S(2)}) async-start(), calls=%async_computation.2 | async-start | bytes 4325376 | tf_op jit(solution)/shard_map/reduce_scatter | solution.py:115
  266.1 9.6 %collective-permute-start = (bf16[32,8192]{1,0:T(8,128)(2,1)}, bf16[32,8192]{1,0:T(8,128)(2,1)S(1)}, u32[]{:S(2)}, u32[]{:S(2)}) collective-permute-start(bf16[32,8192]{1,0:T(8,128)(2,1)} %fusion.58), channel_id=1, source_target_pairs={{32,0},{64,32},{96,64},{128,96},{160,128},{192,160},{224,192},{33,... | collective-permute-start | bytes 1572872 | tf_op jit(solution)/shard_map/while/body/eval_jaxpr/ppermute | solution.py:17
  282.6 10.7 %collective-permute-start = (bf16[32,8192]{1,0:T(8,128)(2,1)}, bf16[32,8192]{1,0:T(8,128)(2,1)S(1)}, u32[]{:S(2)}, u32[]{:S(2)}) collective-permute-start(bf16[32,8192]{1,0:T(8,128)(2,1)} %fusion.58), channel_id=1, source_target_pairs={{32,0},{64,32},{96,64},{128,96},{160,128},{192,160},{224,192},{33,... | collective-permute-start | bytes 1572872 | tf_op jit(solution)/shard_map/while/body/eval_jaxpr/ppermute | solution.py:17
  300.3 10.7 %collective-permute-start = (bf16[32,8192]{1,0:T(8,128)(2,1)}, bf16[32,8192]{1,0:T(8,128)(2,1)S(1)}, u32[]{:S(2)}, u32[]{:S(2)}) collective-permute-start(bf16[32,8192]{1,0:T(8,128)(2,1)} %fusion.58), channel_id=1, source_target_pairs={{32,0},{64,32},{96,64},{128,96},{160,128},{192,160},{224,192},{33,... | collective-permute-start | bytes 1572872 | tf_op jit(solution)/shard_map/while/body/eval_jaxpr/ppermute | solution.py:17
  317.9 10.7 %collective-permute-start = (bf16[32,8192]{1,0:T(8,128)(2,1)}, bf16[32,8192]{1,0:T(8,128)(2,1)S(1)}, u32[]{:S(2)}, u32[]{:S(2)}) collective-permute-start(bf16[32,8192]{1,0:T(8,128)(2,1)} %fusion.58), channel_id=1, source_target_pairs={{32,0},{64,32},{96,64},{128,96},{160,128},{192,160},{224,192},{33,... | collective-permute-start | bytes 1572872 | tf_op jit(solution)/shard_map/while/body/eval_jaxpr/ppermute | solution.py:17
  335.5 10.7 %collective-permute-start = (bf16[32,8192]{1,0:T(8,128)(2,1)}, bf16[32,8192]{1,0:T(8,128)(2,1)S(1)}, u32[]{:S(2)}, u32[]{:S(2)}) collective-permute-start(bf16[32,8192]{1,0:T(8,128)(2,1)} %fusion.58), channel_id=1, source_target_pairs={{32,0},{64,32},{96,64},{128,96},{160,128},{192,160},{224,192},{33,... | collective-permute-start | bytes 1572872 | tf_op jit(solution)/shard_map/while/body/eval_jaxpr/ppermute | solution.py:17
  353.2 10.7 %collective-permute-start = (bf16[32,8192]{1,0:T(8,128)(2,1)}, bf16[32,8192]{1,0:T(8,128)(2,1)S(1)}, u32[]{:S(2)}, u32[]{:S(2)}) collective-permute-start(bf16[32,8192]{1,0:T(8,128)(2,1)} %fusion.58), channel_id=1, source_target_pairs={{32,0},{64,32},{96,64},{128,96},{160,128},{192,160},{224,192},{33,... | collective-permute-start | bytes 1572872 | tf_op jit(solution)/shard_map/while/body/eval_jaxpr/ppermute | solution.py:17
  370.8 10.7 %collective-permute-start = (bf16[32,8192]{1,0:T(8,128)(2,1)}, bf16[32,8192]{1,0:T(8,128)(2,1)S(1)}, u32[]{:S(2)}, u32[]{:S(2)}) collective-permute-start(bf16[32,8192]{1,0:T(8,128)(2,1)} %fusion.58), channel_id=1, source_target_pairs={{32,0},{64,32},{96,64},{128,96},{160,128},{192,160},{224,192},{33,... | collective-permute-start | bytes 1572872 | tf_op jit(solution)/shard_map/while/body/eval_jaxpr/ppermute | solution.py:17
  388.5 10.7 %collective-permute-start = (bf16[32,8192]{1,0:T(8,128)(2,1)}, bf16[32,8192]{1,0:T(8,128)(2,1)S(1)}, u32[]{:S(2)}, u32[]{:S(2)}) collective-permute-start(bf16[32,8192]{1,0:T(8,128)(2,1)} %fusion.58), channel_id=1, source_target_pairs={{32,0},{64,32},{96,64},{128,96},{160,128},{192,160},{224,192},{33,... | collective-permute-start | bytes 1572872 | tf_op jit(solution)/shard_map/while/body/eval_jaxpr/ppermute | solution.py:17
  406.1 10.7 %collective-permute-start = (bf16[32,8192]{1,0:T(8,128)(2,1)}, bf16[32,8192]{1,0:T(8,128)(2,1)S(1)}, u32[]{:S(2)}, u32[]{:S(2)}) collective-permute-start(bf16[32,8192]{1,0:T(8,128)(2,1)} %fusion.58), channel_id=1, source_target_pairs={{32,0},{64,32},{96,64},{128,96},{160,128},{192,160},{224,192},{33,... | collective-permute-start | bytes 1572872 | tf_op jit(solution)/shard_map/while/body/eval_jaxpr/ppermute | solution.py:17
  423.8 10.7 %collective-permute-start = (bf16[32,8192]{1,0:T(8,128)(2,1)}, bf16[32,8192]{1,0:T(8,128)(2,1)S(1)}, u32[]{:S(2)}, u32[]{:S(2)}) collective-permute-start(bf16[32,8192]{1,0:T(8,128)(2,1)} %fusion.58), channel_id=1, source_target_pairs={{32,0},{64,32},{96,64},{128,96},{160,128},{192,160},{224,192},{33,... | collective-permute-start | bytes 1572872 | tf_op jit(solution)/shard_map/while/body/eval_jaxpr/ppermute | solution.py:17
  434.5 4.9 copy-start.2
  441.5 10.6 %collective-permute-start = (bf16[32,8192]{1,0:T(8,128)(2,1)}, bf16[32,8192]{1,0:T(8,128)(2,1)S(1)}, u32[]{:S(2)}, u32[]{:S(2)}) collective-permute-start(bf16[32,8192]{1,0:T(8,128)(2,1)} %fusion.58), channel_id=1, source_target_pairs={{32,0},{64,32},{96,64},{128,96},{160,128},{192,160},{224,192},{33,... | collective-permute-start | bytes 1572872 | tf_op jit(solution)/shard_map/while/body/eval_jaxpr/ppermute | solution.py:17
  452.1 4.9 copy-start.2
  459.1 10.7 %collective-permute-start = (bf16[32,8192]{1,0:T(8,128)(2,1)}, bf16[32,8192]{1,0:T(8,128)(2,1)S(1)}, u32[]{:S(2)}, u32[]{:S(2)}) collective-permute-start(bf16[32,8192]{1,0:T(8,128)(2,1)} %fusion.58), channel_id=1, source_target_pairs={{32,0},{64,32},{96,64},{128,96},{160,128},{192,160},{224,192},{33,... | collective-permute-start | bytes 1572872 | tf_op jit(solution)/shard_map/while/body/eval_jaxpr/ppermute | solution.py:17
  476.8 10.7 %collective-permute-start = (bf16[32,8192]{1,0:T(8,128)(2,1)}, bf16[32,8192]{1,0:T(8,128)(2,1)S(1)}, u32[]{:S(2)}, u32[]{:S(2)}) collective-permute-start(bf16[32,8192]{1,0:T(8,128)(2,1)} %fusion.58), channel_id=1, source_target_pairs={{32,0},{64,32},{96,64},{128,96},{160,128},{192,160},{224,192},{33,... | collective-permute-start | bytes 1572872 | tf_op jit(solution)/shard_map/while/body/eval_jaxpr/ppermute | solution.py:17
  487.5 4.9 copy-start.2
  494.5 10.7 %collective-permute-start = (bf16[32,8192]{1,0:T(8,128)(2,1)}, bf16[32,8192]{1,0:T(8,128)(2,1)S(1)}, u32[]{:S(2)}, u32[]{:S(2)}) collective-permute-start(bf16[32,8192]{1,0:T(8,128)(2,1)} %fusion.58), channel_id=1, source_target_pairs={{32,0},{64,32},{96,64},{128,96},{160,128},{192,160},{224,192},{33,... | collective-permute-start | bytes 1572872 | tf_op jit(solution)/shard_map/while/body/eval_jaxpr/ppermute | solution.py:17
  512.2 10.7 %collective-permute-start = (bf16[32,8192]{1,0:T(8,128)(2,1)}, bf16[32,8192]{1,0:T(8,128)(2,1)S(1)}, u32[]{:S(2)}, u32[]{:S(2)}) collective-permute-start(bf16[32,8192]{1,0:T(8,128)(2,1)} %fusion.58), channel_id=1, source_target_pairs={{32,0},{64,32},{96,64},{128,96},{160,128},{192,160},{224,192},{33,... | collective-permute-start | bytes 1572872 | tf_op jit(solution)/shard_map/while/body/eval_jaxpr/ppermute | solution.py:17
  (13 other events, 61.5 us)
Sparse Core Ops, SparseCore 0:
  10.6 81.0 all-gather.3
  226.7 29.8 all-gather.5
  529.6 226.9 reduce-scatter.1
where the time goes:
time: 768 us; the launch traced here: 766 us
  waiting for transfers between devices  445 us (58%)
  matrix products  106 us (14%)
  blocking collectives  72.7 us (9%)
  starting transfers between devices  54.6 us (7%)
  other arithmetic  48 us (6%)
  local copies, waits for them, and re-layouts  23.8 us (3%)
  between operations  14.5 us (2%)
    reduce_scatter x1, waiting for transfers between devices, body(): lax.psum_scatter(jnp.concatenate([part_down, part_up], axis=1).astype(jnp...  227 us
    ppermute x15, waiting for transfers between devices, from_behind(): lax.ppermute(value, axis, [(source, source + steps) for source in range(f...  105 us
    all_gather x1, waiting for transfers between devices, body(): weights = lax.all_gather(head_weights, 'dp', axis=0, tiled=True)  82.9 us
    psum x1, blocking collectives, body(): gram_matrix = lax.psum(partial_gram, ('section', 'dp'))  72.7 us
    ppermute x15, starting transfers between devices, from_behind(): lax.ppermute(value, axis, [(source, source + steps) for source in range(f...  54.3 us
    dynamic_update_slice x15, other arithmetic, store_row(): return lax.dynamic_update_index_in_dim(buffer, chosen, index, 0)  31.1 us
    all_gather x1, waiting for transfers between devices, body(): cotangents = lax.all_gather(own_grad[None], 'section', axis=0, tiled=True)  29.7 us
    dot_general x15, matrix products, section_back(): lax.dot_general(inner, down_map, (((1,), (1,)), ((), ())), preferred_elem...  24.8 us
  transfers between devices with their start and end apart: 18, of which 18 were waited for; matrix products, arithmetic and copies ran while one was open for 0% of the time, Pallas kernels for 0%

commit v1 on v0

v1 whole, which is shorter than its diff:
```python
import jax
import jax.numpy as jnp
from jax import lax
from jax.experimental import pallas as pl
from jax.experimental.pallas import tpu as pltpu
from jax.sharding import Mesh
from jax.sharding import PartitionSpec as P

HEAD_OUT = 16
TASKS = 6
STEPS = 20
STEP_RATE = 3.0
NX = 4
NC = 2
NY = 4
NZ = 8
SECTIONS = NX * NC
DP = NY * NZ
BF16 = jnp.bfloat16
F32 = jnp.float32


def shift(value, axis, steps):
    count = lax.axis_size(axis)
    return lax.ppermute(value, axis, [(src, (src + steps) % count) for src in range(count)])


def gather_x(value):
    return jnp.stack([value] + [shift(value, "x", -k) for k in range(1, NX)])


def swap_c(value):
    return lax.ppermute(value, "c", [(0, 1), (1, 0)])


def exchange_dp(blocks):
    return lax.all_to_all(blocks, ("y", "z"), 0, 0, tiled=True)


def gather_dp(block):
    return exchange_dp(jnp.broadcast_to(block[None], (DP,) + block.shape))


def split_hi_lo(value):
    high = value.astype(BF16)
    low = (value - high.astype(F32)).astype(BF16)
    return jnp.concatenate([high, low], axis=0)


def col_slot(stage, column):
    if stage == column:
        return 0
    away = (stage // NC - column // NC) % NX
    return (NX if stage % NC != column % NC else 0) + away


def chain_kernel(
    where_ref, gram_ref, mask_ref, own_ref, other_ref, slope_own_ref, slope_other_ref,
    left_ref, inner_ref, mix_ref,
):
    my_x = where_ref[0]
    my_c = where_ref[1]
    my_stage = my_x * NC + my_c
    gram = gram_ref[...]
    rows = lax.broadcasted_iota(jnp.int32, gram.shape, 0)
    lanes = lax.broadcasted_iota(jnp.int32, gram.shape, 1)
    diagonal = jnp.where(rows == lanes, gram, 0.0)
    trace_sum = jnp.sum(jnp.sum(diagonal, axis=1, keepdims=True), axis=0, keepdims=True) + 1e-06
    scaled = gram / trace_sum
    down0 = jnp.where(rows < TASKS, 1.0 / TASKS, 0.0)
    along0 = jnp.where(lanes < TASKS, 1.0 / TASKS, 0.0)

    def advance(counter, carry):
        down, along = carry
        step_down = jnp.sum(scaled * along, axis=1, keepdims=True)
        step_along = jnp.sum(scaled * down, axis=0, keepdims=True)
        total = jnp.sum(along[0:1], axis=1, keepdims=True)
        rate = -STEP_RATE / total
        down = down * jnp.exp(rate * step_down)
        along = along * jnp.exp(rate * step_along)
        return down, along

    down, along = lax.fori_loop(0, STEPS, advance, (down0, along0))
    total_along = jnp.sum(along[0:1], axis=1, keepdims=True)
    total_down = jnp.sum(down, axis=0, keepdims=True)
    mix_ref[...] = along / total_along
    column_weight = jnp.sum((down / total_down) * mask_ref[...], axis=0, keepdims=True)

    def pick(own, other, stage, lo, size):
        slot = (stage // NC - my_x) % NX
        same = my_c == stage % NC
        return jnp.where(same, own[slot, lo : lo + size, :], other[slot, lo : lo + size, :])

    tok = 32
    parts = [
        (pick(own_ref, other_ref, stage, 1024, tok).astype(F32) * column_weight).astype(BF16)
        for stage in range(SECTIONS)
    ]
    weighted = jnp.concatenate(parts, axis=0)
    left_ref[0] = weighted
    inners = {}
    for stage in range(SECTIONS - 1, -1, -1):
        sources = [(weighted, stage)] + [(inners[s], s) for s in range(stage + 1, SECTIONS)]
        branch = None
        for value, s in sources:
            block = pick(own_ref, other_ref, stage, 128 * col_slot(s, stage), 128)
            term = jnp.dot(value, block, preferred_element_type=F32)
            branch = term if branch is None else branch + term
        slope = pick(slope_own_ref, slope_other_ref, stage, 256, 256)
        inner = (branch * slope.astype(F32)).astype(BF16)
        inners[stage] = inner
        slot = (stage // NC - my_x) % NX + jnp.where(my_c == stage % NC, 0, NX)

        @pl.when(stage == my_stage)
        def _():
            inner_ref[...] = inner

        @pl.when(stage != my_stage)
        def _():
            left_ref[slot] = jnp.where(stage > my_stage, inner, jnp.zeros_like(inner))


def run_chain(where, gram, mask, own, other, slope_own, slope_other):
    tokens = 256
    vmem = pl.BlockSpec(memory_space=pltpu.VMEM)
    return pl.pallas_call(
        chain_kernel,
        out_shape=(
            jax.ShapeDtypeStruct((SECTIONS, tokens, 128), BF16),
            jax.ShapeDtypeStruct((tokens, 128), BF16),
            jax.ShapeDtypeStruct((8, 128), F32),
        ),
        in_specs=[pl.BlockSpec(memory_space=pltpu.SMEM)] + [vmem] * 6,
        out_specs=(vmem, vmem, vmem),
        name="mix_chain",
    )(where, gram, mask, own, other, slope_own, slope_other)


def body(
    section_inputs, adapter_down, adapter_up, representation, head_weights, head_targets, head_task
):
    my_x = lax.axis_index("x")
    my_c = lax.axis_index("c")
    my_dp = lax.axis_index("y") * NZ + lax.axis_index("z")
    dim_model = section_inputs.shape[3]
    saved = section_inputs[0].reshape(-1, dim_model)
    down_map = adapter_down[0]
    up_map = adapter_up[0]
    heads = head_weights
    share = heads.shape[0]
    rank = heads.shape[1]

    preact = jnp.dot(saved, down_map, preferred_element_type=F32)
    logistic = jax.nn.sigmoid(preact)
    active = (preact * logistic).astype(BF16)
    slope = (logistic * (1.0 + preact * (1.0 - logistic))).astype(BF16)

    down_rows = lax.dynamic_slice_in_dim(down_map, my_dp * share, share, 0)
    near = gather_x(jnp.concatenate([down_rows, slope], axis=0))
    far = swap_c(near)
    factors = jnp.concatenate([heads[None], near[1:, :share], far[:, :share]], axis=0)
    up_rows = lax.dynamic_slice_in_dim(up_map, my_dp * share, share, 0)
    part_cross = lax.dot_general(
        factors, up_rows, (((1,), (0,)), ((), ())), preferred_element_type=F32
    ).astype(BF16)

    half = share // NC
    head_half = lax.dynamic_slice_in_dim(heads, my_c * half, half, 0)
    sent = jnp.concatenate(
        [
            jnp.broadcast_to(head_half[None], (DP, half, rank)),
            part_cross.reshape(DP, -1, rank),
        ],
        axis=1,
    )
    got = exchange_dp(sent)
    mine = got[:, :half]
    cross_rows = jnp.sum(got[:, half:].astype(F32), axis=0).astype(BF16)
    theirs = swap_c(mine)
    first = jnp.where(my_c == 0, mine, theirs)
    second = jnp.where(my_c == 0, theirs, mine)
    weights = jnp.concatenate([first, second], axis=1).reshape(dim_model, rank)

    predicted = jnp.dot(representation[0], weights, preferred_element_type=F32)
    residual = (predicted - head_targets[0].astype(F32)).astype(BF16)
    head_gram = lax.dot_general(
        weights, weights, (((0,), (0,)), ((), ())), preferred_element_type=F32
    )
    residual_gram = lax.dot_general(
        residual, residual, (((0,), (0,)), ((), ())), preferred_element_type=F32
    )
    column_task = jnp.repeat(head_task[:, 0], HEAD_OUT)
    mask = (column_task[None, :] == jnp.arange(8, dtype=jnp.int32)[:, None]).astype(F32)
    product = head_gram * residual_gram
    high = lax.Precision.HIGHEST
    part_gram = jnp.dot(mask, jnp.dot(product, mask.T, precision=high), precision=high)
    part_gram = jnp.pad(part_gram, ((0, 0), (0, rank - 8)))

    got = gather_dp(jnp.concatenate([cross_rows, split_hi_lo(part_gram)], axis=0))
    cross = got[:, :32].reshape(-1, rank)
    gram_stage = jnp.sum(got[:, 32:].astype(F32), axis=0)
    gram_stage = gram_stage[:8] + gram_stage[8:]
    payload = jnp.concatenate([cross, residual, split_hi_lo(gram_stage)], axis=0)
    own = gather_x(payload)
    other = swap_c(own)
    gram = jnp.sum(own[:, 1056:].astype(F32) + other[:, 1056:].astype(F32), axis=0)
    gram = gram[:8] + gram[8:]

    where = jnp.stack([my_x, my_c]).astype(jnp.int32)
    left, inner, mix = run_chain(where, gram, mask, own, other, near, far)

    part_down = lax.dot_general(
        saved, inner, (((0,), (0,)), ((), ())), preferred_element_type=F32
    ).astype(BF16)
    blocks = part_down.reshape(NY, NZ * share, rank)
    my_y = lax.axis_index("y")
    total = lax.dynamic_index_in_dim(blocks, my_y, 0, keepdims=False).astype(F32)
    for k in range(1, NY):
        block = lax.dynamic_index_in_dim(blocks, (my_y + k) % NY, 0, keepdims=False)
        total = total + shift(block, "y", k).astype(F32)

    part_mid = lax.dot_general(
        left, active, (((1,), (0,)), ((), ())), preferred_element_type=F32
    ).astype(BF16)
    got = exchange_dp(part_mid.reshape(DP, -1, rank))
    mid_rows = jnp.sum(got.astype(F32), axis=0).astype(BF16)
    middle = gather_dp(mid_rows).reshape(SECTIONS, rank, rank)
    grad_up = lax.dot_general(
        factors, middle, (((0, 2), (0, 1)), ((), ())), preferred_element_type=F32
    )

    got = lax.all_to_all(
        total.astype(BF16).reshape(NZ, share, rank), "z", 0, 0, tiled=True
    )
    grad_down = jnp.sum(got.astype(F32), axis=0)
    return (grad_down[None], grad_up[None], mix[0, :TASKS])


def solution(mesh):
    fine = Mesh(mesh.devices.reshape(NX, NC, NY, NZ), ("x", "c", "y", "z"))
    section = ("x", "c")
    dp = ("y", "z")
    in_specs = (
        P(section, None, dp, None),
        P(section, None, None),
        P(section, None, None),
        P(section, dp, None),
        P(dp, None),
        P(section, dp, None),
        P(),
    )
    out_specs = (P(section, dp, None), P(section, dp, None), P())
    return jax.shard_map(body, mesh=fine, in_specs=in_specs, out_specs=out_specs, check_vma=False)
```

time: 768 us -> 200 us (0.26)
  waiting for transfers between devices: 445 us -> 41.2 us
  matrix products: 106 us -> 14.3 us
  other arithmetic: 48 us -> 8.18 us
  starting transfers between devices: 54.6 us -> 24.3 us
  blocking collectives: 72.7 us -> 90.1 us
  between operations: 14.5 us -> 1.04 us
  local copies, waits for them, and re-layouts: 23.8 us -> 12.6 us
    reduce_scatter x1 -> x0, waiting for transfers between devices: 227 us -> none  [body(): lax.psum_scatter(jnp.concatenate([part_down, part_up], axis=1).astype(jnp...]
    all_gather x2 -> x0, waiting for transfers between devices: 113 us -> none  [the longest x1 82.9 us: body(): weights = lax.all_gather(head_weights, 'dp', axis=0, tiled=True)]
    dot_general x72 -> x10, matrix products: 106 us -> 14.3 us  [the longest x1 4.76 us: body(): preact = jnp.dot(saved, down_map, preferred_element_type=F32)]
    all_to_all x0 -> x3, blocking collectives: none -> 90.1 us  [exchange_dp(): return lax.all_to_all(blocks, ('y', 'z'), 0, 0, tiled=True)]
    ppermute x15 -> x12, waiting for transfers between devices: 105 us -> 20.6 us  [the longest x9 15.3 us: shift(): lax.ppermute(value, axis, [(src, (src + steps) % count) for src in range(...]
    psum x1 -> x0, blocking collectives: 72.7 us -> none  [body(): gram_matrix = lax.psum(partial_gram, ('section', 'dp'))]
    ppermute x15 -> x12, starting transfers between devices: 54.3 us -> 12.5 us  [the longest x9 12.3 us: shift(): lax.ppermute(value, axis, [(src, (src + steps) % count) for src in range(...]
    dynamic_update_slice x15 -> x0, other arithmetic: 31.1 us -> none  [store_row(): return lax.dynamic_update_index_in_dim(buffer, chosen, index, 0)]
  transfers between devices with their start and end apart: 18 -> 14, of which waited for: 18 -> 11; matrix products, arithmetic and copies ran while one was open for 0% -> 5% of each run, Pallas kernels for 0% -> 0%
where the time goes in v1:
time: 200 us; the launch traced here: 199 us
  blocking collectives  90.1 us (45%)
  waiting for transfers between devices  41.2 us (21%)
  starting transfers between devices  24.3 us (12%)
  matrix products  14.3 us (7%)
  local copies, waits for them, and re-layouts  12.6 us (6%)
  other arithmetic  8.18 us (4%)
  Pallas kernels  7.19 us (4%)
    all_to_all x3, blocking collectives, exchange_dp(): return lax.all_to_all(blocks, ('y', 'z'), 0, 0, tiled=True)  90.1 us
    ppermute x9, waiting for transfers between devices, shift(): lax.ppermute(value, axis, [(src, (src + steps) % count) for src in range(...  15.3 us
    ppermute x9, starting transfers between devices, shift(): lax.ppermute(value, axis, [(src, (src + steps) % count) for src in range(...  12.3 us
    all_to_all x1, waiting for transfers between devices, body(): lax.all_to_all(total.astype(BF16).reshape(NZ, share, rank), 'z', 0, 0, ti...  12.1 us
    all_to_all x1, waiting for transfers between devices, exchange_dp(): return lax.all_to_all(blocks, ('y', 'z'), 0, 0, tiled=True)  8.58 us
    all_to_all x1, starting transfers between devices, exchange_dp(): return lax.all_to_all(blocks, ('y', 'z'), 0, 0, tiled=True)  8.33 us
    pallas_call x1, Pallas kernels, run_chain(): pl.pallas_call(chain_kernel, out_shape=(jax.ShapeDtypeStruct((SECTIONS, t...  7.19 us
    ppermute x3, waiting for transfers between devices, swap_c(): return lax.ppermute(value, 'c', [(0, 1), (1, 0)])  5.3 us
  transfers between devices with their start and end apart: 14, of which 11 were waited for; matrix products, arithmetic and copies ran while one was open for 5% of the time, Pallas kernels for 0%

profile of v1, /device:TPU:4, one launch (start us, length us, event | category | flops | bytes accessed | tf_op | source)
XLA Modules:
  0.0 198.9 jit_solution(8669912594891405571)
XLA Ops:
  1.6 4.8 %multiply_convert_fusion.1 = (bf16[256,128]{1,0:T(8,128)(2,1)S(1)}, f32[256,128]{1,0:T(8,128)}) fusion(bf16[256,8192]{1,0:T(8,128)(2,1)} %bitcast.82, bf16[1,8192,128]{2,1,0:T(8,128)(2,1)} %param.8), kind=kOutput, calls=%fused_computation.36 | convolution fusion | flops 537133056 | bytes 6488064 | tf_op jit(solution)/shard_map/dot_general | solution.py:153
  8.8 2.5 %collective-permute-start = (bf16[512,128]{1,0:T(8,128)(2,1)S(1)}, bf16[512,128]{1,0:T(8,128)(2,1)S(1)}, u32[]{:S(2)}, u32[]{:S(2)}) collective-permute-start(bf16[512,128]{1,0:T(8,128)(2,1)S(1)} %get-tuple-element.19), channel_id=1, source_target_pairs={{0,192},{64,0},{128,64},{192,128},{1,193},{65,1},{129,65},{193,129... | collective-permute-start | bytes 393224 | tf_op jit(solution)/shard_map/ppermute | solution.py:25
  12.1 2.4 %collective-permute-done.1 = bf16[512,128]{1,0:T(8,128)(2,1)S(1)} collective-permute-done((bf16[512,128]{1,0:T(8,128)(2,1)S(1)}, bf16[512,128]{1,0:T(8,128)(2,1)S(1)}, u32[]{:S(2)}, u32[]{:S(2)}) %collective-permute-start.1) | collective-permute-done | bytes 131104 | tf_op jit(solution)/shard_map/ppermute | solution.py:25
  14.6 1.8 collective-permute-done
  20.2 46.0 %all_to_all.25 = bf16[32,160,128]{2,1,0:T(8,128)(2,1)S(1)} all-to-all(bf16[32,160,128]{2,1,0:T(8,128)(2,1)S(1)} %pad_maximum_fusion.1), channel_id=1, replica_groups=mesh['x'=4,'c'=2,'y'=4,'z'=8] {'y','z'}, dimensions={0} | all-to-all | bytes 2621440 | tf_op jit(solution)/shard_map/all_to_all | solution.py:37
  67.5 2.8 %collective-permute-done.4 = bf16[32,128,128]{2,1,0:T(8,128)(2,1)} collective-permute-done((bf16[32,128,128]{2,1,0:T(8,128)(2,1)}, bf16[32,128,128]{2,1,0:T(8,128)(2,1)}, u32[]{:S(2)}, u32[]{:S(2)}) %collective-permute-start.4) | collective-permute-done | bytes 1048608 | tf_op jit(solution)/shard_map/ppermute | solution.py:33
  70.3 1.4 broadcast_select_fusion.1
  74.6 19.1 %all_to_all.26 = bf16[32,48,128]{2,1,0:T(8,128)(2,1)S(1)} all-to-all(bf16[32,48,128]{2,1,0:T(8,128)(2,1)S(1)} %broadcast_in_dim.34), channel_id=1, replica_groups=mesh['x'=4,'c'=2,'y'=4,'z'=8] {'y','z'}, dimensions={0} | all-to-all | bytes 786432 | tf_op jit(solution)/shard_map/all_to_all | solution.py:37
  94.8 1.7 collective-permute-start.5
  96.8 7.4 %collective-permute-done.6 = bf16[1072,128]{1,0:T(8,128)(2,1)S(1)} collective-permute-done((bf16[1072,128]{1,0:T(8,128)(2,1)S(1)}, bf16[1072,128]{1,0:T(8,128)(2,1)S(1)}, u32[]{:S(2)}, u32[]{:S(2)}) %collective-permute-start.6) | collective-permute-done | bytes 274464 | tf_op jit(solution)/shard_map/ppermute | solution.py:25
  104.2 2.1 %collective-permute-done.5 = bf16[1072,128]{1,0:T(8,128)(2,1)S(1)} collective-permute-done((bf16[1072,128]{1,0:T(8,128)(2,1)S(1)}, bf16[1072,128]{1,0:T(8,128)(2,1)S(1)}, u32[]{:S(2)}, u32[]{:S(2)}) %collective-permute-start.5) | collective-permute-done | bytes 274464 | tf_op jit(solution)/shard_map/ppermute | solution.py:25
  108.7 1.4 collective-permute-done.8.other_ref
  111.5 7.2 %mix_chain.1 = (bf16[8,256,128]{2,1,0:T(8,128)(2,1)}, bf16[256,128]{1,0:T(8,128)(2,1)}, f32[8,128]{1,0:T(8,128)}) custom-call(s32[2]{0:T(128)} %pad_add_fusion.where_ref, f32[8,128]{1,0:T(8,128)} %slice_add_fusion.gram_ref, f32[8,128]{1,0:T(8,128)} %fusion.15.mask_ref, bf16[4,1072,128]{2,1,0:T(8,128)(2,1)} %copy-done.1, ...), custom_call_target="tpu_custom_call" | custom-call | tf_op jit(solution)/shard_map/mix_chain/pallas_call | solution.py:126
  118.6 4.3 %fusion = bf16[8192,128]{0,1:T(8,128)(2,1)} fusion(bf16[256,128]{1,0:T(8,128)(2,1)} %get-tuple-element.6, bf16[256,8192]{1,0:T(8,128)(2,1)} %bitcast.83), kind=kOutput, calls=%fused_computation.1 | convolution fusion | flops 537919488 | bytes 6356992 | tf_op jit(solution)/shard_map/dot_general | solution.py:212
  122.9 4.1 %copy.28 = bf16[8192,128]{1,0:T(8,128)(2,1)} copy(bf16[8192,128]{0,1:T(8,128)(2,1)} %fusion) | data formatting | bytes 4194304 | tf_op jit(solution)/shard_map/reshape | solution.py:215
  127.0 2.3 %dynamic-slice_bitcast_fusion.2 = (bf16[2048,128]{1,0:T(8,128)(2,1)}, bf16[2048,128]{1,0:T(8,128)(2,1)S(1)}, bf16[2048,128]{1,0:T(8,128)(2,1)S(1)}) fusion(bf16[4,2048,128]{2,1,0:T(8,128)(2,1)} %bitcast.80, s32[]{:T(128)S(6)} %select_n.54, s32[]{:T(128)S(6)} %select_n.58, s32[]{:T(128)S(6)} %select_n.56), kind=kLoop, calls=%fused_computation.30 | loop fusion | bytes 3145740 | tf_op jit(solution)/shard_map/jit(dynamic_index_in_dim)/squeeze | solution.py:219
  130.0 2.6 %collective-permute-start.11 = (bf16[2048,128]{1,0:T(8,128)(2,1)S(1)}, bf16[2048,128]{1,0:T(8,128)(2,1)}, u32[]{:S(2)}, u32[]{:S(2)}) collective-permute-start(bf16[2048,128]{1,0:T(8,128)(2,1)S(1)} %get-tuple-element.14), channel_id=1, source_target_pairs={{0,24},{8,0},{16,8},{24,16},{1,25},{9,1},{17,9},{25,17},{2,26},{10... | collective-permute-start | bytes 1572872 | tf_op jit(solution)/shard_map/ppermute | solution.py:25
  134.1 24.9 %all_to_all.27 = bf16[32,32,128]{2,1,0:T(8,128)(2,1)S(1)} all-to-all(bf16[32,32,128]{2,1,0:T(8,128)(2,1)S(1)} %bitcast.89), channel_id=1, replica_groups=mesh['x'=4,'c'=2,'y'=4,'z'=8] {'y','z'}, dimensions={0} | all-to-all | bytes 524288 | tf_op jit(solution)/shard_map/all_to_all | solution.py:37
  159.9 8.3 %all-to-all-start.4 = ((bf16[32,32,128]{2,1,0:T(8,128)(2,1)}), bf16[32,32,128]{2,1,0:T(8,128)(2,1)}, u32[]{:S(2)}, u32[]{:S(2)}) async-start(bf16[32,32,128]{2,1,0:T(8,128)(2,1)} %broadcast_in_dim.36), calls=%async_computation.4 | async-start | bytes 524288 | tf_op jit(solution)/shard_map/all_to_all | solution.py:37
  168.3 2.7 %fusion.8 = bf16[2048,128]{1,0:T(8,128)(2,1)} fusion(bf16[2048,128]{1,0:T(8,128)(2,1)} %collective-permute-done.11, bf16[2048,128]{1,0:T(8,128)(2,1)} %collective-permute-done.10, bf16[2048,128]{1,0:T(8,128)(2,1)} %collective-permute-done.9, bf16[4,2048,128]{2,1,0:T(8,128)(2,1)} %bitcast.81, s32[]{:T(128)S(6)} %select_n.52), kind=kLoop, calls=%fused_computation.18 | loop fusion | flops 2097152 | bytes 2621444 | tf_op jit(solution)/shard_map/convert_element_type | solution.py:233
  171.0 8.6 %all-to-all-done.4 = bf16[32,32,128]{2,1,0:T(8,128)(2,1)} async-done(((bf16[32,32,128]{2,1,0:T(8,128)(2,1)}), bf16[32,32,128]{2,1,0:T(8,128)(2,1)}, u32[]{:S(2)}, u32[]{:S(2)}) %all-to-all-start.4) | async-done | bytes 262176 | tf_op jit(solution)/shard_map/all_to_all | solution.py:37
  179.5 3.5 %all-to-all-start.2 = ((bf16[8,256,128]{2,1,0:T(8,128)(2,1)}), bf16[8,256,128]{2,1,0:T(8,128)(2,1)S(1)}, u32[]{:S(2)}, u32[]{:S(2)}) async-start(bf16[8,256,128]{2,1,0:T(8,128)(2,1)} %bitcast.29), calls=%async_computation.2 | async-start | bytes 1048576 | tf_op jit(solution)/shard_map/all_to_all | solution.py:232
  184.2 1.9 convolution_bitcast_fusion
  186.1 12.1 %all-to-all-done.2 = bf16[8,256,128]{2,1,0:T(8,128)(2,1)S(1)} async-done(((bf16[8,256,128]{2,1,0:T(8,128)(2,1)}), bf16[8,256,128]{2,1,0:T(8,128)(2,1)S(1)}, u32[]{:S(2)}, u32[]{:S(2)}) %all-to-all-start.2) | async-done | bytes 524320 | tf_op jit(solution)/shard_map/all_to_all | solution.py:232
  (83 shorter events, 22.0 us)
Async XLA Ops:
  0.6 17.9 %copy-start = (bf16[1,8192,128]{2,1,0:T(8,128)(2,1)S(1)}, bf16[1,8192,128]{2,1,0:T(8,128)(2,1)}, u32[]{:S(2)}) copy-start(bf16[1,8192,128]{2,1,0:T(8,128)(2,1)} %param.9) | copy-start | bytes 6291460
  6.4 5.7 %collective-permute-start.2 = (bf16[512,128]{1,0:T(8,128)(2,1)S(1)}, bf16[512,128]{1,0:T(8,128)(2,1)S(1)}, u32[]{:S(2)}, u32[]{:S(2)}) collective-permute-start(bf16[512,128]{1,0:T(8,128)(2,1)S(1)} %get-tuple-element.19), channel_id=1, source_target_pairs={{0,64},{64,128},{128,192},{192,0},{1,65},{65,129},{129,193},{193,1... | collective-permute-start | bytes 393224 | tf_op jit(solution)/shard_map/ppermute | solution.py:25
  7.7 6.8 %collective-permute-start.1 = (bf16[512,128]{1,0:T(8,128)(2,1)S(1)}, bf16[512,128]{1,0:T(8,128)(2,1)S(1)}, u32[]{:S(2)}, u32[]{:S(2)}) collective-permute-start(bf16[512,128]{1,0:T(8,128)(2,1)S(1)} %get-tuple-element.19), channel_id=1, source_target_pairs={{0,128},{64,192},{128,0},{192,64},{1,129},{65,193},{129,1},{193,65... | collective-permute-start | bytes 393224 | tf_op jit(solution)/shard_map/ppermute | solution.py:25
  8.8 7.6 %collective-permute-start = (bf16[512,128]{1,0:T(8,128)(2,1)S(1)}, bf16[512,128]{1,0:T(8,128)(2,1)S(1)}, u32[]{:S(2)}, u32[]{:S(2)}) collective-permute-start(bf16[512,128]{1,0:T(8,128)(2,1)S(1)} %get-tuple-element.19), channel_id=1, source_target_pairs={{0,192},{64,0},{128,64},{192,128},{1,193},{65,1},{129,65},{193,129... | collective-permute-start | bytes 393224 | tf_op jit(solution)/shard_map/ppermute | solution.py:25
  14.6 5.3 %copy-start.7 = (bf16[512,128]{1,0:T(8,128)(2,1)}, bf16[512,128]{1,0:T(8,128)(2,1)S(1)}, u32[]{:S(2)}) copy-start(bf16[512,128]{1,0:T(8,128)(2,1)S(1)} %collective-permute-done.1) | copy-start | bytes 393220
  16.5 2.0 %collective-permute-start.3 = (bf16[4,512,128]{2,1,0:T(8,128)(2,1)S(1)}, bf16[4,512,128]{2,1,0:T(8,128)(2,1)S(1)}, u32[]{:S(2)}, u32[]{:S(2)}) collective-permute-start(bf16[4,512,128]{2,1,0:T(8,128)(2,1)S(1)} %pad_maximum_fusion.5.slope_own_ref), channel_id=1, source_target_pairs={{0,32},{32,0},{1,33},{33,1},{2,34},{34,2},{3,35},{35,3},{4,36},{36... | collective-permute-start | bytes 1572872 | tf_op jit(solution)/shard_map/ppermute | solution.py:33
  20.2 47.2 %copy-start.13 = (s32[8,1]{0,1:T(1,128)S(1)}, s32[8,1]{0,1:T(1,128)}, u32[]{:S(2)}) copy-start(s32[8,1]{0,1:T(1,128)} %param.13) | copy-start | bytes 100
  67.3 3.0 %collective-permute-start.4 = (bf16[32,128,128]{2,1,0:T(8,128)(2,1)}, bf16[32,128,128]{2,1,0:T(8,128)(2,1)}, u32[]{:S(2)}, u32[]{:S(2)}) collective-permute-start(bf16[32,128,128]{2,1,0:T(8,128)(2,1)} %slice.55), channel_id=1, source_target_pairs={{0,32},{32,0},{1,33},{33,1},{2,34},{34,2},{3,35},{35,3},{4,36},{36... | collective-permute-start | bytes 3145736 | tf_op jit(solution)/shard_map/ppermute | solution.py:33
  93.8 10.4 %collective-permute-start.6 = (bf16[1072,128]{1,0:T(8,128)(2,1)S(1)}, bf16[1072,128]{1,0:T(8,128)(2,1)S(1)}, u32[]{:S(2)}, u32[]{:S(2)}) collective-permute-start(bf16[1072,128]{1,0:T(8,128)(2,1)S(1)} %get-tuple-element.17), channel_id=1, source_target_pairs={{0,128},{64,192},{128,0},{192,64},{1,129},{65,193},{129,1},{193,65... | collective-permute-start | bytes 823304 | tf_op jit(solution)/shard_map/ppermute | solution.py:25
  94.8 11.6 %collective-permute-start.5 = (bf16[1072,128]{1,0:T(8,128)(2,1)S(1)}, bf16[1072,128]{1,0:T(8,128)(2,1)S(1)}, u32[]{:S(2)}, u32[]{:S(2)}) collective-permute-start(bf16[1072,128]{1,0:T(8,128)(2,1)S(1)} %get-tuple-element.17), channel_id=1, source_target_pairs={{0,192},{64,0},{128,64},{192,128},{1,193},{65,1},{129,65},{193,129... | collective-permute-start | bytes 823304 | tf_op jit(solution)/shard_map/ppermute | solution.py:25
  96.4 10.6 %collective-permute-start.7 = (bf16[1072,128]{1,0:T(8,128)(2,1)S(1)}, bf16[1072,128]{1,0:T(8,128)(2,1)S(1)}, u32[]{:S(2)}, u32[]{:S(2)}) collective-permute-start(bf16[1072,128]{1,0:T(8,128)(2,1)S(1)} %get-tuple-element.17), channel_id=1, source_target_pairs={{0,64},{64,128},{128,192},{192,0},{1,65},{65,129},{129,193},{193,1... | collective-permute-start | bytes 823304 | tf_op jit(solution)/shard_map/ppermute | solution.py:25
  107.2 4.3 %copy-start.1 = (bf16[4,1072,128]{2,1,0:T(8,128)(2,1)}, bf16[4,1072,128]{2,1,0:T(8,128)(2,1)S(1)}, u32[]{:S(2)}) copy-start(bf16[4,1072,128]{2,1,0:T(8,128)(2,1)S(1)} %pad_maximum_fusion.2.own_ref) | copy-start | bytes 3293188
  107.2 2.9 %collective-permute-start.8 = (bf16[4,1072,128]{2,1,0:T(8,128)(2,1)S(1)}, bf16[4,1072,128]{2,1,0:T(8,128)(2,1)}, u32[]{:S(2)}, u32[]{:S(2)}) collective-permute-start(bf16[4,1072,128]{2,1,0:T(8,128)(2,1)S(1)} %pad_maximum_fusion.2.own_ref), channel_id=1, source_target_pairs={{0,32},{32,0},{1,33},{33,1},{2,34},{34,2},{3,35},{35,3},{4,36},{36... | collective-permute-start | bytes 3293192 | tf_op jit(solution)/shard_map/ppermute | solution.py:33
  127.0 6.8 %copy-start.14 = (bf16[8,256,128]{2,1,0:T(8,128)(2,1)S(1)}, bf16[8,256,128]{2,1,0:T(8,128)(2,1)}, u32[]{:S(2)}) copy-start(bf16[8,256,128]{2,1,0:T(8,128)(2,1)} %get-tuple-element.7) | copy-start | bytes 1572868
  127.0 6.8 %copy-start.15 = (f32[256,128]{1,0:T(8,128)S(1)}, f32[256,128]{1,0:T(8,128)}, u32[]{:S(2)}) copy-start(f32[256,128]{1,0:T(8,128)} %get-tuple-element.21) | copy-start | bytes 393220
  129.3 38.9 %collective-permute-start.9 = (bf16[2048,128]{1,0:T(8,128)(2,1)}, bf16[2048,128]{1,0:T(8,128)(2,1)}, u32[]{:S(2)}, u32[]{:S(2)}) collective-permute-start(bf16[2048,128]{1,0:T(8,128)(2,1)} %get-tuple-element.13), channel_id=1, source_target_pairs={{0,8},{8,16},{16,24},{24,0},{1,9},{9,17},{17,25},{25,1},{2,10},{10... | collective-permute-start | bytes 1572872 | tf_op jit(solution)/shard_map/ppermute | solution.py:25
  130.0 38.3 %collective-permute-start.11 = (bf16[2048,128]{1,0:T(8,128)(2,1)S(1)}, bf16[2048,128]{1,0:T(8,128)(2,1)}, u32[]{:S(2)}, u32[]{:S(2)}) collective-permute-start(bf16[2048,128]{1,0:T(8,128)(2,1)S(1)} %get-tuple-element.14), channel_id=1, source_target_pairs={{0,24},{8,0},{16,8},{24,16},{1,25},{9,1},{17,9},{25,17},{2,26},{10... | collective-permute-start | bytes 1572872 | tf_op jit(solution)/shard_map/ppermute | solution.py:25
  132.6 35.7 %collective-permute-start.10 = (bf16[2048,128]{1,0:T(8,128)(2,1)S(1)}, bf16[2048,128]{1,0:T(8,128)(2,1)}, u32[]{:S(2)}, u32[]{:S(2)}) collective-permute-start(bf16[2048,128]{1,0:T(8,128)(2,1)S(1)} %get-tuple-element.15), channel_id=1, source_target_pairs={{0,16},{8,24},{16,0},{24,8},{1,17},{9,25},{17,1},{25,9},{2,18},{10... | collective-permute-start | bytes 1572872 | tf_op jit(solution)/shard_map/ppermute | solution.py:25
  159.9 24.3 %copy-start.6 = (bf16[4,256,128]{2,1,0:T(8,128)(2,1)S(1)}, bf16[4,256,128]{2,1,0:T(8,128)(2,1)}, u32[]{:S(2)}) copy-start(bf16[4,256,128]{2,1,0:T(8,128)(2,1)} %copy-done.5) | copy-start | bytes 786436
  159.9 19.6 %all-to-all-start.4 = ((bf16[32,32,128]{2,1,0:T(8,128)(2,1)}), bf16[32,32,128]{2,1,0:T(8,128)(2,1)}, u32[]{:S(2)}, u32[]{:S(2)}) async-start(bf16[32,32,128]{2,1,0:T(8,128)(2,1)} %broadcast_in_dim.36), calls=%async_computation.4 | async-start | bytes 524288 | tf_op jit(solution)/shard_map/all_to_all | solution.py:37
  168.2 16.0 %copy-start.8 = (bf16[512,128]{1,0:T(8,128)(2,1)S(1)}, bf16[512,128]{1,0:T(8,128)(2,1)}, u32[]{:S(2)}) copy-start(bf16[512,128]{1,0:T(8,128)(2,1)} %copy-done.7) | copy-start | bytes 393220
  168.3 16.0 %copy-start.10 = (bf16[512,128]{1,0:T(8,128)(2,1)S(1)}, bf16[512,128]{1,0:T(8,128)(2,1)}, u32[]{:S(2)}) copy-start(bf16[512,128]{1,0:T(8,128)(2,1)} %copy-done.9) | copy-start | bytes 393220
  168.3 16.0 %copy-start.11 = (bf16[256,128]{1,0:T(8,128)(2,1)S(1)}, bf16[256,128]{1,0:T(8,128)(2,1)}, u32[]{:S(2)}) copy-start(bf16[256,128]{1,0:T(8,128)(2,1)} %param.11) | copy-start | bytes 196612
  179.5 18.7 %all-to-all-start.2 = ((bf16[8,256,128]{2,1,0:T(8,128)(2,1)}), bf16[8,256,128]{2,1,0:T(8,128)(2,1)S(1)}, u32[]{:S(2)}, u32[]{:S(2)}) async-start(bf16[8,256,128]{2,1,0:T(8,128)(2,1)} %bitcast.29), calls=%async_computation.2 | async-start | bytes 1048576 | tf_op jit(solution)/shard_map/all_to_all | solution.py:232
  (6 other events, 12.1 us)

commit v2 on v1

v2 whole, which is shorter than its diff:
```python
import jax
import jax.numpy as jnp
from jax import lax
from jax.experimental import pallas as pl
from jax.experimental.pallas import tpu as pltpu
from jax.sharding import Mesh
from jax.sharding import PartitionSpec as P

HEAD_OUT = 16
TASKS = 6
STEPS = 20
STEP_RATE = 3.0
NX = 4
NC = 2
NY = 4
NZ = 8
SECTIONS = NX * NC
DP = NY * NZ
BF16 = jnp.bfloat16
F32 = jnp.float32


def shift(value, axis, steps):
    count = lax.axis_size(axis)
    return lax.ppermute(value, axis, [(src, (src + steps) % count) for src in range(count)])


def swap_c(value):
    return lax.ppermute(value, "c", [(0, 1), (1, 0)])


def gather_x(value):
    return [value] + [shift(value, "x", -k) for k in range(1, NX)]


def gather_section(value):
    near = jnp.stack(gather_x(value))
    return near, swap_c(near)


def exchange_dp(blocks):
    return lax.all_to_all(blocks, ("y", "z"), 0, 0, tiled=True)


def gather_dp(block):
    return exchange_dp(jnp.broadcast_to(block[None], (DP,) + block.shape))


def at(value, index):
    return lax.dynamic_index_in_dim(value, index, 0, keepdims=False)


def rows_at(value, start, size):
    return lax.dynamic_slice_in_dim(value, start, size, 0)


def col_slot(stage, column):
    if stage == column:
        return 0
    away = (stage // NC - column // NC) % NX
    return (NX if stage % NC != column % NC else 0) + away


def across(left, right):
    return lax.dot_general(left, right, (((0,), (0,)), ((), ())), preferred_element_type=F32)


def chain_kernel(
    where_ref, gram_ref, mask_ref, residual_ref, active_ref, own_ref, other_ref,
    slope_own_ref, slope_other_ref, middle_ref, inner_ref, mix_ref,
):
    my_x = where_ref[0]
    my_c = where_ref[1]
    my_stage = my_x * NC + my_c
    gram = jnp.sum(gram_ref[...], axis=0)
    rows = lax.broadcasted_iota(jnp.int32, gram.shape, 0)
    lanes = lax.broadcasted_iota(jnp.int32, gram.shape, 1)
    diagonal = jnp.where(rows == lanes, gram, 0.0)
    trace_sum = jnp.sum(jnp.sum(diagonal, axis=1, keepdims=True), axis=0, keepdims=True) + 1e-06
    scaled = gram / trace_sum
    down0 = jnp.where(rows < TASKS, 1.0 / TASKS, 0.0)
    along0 = jnp.where(lanes < TASKS, 1.0 / TASKS, 0.0)

    def advance(counter, carry):
        down, along = carry
        step_down = jnp.sum(scaled * along, axis=1, keepdims=True)
        step_along = jnp.sum(scaled * down, axis=0, keepdims=True)
        total = jnp.sum(along[0:1], axis=1, keepdims=True)
        rate = -STEP_RATE / total
        down = down * jnp.exp(rate * step_down)
        along = along * jnp.exp(rate * step_along)
        return down, along

    down, along = lax.fori_loop(0, STEPS, advance, (down0, along0))
    total_along = jnp.sum(along[0:1], axis=1, keepdims=True)
    total_down = jnp.sum(down, axis=0, keepdims=True)
    mix_ref[...] = along / total_along
    column_weight = jnp.sum((down / total_down) * mask_ref[...], axis=0, keepdims=True)

    def pick(own, other, stage, lo, size):
        slot = (stage // NC - my_x) % NX
        same = my_c == stage % NC
        return jnp.where(same, own[slot, lo : lo + size, :], other[slot, lo : lo + size, :])

    active = active_ref[...]
    weighted = (residual_ref[...].astype(F32) * column_weight).astype(BF16)
    middle_ref[0] = across(weighted, active).astype(BF16)
    inners = {}
    for stage in range(SECTIONS - 1, -1, -1):
        sources = [(weighted, stage)] + [(inners[s], s) for s in range(stage + 1, SECTIONS)]
        branch = None
        for value, s in sources:
            block = pick(own_ref, other_ref, stage, 128 * col_slot(s, stage), 128)
            term = jnp.dot(value, block, preferred_element_type=F32)
            branch = term if branch is None else branch + term
        slope = pick(slope_own_ref, slope_other_ref, stage, 0, 256)
        inner = (branch * slope.astype(F32)).astype(BF16)
        inners[stage] = inner

        @pl.when(stage == my_stage)
        def _():
            inner_ref[...] = inner

    for stage in range(SECTIONS):
        slot = (stage // NC - my_x) % NX + jnp.where(my_c == stage % NC, 0, NX)
        product = across(inners[stage], active)

        @pl.when(stage != my_stage)
        def _():
            middle_ref[slot] = jnp.where(stage > my_stage, product, 0.0).astype(BF16)


def run_chain(*operands):
    vmem = pl.BlockSpec(memory_space=pltpu.VMEM)
    return pl.pallas_call(
        chain_kernel,
        out_shape=(
            jax.ShapeDtypeStruct((SECTIONS, 128, 128), BF16),
            jax.ShapeDtypeStruct((256, 128), BF16),
            jax.ShapeDtypeStruct((8, 128), F32),
        ),
        in_specs=[pl.BlockSpec(memory_space=pltpu.SMEM)] + [vmem] * (len(operands) - 1),
        out_specs=(vmem, vmem, vmem),
        name="mix_chain",
    )(*operands)


def down_kernel(y_ref, *refs):
    inputs = refs[:NY]
    inners = refs[NY : 2 * NY]
    out_ref = refs[2 * NY]
    total = across(inners[0][...], inputs[0][...])
    for k in range(1, NY):
        total = total + across(inners[k][...], inputs[k][...])
    total = total.astype(BF16)
    for j in range(2):
        out_ref[j] = total[:, 256 * j : 256 * (j + 1)]


def run_down(my_y, saved, received, inners):
    tokens = saved.shape[0]
    cols = 512
    steps = received[0].shape[1] // cols
    whole = pl.BlockSpec((tokens, 128), lambda i, y: (0, 0))
    return pl.pallas_call(
        down_kernel,
        grid_spec=pltpu.PrefetchScalarGridSpec(
            num_scalar_prefetch=1,
            grid=(steps,),
            in_specs=[pl.BlockSpec((tokens, cols), lambda i, y: (0, y[0] * steps + i))]
            + [pl.BlockSpec((tokens, cols), lambda i, y: (0, i))] * (NY - 1)
            + [whole] * NY,
            out_specs=pl.BlockSpec((2, 128, 256), lambda i, y: (i, 0, 0)),
        ),
        out_shape=jax.ShapeDtypeStruct((NZ, 128, 256), BF16),
        name="down_product",
    )(my_y.reshape(1), saved, *received, *inners)


def body(
    section_inputs, adapter_down, adapter_up, representation, head_weights, head_targets, head_task
):
    my_x = lax.axis_index("x")
    my_c = lax.axis_index("c")
    my_y = lax.axis_index("y")
    my_dp = my_y * NZ + lax.axis_index("z")
    my_stage = my_x * NC + my_c
    dim_model = section_inputs.shape[3]
    saved = section_inputs[0].reshape(-1, dim_model)
    down_map = adapter_down[0]
    up_map = adapter_up[0]
    heads = head_weights
    share, rank = heads.shape
    tok = representation.shape[1]

    piece = rows_at(heads, my_c * 128 + my_x * 32, 32)
    turn = [(a * NY + b, b * NY + a) for a in range(NX) for b in range(NY)]
    piece = lax.ppermute(piece, ("x", "y"), turn)

    blocks = representation[0].reshape(tok, NX, NZ, NC, 128).transpose(3, 1, 2, 0, 4)
    keep = at(blocks, my_c)
    swapped = swap_c(at(blocks, 1 - my_c))
    pair = jnp.stack([keep, swapped], axis=1)
    down_rows = rows_at(down_map, my_dp * share, share)
    near_rep = [at(pair, my_x)]
    near_down = [down_rows]
    for k in range(1, NX):
        sent = jnp.concatenate([at(pair, (my_x - k) % NX).reshape(-1, 128), down_rows], axis=0)
        got = shift(sent, "x", -k)
        near_rep.append(got[: 2 * NZ * tok].reshape(NC, NZ, tok, 128))
        near_down.append(got[2 * NZ * tok :])
    near = jnp.stack(near_down)
    far = swap_c(near)
    factors = jnp.concatenate([heads[None], near[1:], far], axis=0)
    up_rows = rows_at(up_map, my_dp * share, share)
    part_cross = lax.dot_general(
        factors, up_rows, (((1,), (0,)), ((), ())), preferred_element_type=F32
    ).astype(BF16)

    preact = jnp.dot(saved, down_map, preferred_element_type=F32)
    logistic = jax.nn.sigmoid(preact)
    active = (preact * logistic).astype(BF16)
    slope = (logistic * (1.0 + preact * (1.0 - logistic))).astype(BF16)
    slope_own, slope_other = gather_section(slope)

    wide = dim_model // NY
    received = []
    for k in range(1, NY):
        cut = lax.dynamic_slice_in_dim(saved, ((my_y - k) % NY) * wide, wide, 1)
        received.append(shift(cut, "y", -k))

    got = exchange_dp(
        jnp.concatenate(
            [jnp.broadcast_to(piece[None], (DP, 32, rank)), part_cross.reshape(DP, 32, rank)],
            axis=1,
        )
    )
    head_part = got[:, :32].reshape(NY, NZ, 32, rank).transpose(1, 0, 2, 3)
    head_part = head_part.reshape(NZ, 128, rank)
    cross_rows = jnp.sum(got[:, 32:].astype(F32), axis=0).astype(BF16)
    cross = gather_dp(cross_rows).reshape(-1, rank)

    rep_part = jnp.stack(near_rep)
    part = lax.dot_general(
        rep_part, head_part, (((2, 4), (0, 1)), ((), ())), preferred_element_type=F32
    )
    part = jnp.where(my_c == 0, part, part[:, ::-1])
    part = rows_at(jnp.concatenate([part, part], axis=0), (NX - my_x) % NX, NX)
    part = part.reshape(SECTIONS, tok, rank)
    is_mine = (jnp.arange(SECTIONS) == my_stage)[:, None, None]
    part = part - jnp.where(is_mine, head_targets.astype(F32), 0.0)
    flat = head_part.reshape(-1, rank)
    part = jnp.concatenate([part.reshape(-1, rank), across(flat, flat)], axis=0)
    part = part + swap_c(part)
    first, second, third, fourth = gather_x(part)
    part = (first + third) + (second + fourth)
    residual = part[: SECTIONS * tok].astype(BF16)
    head_gram = part[SECTIONS * tok :]

    column_task = jnp.repeat(head_task[:, 0], HEAD_OUT)
    mask = (column_task[None, :] == jnp.arange(8, dtype=jnp.int32)[:, None]).astype(F32)
    product = head_gram * across(residual, residual)
    high = lax.Precision.HIGHEST
    part_gram = jnp.dot(mask, jnp.dot(product, mask.T, precision=high), precision=high)
    part_gram = jnp.pad(part_gram, ((0, 0), (0, rank - 8)))
    cross_own, cross_other = gather_section(cross)
    gram = gather_dp(part_gram)

    where = jnp.stack([my_x, my_c]).astype(jnp.int32)
    middle, inner, mix = run_chain(
        where, gram, mask, residual, active, cross_own, cross_other, slope_own, slope_other
    )

    got = exchange_dp(middle.reshape(DP, 32, rank))
    inners = [inner] + [shift(inner, "y", -k) for k in range(1, NY)]
    part_down = run_down(my_y, saved, received, inners)
    got_down = lax.all_to_all(part_down, "z", 0, 0, tiled=True)
    middle = gather_dp(jnp.sum(got.astype(F32), axis=0).astype(BF16))
    middle = middle.reshape(SECTIONS, rank, rank)
    grad_up = lax.dot_general(
        factors, middle, (((0, 2), (0, 1)), ((), ())), preferred_element_type=F32
    )
    grad_down = jnp.sum(got_down.astype(F32), axis=0).T
    return (grad_down[None], grad_up[None], mix[0, :TASKS])


def solution(mesh):
    fine = Mesh(mesh.devices.reshape(NX, NC, NY, NZ), ("x", "c", "y", "z"))
    section = ("x", "c")
    dp = ("y", "z")
    in_specs = (
        P(section, None, dp, None),
        P(section, None, None),
        P(section, None, None),
        P(section, dp, None),
        P(dp, None),
        P(section, dp, None),
        P(),
    )
    out_specs = (P(section, dp, None), P(section, dp, None), P())
    return jax.shard_map(body, mesh=fine, in_specs=in_specs, out_specs=out_specs, check_vma=False)
```

time: 200 us -> 217 us (1.085)
  blocking collectives: 90.1 us -> 0 us
  waiting for transfers between devices: 41.2 us -> 94.2 us
  starting transfers between devices: 24.3 us -> 72.7 us
  matrix products: 14.3 us -> 8 us
  Pallas kernels: 7.19 us -> 13 us
  local copies, waits for them, and re-layouts: 12.6 us -> 18.1 us
    all_to_all x3 -> x0, blocking collectives: 90.1 us -> none  [exchange_dp(): return lax.all_to_all(blocks, ('y', 'z'), 0, 0, tiled=True)]
    all_to_all x1 -> x5, waiting for transfers between devices: 8.58 us -> 56.4 us  [exchange_dp(): return lax.all_to_all(blocks, ('y', 'z'), 0, 0, tiled=True)]
    all_to_all x1 -> x5, starting transfers between devices: 8.33 us -> 33.3 us  [exchange_dp(): return lax.all_to_all(blocks, ('y', 'z'), 0, 0, tiled=True)]
    ppermute x9 -> x18, starting transfers between devices: 12.3 us -> 26.7 us  [shift(): lax.ppermute(value, axis, [(src, (src + steps) % count) for src in range(...]
    pallas_call x1 -> x2, Pallas kernels: 7.19 us -> 13 us  [the longest x1 8.51 us: run_chain(): pl.pallas_call(chain_kernel, out_shape=(jax.ShapeDtypeStruct((SECTIONS, 1...]
    all_to_all x1, waiting for transfers between devices: 12.1 us -> 17.2 us  [body(): got_down = lax.all_to_all(part_down, 'z', 0, 0, tiled=True)]
    ppermute x0 -> x1, starting transfers between devices: none -> 5.03 us  [body(): piece = lax.ppermute(piece, ('x', 'y'), turn)]
    dot_general x5 -> x3, matrix products: 6.01 us -> 1.65 us  [the longest x1 1.19 us: body(): lax.dot_general(rep_part, head_part, (((2, 4), (0, 1)), ((), ())), prefer...]
  transfers between devices with their start and end apart: 14 -> 30, of which waited for: 11 -> 12; matrix products, arithmetic and copies ran while one was open for 5% -> 12% of each run, Pallas kernels for 0% -> 6%
where the time goes in v2:
time: 217 us; the launch traced here: 214 us
  waiting for transfers between devices  94.2 us (43%)
  starting transfers between devices  72.7 us (34%)
  local copies, waits for them, and re-layouts  18.1 us (8%)
  Pallas kernels  13 us (6%)
  matrix products  8 us (4%)
  other arithmetic  6.61 us (3%)
    all_to_all x5, waiting for transfers between devices, exchange_dp(): return lax.all_to_all(blocks, ('y', 'z'), 0, 0, tiled=True)  56.4 us
    all_to_all x5, starting transfers between devices, exchange_dp(): return lax.all_to_all(blocks, ('y', 'z'), 0, 0, tiled=True)  33.3 us
    ppermute x18, starting transfers between devices, shift(): lax.ppermute(value, axis, [(src, (src + steps) % count) for src in range(...  26.7 us
    ppermute x18, waiting for transfers between devices, shift(): lax.ppermute(value, axis, [(src, (src + steps) % count) for src in range(...  19.1 us
    all_to_all x1, waiting for transfers between devices, body(): got_down = lax.all_to_all(part_down, 'z', 0, 0, tiled=True)  17.2 us
    pallas_call x1, Pallas kernels, run_chain(): pl.pallas_call(chain_kernel, out_shape=(jax.ShapeDtypeStruct((SECTIONS, 1...  8.51 us
    all_to_all x1, starting transfers between devices, body(): got_down = lax.all_to_all(part_down, 'z', 0, 0, tiled=True)  6.8 us
    ppermute x1, starting transfers between devices, body(): piece = lax.ppermute(piece, ('x', 'y'), turn)  5.03 us
  transfers between devices with their start and end apart: 30, of which 12 were waited for; matrix products, arithmetic and copies ran while one was open for 12% of the time, Pallas kernels for 6%

profile of v2, /device:TPU:4, one launch (start us, length us, event | category | flops | bytes accessed | tf_op | source)
XLA Modules:
  0.0 213.9 jit_solution(935213724445286845)
XLA Ops:
  4.5 5.0 %collective-permute-start.7 = (bf16[32,128]{1,0:T(8,128)(2,1)S(1)}, bf16[32,128]{1,0:T(8,128)(2,1)S(1)}, u32[]{:S(2)}, u32[]{:S(2)}) collective-permute-start(bf16[32,128]{1,0:T(8,128)(2,1)S(1)} %constant_dynamic-slice_fusion), channel_id=1, source_target_pairs={{0,0},{8,64},{16,128},{24,192},{64,8},{72,72},{80,136},{88,200},{1... | collective-permute-start | bytes 24584 | tf_op jit(solution)/shard_map/ppermute | solution.py:198
  15.6 8.7 %collective-permute-done.6 = bf16[768,128]{0,1:T(8,128)(2,1)S(1)} collective-permute-done((bf16[768,128]{0,1:T(8,128)(2,1)S(1)}, bf16[768,128]{0,1:T(8,128)(2,1)S(1)}, u32[]{:S(2)}, u32[]{:S(2)}) %collective-permute-start.6) | collective-permute-done | bytes 196640 | tf_op jit(solution)/shard_map/ppermute | solution.py:25
  29.8 9.9 %all-to-all-start = ((bf16[32,64,128]{2,1,0:T(8,128)(2,1)}), bf16[32,64,128]{2,1,0:T(8,128)(2,1)S(1)}, u32[]{:S(2)}, u32[]{:S(2)}) async-start(bf16[32,64,128]{2,1,0:T(8,128)(2,1)} %pad_maximum_fusion.1), calls=%async_computation | async-start | bytes 1048576 | tf_op jit(solution)/shard_map/all_to_all | solution.py:42
  39.7 4.7 %multiply_convert_fusion = (bf16[256,128]{1,0:T(8,128)(2,1)S(1)}, bf16[256,128]{1,0:T(8,128)(2,1)}) fusion(bf16[256,8192]{1,0:T(8,128)(2,1)} %bitcast.98, bf16[1,8192,128]{2,1,0:T(8,128)(2,1)} %param.8), kind=kOutput, calls=%fused_computation.46 | convolution fusion | flops 537198592 | bytes 6422528 | tf_op jit(solution)/shard_map/dot_general | solution.py:220
  44.5 2.1 %collective-permute-start.19 = (bf16[256,128]{1,0:T(8,128)(2,1)S(1)}, bf16[256,128]{1,0:T(8,128)(2,1)}, u32[]{:S(2)}, u32[]{:S(2)}) collective-permute-start(bf16[256,128]{1,0:T(8,128)(2,1)S(1)} %get-tuple-element.23), channel_id=1, source_target_pairs={{0,64},{64,128},{128,192},{192,0},{1,65},{65,129},{129,193},{193,1... | collective-permute-start | bytes 196616 | tf_op jit(solution)/shard_map/ppermute | solution.py:25
  50.1 6.7 %all-to-all-done = bf16[32,64,128]{2,1,0:T(8,128)(2,1)S(1)} async-done(((bf16[32,64,128]{2,1,0:T(8,128)(2,1)}), bf16[32,64,128]{2,1,0:T(8,128)(2,1)S(1)}, u32[]{:S(2)}, u32[]{:S(2)}) %all-to-all-start) | async-done | bytes 524320 | tf_op jit(solution)/shard_map/all_to_all | solution.py:42
  57.5 5.9 %all-to-all-start.2 = ((bf16[32,32,128]{2,1,0:T(8,128)(2,1)}), bf16[32,32,128]{2,1,0:T(8,128)(2,1)S(1)}, u32[]{:S(2)}, u32[]{:S(2)}) async-start(bf16[32,32,128]{2,1,0:T(8,128)(2,1)} %broadcast_in_dim.81), calls=%async_computation.2 | async-start | bytes 524288 | tf_op jit(solution)/shard_map/all_to_all | solution.py:42
  65.4 10.2 %all-to-all-done.2 = bf16[32,32,128]{2,1,0:T(8,128)(2,1)S(1)} async-done(((bf16[32,32,128]{2,1,0:T(8,128)(2,1)}), bf16[32,32,128]{2,1,0:T(8,128)(2,1)S(1)}, u32[]{:S(2)}, u32[]{:S(2)}) %all-to-all-start.2) | async-done | bytes 262176 | tf_op jit(solution)/shard_map/all_to_all | solution.py:42
  75.6 2.1 %collective-permute-start.15 = (bf16[1024,128]{1,0:T(8,128)(2,1)S(1)}, bf16[1024,128]{1,0:T(8,128)(2,1)S(1)}, u32[]{:S(2)}, u32[]{:S(2)}) collective-permute-start(bf16[1024,128]{1,0:T(8,128)(2,1)S(1)} %bitcast.106), channel_id=1, source_target_pairs={{0,64},{64,128},{128,192},{192,0},{1,65},{65,129},{129,193},{193,1... | collective-permute-start | bytes 786440 | tf_op jit(solution)/shard_map/ppermute | solution.py:25
  77.7 3.6 %constant_dynamic-slice_fusion.4 = (bf16[256,2048]{1,0:T(8,128)(2,1)}, bf16[256,2048]{1,0:T(8,128)(2,1)}, bf16[256,2048]{1,0:T(8,128)(2,1)}) fusion(bf16[256,8192]{1,0:T(8,128)(2,1)} %bitcast.99, s32[]{:T(128)S(6)} %select_n.88, s32[]{:T(128)S(6)} %select_n.86, s32[]{:T(128)S(6)} %select_n.84), kind=kLoop, calls=%fused_computation.67 | loop fusion | bytes 6291468 | tf_op jit(solution)/shard_map/dynamic_slice | solution.py:229
  86.0 2.9 %collective-permute-start.10 = (f32[384,128]{1,0:T(8,128)S(1)}, f32[384,128]{1,0:T(8,128)S(1)}, u32[]{:S(2)}, u32[]{:S(2)}) collective-permute-start(f32[384,128]{1,0:T(8,128)S(1)} %fusion.26), channel_id=1, source_target_pairs={{0,128},{64,192},{128,0},{192,64},{1,129},{65,193},{129,1},{193,65... | collective-permute-start | bytes 589832 | tf_op jit(solution)/shard_map/ppermute | solution.py:25
  93.0 3.2 %collective-permute-done.13 = bf16[1024,128]{1,0:T(8,128)(2,1)S(1)} collective-permute-done((bf16[1024,128]{1,0:T(8,128)(2,1)S(1)}, bf16[1024,128]{1,0:T(8,128)(2,1)S(1)}, u32[]{:S(2)}, u32[]{:S(2)}) %collective-permute-start.13) | collective-permute-done | bytes 262176 | tf_op jit(solution)/shard_map/ppermute | solution.py:25
  102.4 4.1 %all-to-all-start.1 = ((f32[32,8,128]{2,1,0:T(8,128)}), f32[32,8,128]{2,1,0:T(8,128)S(1)}, u32[]{:S(2)}, u32[]{:S(2)}) async-start(f32[32,8,128]{2,1,0:T(8,128)} %broadcast_in_dim.80), calls=%async_computation.1 | async-start | bytes 262144 | tf_op jit(solution)/shard_map/all_to_all | solution.py:42
  108.9 28.8 %all-to-all-done.1.gram_ref = f32[32,8,128]{2,1,0:T(8,128)S(1)} async-done(((f32[32,8,128]{2,1,0:T(8,128)}), f32[32,8,128]{2,1,0:T(8,128)S(1)}, u32[]{:S(2)}, u32[]{:S(2)}) %all-to-all-start.1) | async-done | bytes 131104 | tf_op jit(solution)/shard_map/all_to_all | solution.py:42
  138.4 8.5 %mix_chain.1 = (bf16[8,128,128]{2,1,0:T(8,128)(2,1)}, bf16[256,128]{1,0:T(8,128)(2,1)}, f32[8,128]{1,0:T(8,128)}) custom-call(s32[2]{0:T(128)} %pad_add_fusion.where_ref, f32[32,8,128]{2,1,0:T(8,128)} %copy-done.4, f32[8,128]{1,0:T(8,128)} %fusion.20.mask_ref, bf16[256,128]{1,0:T(8,128)(2,1)} %slice.71.residual_ref, ...), custom_call_target="tpu_custom_call" | custom-call | tf_op jit(solution)/shard_map/mix_chain/pallas_call | solution.py:135
  146.9 9.6 %all-to-all-start.4 = ((bf16[32,32,128]{2,1,0:T(8,128)(2,1)}), bf16[32,32,128]{2,1,0:T(8,128)(2,1)S(1)}, u32[]{:S(2)}, u32[]{:S(2)}) async-start(bf16[32,32,128]{2,1,0:T(8,128)(2,1)} %bitcast.116), calls=%async_computation.4 | async-start | bytes 524288 | tf_op jit(solution)/shard_map/all_to_all | solution.py:42
  156.5 1.9 collective-permute-start.23
  158.4 2.7 %collective-permute-start.22 = (bf16[256,128]{1,0:T(8,128)(2,1)}, bf16[256,128]{1,0:T(8,128)(2,1)S(1)}, u32[]{:S(2)}, u32[]{:S(2)}) collective-permute-start(bf16[256,128]{1,0:T(8,128)(2,1)} %get-tuple-element.6.refs_4_), channel_id=1, source_target_pairs={{0,16},{8,24},{16,0},{24,8},{1,17},{9,25},{17,1},{25,9},{2,18},{10... | collective-permute-start | bytes 196616 | tf_op jit(solution)/shard_map/ppermute | solution.py:25
  163.0 3.2 %collective-permute-done.22.refs_6_ = bf16[256,128]{1,0:T(8,128)(2,1)S(1)} collective-permute-done((bf16[256,128]{1,0:T(8,128)(2,1)}, bf16[256,128]{1,0:T(8,128)(2,1)S(1)}, u32[]{:S(2)}, u32[]{:S(2)}) %collective-permute-start.22) | collective-permute-done | bytes 65568 | tf_op jit(solution)/shard_map/ppermute | solution.py:25
  166.9 4.5 %down_product.1 = bf16[8,128,256]{2,1,0:T(8,128)(2,1)} custom-call(s32[1]{0:T(128)} %bitcast.y_ref, bf16[256,8192]{1,0:T(8,128)(2,1)} %bitcast.100, bf16[256,2048]{1,0:T(8,128)(2,1)} %collective-permute-done.refs_1_, bf16[256,2048]{1,0:T(8,128)(2,1)} %collective-permute-done.1.refs_2_, bf16[256,2048]{1,0:T(8,128)(2,1)} %collective-permute-done.2.refs_3_, ...), custom_call_target="tpu_custom_call" | custom-call | tf_op jit(solution)/shard_map/down_product/pallas_call | solution.py:165
  171.4 6.8 %all-to-all-start.3 = ((bf16[8,128,256]{2,1,0:T(8,128)(2,1)}), bf16[8,128,256]{2,1,0:T(8,128)(2,1)S(1)}, u32[]{:S(2)}, u32[]{:S(2)}) async-start(bf16[8,128,256]{2,1,0:T(8,128)(2,1)} %down_product.1), calls=%async_computation.3 | async-start | bytes 1048576 | tf_op jit(solution)/shard_map/all_to_all | solution.py:277
  178.3 17.2 %all-to-all-done.3 = bf16[8,128,256]{2,1,0:T(8,128)(2,1)S(1)} async-done(((bf16[8,128,256]{2,1,0:T(8,128)(2,1)}), bf16[8,128,256]{2,1,0:T(8,128)(2,1)S(1)}, u32[]{:S(2)}, u32[]{:S(2)}) %all-to-all-start.3) | async-done | bytes 524320 | tf_op jit(solution)/shard_map/all_to_all | solution.py:277
  196.2 3.9 %all-to-all-start.5 = ((bf16[32,32,128]{2,1,0:T(8,128)(2,1)}), bf16[32,32,128]{2,1,0:T(8,128)(2,1)S(1)}, u32[]{:S(2)}, u32[]{:S(2)}) async-start(bf16[32,32,128]{2,1,0:T(8,128)(2,1)} %broadcast_in_dim.83), calls=%async_computation.5 | async-start | bytes 524288 | tf_op jit(solution)/shard_map/all_to_all | solution.py:42
  202.1 10.7 %all-to-all-done.5 = bf16[32,32,128]{2,1,0:T(8,128)(2,1)S(1)} async-done(((bf16[32,32,128]{2,1,0:T(8,128)(2,1)}), bf16[32,32,128]{2,1,0:T(8,128)(2,1)S(1)}, u32[]{:S(2)}, u32[]{:S(2)}) %all-to-all-start.5) | async-done | bytes 262176 | tf_op jit(solution)/shard_map/all_to_all | solution.py:42
  (130 shorter events, 45.8 us)
Async XLA Ops:
  4.5 24.4 %collective-permute-start.7 = (bf16[32,128]{1,0:T(8,128)(2,1)S(1)}, bf16[32,128]{1,0:T(8,128)(2,1)S(1)}, u32[]{:S(2)}, u32[]{:S(2)}) collective-permute-start(bf16[32,128]{1,0:T(8,128)(2,1)S(1)} %constant_dynamic-slice_fusion), channel_id=1, source_target_pairs={{0,0},{8,64},{16,128},{24,192},{64,8},{72,72},{80,136},{88,200},{1... | collective-permute-start | bytes 24584 | tf_op jit(solution)/shard_map/ppermute | solution.py:198
  12.9 11.3 %collective-permute-start.6 = (bf16[768,128]{0,1:T(8,128)(2,1)S(1)}, bf16[768,128]{0,1:T(8,128)(2,1)S(1)}, u32[]{:S(2)}, u32[]{:S(2)}) collective-permute-start(bf16[768,128]{0,1:T(8,128)(2,1)S(1)} %get-tuple-element.25), channel_id=1, source_target_pairs={{0,64},{64,128},{128,192},{192,0},{1,65},{65,129},{129,193},{193,1... | collective-permute-start | bytes 589832 | tf_op jit(solution)/shard_map/ppermute | solution.py:25
  14.0 10.2 %collective-permute-start.5 = (bf16[768,128]{0,1:T(8,128)(2,1)S(1)}, bf16[768,128]{0,1:T(8,128)(2,1)S(1)}, u32[]{:S(2)}, u32[]{:S(2)}) collective-permute-start(bf16[768,128]{0,1:T(8,128)(2,1)S(1)} %get-tuple-element.26), channel_id=1, source_target_pairs={{0,128},{64,192},{128,0},{192,64},{1,129},{65,193},{129,1},{193,65... | collective-permute-start | bytes 589832 | tf_op jit(solution)/shard_map/ppermute | solution.py:25
  14.0 12.1 %collective-permute-start.4 = (bf16[768,128]{0,1:T(8,128)(2,1)S(1)}, bf16[768,128]{0,1:T(8,128)(2,1)S(1)}, u32[]{:S(2)}, u32[]{:S(2)}) collective-permute-start(bf16[768,128]{0,1:T(8,128)(2,1)S(1)} %get-tuple-element.27), channel_id=1, source_target_pairs={{0,192},{64,0},{128,64},{192,128},{1,193},{65,1},{129,65},{193,129... | collective-permute-start | bytes 589832 | tf_op jit(solution)/shard_map/ppermute | solution.py:25
  29.8 26.9 %all-to-all-start = ((bf16[32,64,128]{2,1,0:T(8,128)(2,1)}), bf16[32,64,128]{2,1,0:T(8,128)(2,1)S(1)}, u32[]{:S(2)}, u32[]{:S(2)}) async-start(bf16[32,64,128]{2,1,0:T(8,128)(2,1)} %pad_maximum_fusion.1), calls=%async_computation | async-start | bytes 1048576 | tf_op jit(solution)/shard_map/all_to_all | solution.py:42
  44.5 37.0 %collective-permute-start.19 = (bf16[256,128]{1,0:T(8,128)(2,1)S(1)}, bf16[256,128]{1,0:T(8,128)(2,1)}, u32[]{:S(2)}, u32[]{:S(2)}) collective-permute-start(bf16[256,128]{1,0:T(8,128)(2,1)S(1)} %get-tuple-element.23), channel_id=1, source_target_pairs={{0,64},{64,128},{128,192},{192,0},{1,65},{65,129},{129,193},{193,1... | collective-permute-start | bytes 196616 | tf_op jit(solution)/shard_map/ppermute | solution.py:25
  46.6 37.3 %collective-permute-start.18 = (bf16[256,128]{1,0:T(8,128)(2,1)S(1)}, bf16[256,128]{1,0:T(8,128)(2,1)}, u32[]{:S(2)}, u32[]{:S(2)}) collective-permute-start(bf16[256,128]{1,0:T(8,128)(2,1)S(1)} %get-tuple-element.23), channel_id=1, source_target_pairs={{0,128},{64,192},{128,0},{192,64},{1,129},{65,193},{129,1},{193,65... | collective-permute-start | bytes 196616 | tf_op jit(solution)/shard_map/ppermute | solution.py:25
  47.3 37.1 %collective-permute-start.17 = (bf16[256,128]{1,0:T(8,128)(2,1)S(1)}, bf16[256,128]{1,0:T(8,128)(2,1)}, u32[]{:S(2)}, u32[]{:S(2)}) collective-permute-start(bf16[256,128]{1,0:T(8,128)(2,1)S(1)} %get-tuple-element.23), channel_id=1, source_target_pairs={{0,192},{64,0},{128,64},{192,128},{1,193},{65,1},{129,65},{193,129... | collective-permute-start | bytes 196616 | tf_op jit(solution)/shard_map/ppermute | solution.py:25
  57.5 18.0 %all-to-all-start.2 = ((bf16[32,32,128]{2,1,0:T(8,128)(2,1)}), bf16[32,32,128]{2,1,0:T(8,128)(2,1)S(1)}, u32[]{:S(2)}, u32[]{:S(2)}) async-start(bf16[32,32,128]{2,1,0:T(8,128)(2,1)} %broadcast_in_dim.81), calls=%async_computation.2 | async-start | bytes 524288 | tf_op jit(solution)/shard_map/all_to_all | solution.py:42
  65.1 17.2 %collective-permute-start.9 = (f32[384,128]{1,0:T(8,128)S(1)}, f32[384,128]{1,0:T(8,128)S(1)}, u32[]{:S(2)}, u32[]{:S(2)}) collective-permute-start(f32[384,128]{1,0:T(8,128)S(1)} %pad_maximum_fusion.7), channel_id=1, source_target_pairs={{0,32},{32,0},{1,33},{33,1},{2,34},{34,2},{3,35},{35,3},{4,36},{36... | collective-permute-start | bytes 589832 | tf_op jit(solution)/shard_map/ppermute | solution.py:29
  75.6 10.4 %collective-permute-start.15 = (bf16[1024,128]{1,0:T(8,128)(2,1)S(1)}, bf16[1024,128]{1,0:T(8,128)(2,1)S(1)}, u32[]{:S(2)}, u32[]{:S(2)}) collective-permute-start(bf16[1024,128]{1,0:T(8,128)(2,1)S(1)} %bitcast.106), channel_id=1, source_target_pairs={{0,64},{64,128},{128,192},{192,0},{1,65},{65,129},{129,193},{193,1... | collective-permute-start | bytes 786440 | tf_op jit(solution)/shard_map/ppermute | solution.py:25
  81.5 10.9 %collective-permute-start.14 = (bf16[1024,128]{1,0:T(8,128)(2,1)S(1)}, bf16[1024,128]{1,0:T(8,128)(2,1)S(1)}, u32[]{:S(2)}, u32[]{:S(2)}) collective-permute-start(bf16[1024,128]{1,0:T(8,128)(2,1)S(1)} %bitcast.107), channel_id=1, source_target_pairs={{0,128},{64,192},{128,0},{192,64},{1,129},{65,193},{129,1},{193,65... | collective-permute-start | bytes 786440 | tf_op jit(solution)/shard_map/ppermute | solution.py:25
  82.3 13.8 %collective-permute-start.13 = (bf16[1024,128]{1,0:T(8,128)(2,1)S(1)}, bf16[1024,128]{1,0:T(8,128)(2,1)S(1)}, u32[]{:S(2)}, u32[]{:S(2)}) collective-permute-start(bf16[1024,128]{1,0:T(8,128)(2,1)S(1)} %bitcast.108), channel_id=1, source_target_pairs={{0,192},{64,0},{128,64},{192,128},{1,193},{65,1},{129,65},{193,129... | collective-permute-start | bytes 786440 | tf_op jit(solution)/shard_map/ppermute | solution.py:25
  83.9 14.9 %collective-permute-start.12 = (f32[384,128]{1,0:T(8,128)S(1)}, f32[384,128]{1,0:T(8,128)S(1)}, u32[]{:S(2)}, u32[]{:S(2)}) collective-permute-start(f32[384,128]{1,0:T(8,128)S(1)} %fusion.26), channel_id=1, source_target_pairs={{0,64},{64,128},{128,192},{192,0},{1,65},{65,129},{129,193},{193,1... | collective-permute-start | bytes 589832 | tf_op jit(solution)/shard_map/ppermute | solution.py:25
  84.5 16.2 %collective-permute-start.11 = (f32[384,128]{1,0:T(8,128)S(1)}, f32[384,128]{1,0:T(8,128)S(1)}, u32[]{:S(2)}, u32[]{:S(2)}) collective-permute-start(f32[384,128]{1,0:T(8,128)S(1)} %fusion.26), channel_id=1, source_target_pairs={{0,192},{64,0},{128,64},{192,128},{1,193},{65,1},{129,65},{193,129... | collective-permute-start | bytes 589832 | tf_op jit(solution)/shard_map/ppermute | solution.py:25
  86.0 14.7 %collective-permute-start.10 = (f32[384,128]{1,0:T(8,128)S(1)}, f32[384,128]{1,0:T(8,128)S(1)}, u32[]{:S(2)}, u32[]{:S(2)}) collective-permute-start(f32[384,128]{1,0:T(8,128)S(1)} %fusion.26), channel_id=1, source_target_pairs={{0,128},{64,192},{128,0},{192,64},{1,129},{65,193},{129,1},{193,65... | collective-permute-start | bytes 589832 | tf_op jit(solution)/shard_map/ppermute | solution.py:25
  92.3 68.8 %collective-permute-start.2 = (bf16[256,2048]{1,0:T(8,128)(2,1)}, bf16[256,2048]{1,0:T(8,128)(2,1)}, u32[]{:S(2)}, u32[]{:S(2)}) collective-permute-start(bf16[256,2048]{1,0:T(8,128)(2,1)} %get-tuple-element.12), channel_id=1, source_target_pairs={{0,8},{8,16},{16,24},{24,0},{1,9},{9,17},{17,25},{25,1},{2,10},{10... | collective-permute-start | bytes 3145736 | tf_op jit(solution)/shard_map/ppermute | solution.py:25
  96.1 66.4 %collective-permute-start.1 = (bf16[256,2048]{1,0:T(8,128)(2,1)}, bf16[256,2048]{1,0:T(8,128)(2,1)}, u32[]{:S(2)}, u32[]{:S(2)}) collective-permute-start(bf16[256,2048]{1,0:T(8,128)(2,1)} %get-tuple-element.13), channel_id=1, source_target_pairs={{0,16},{8,24},{16,0},{24,8},{1,17},{9,25},{17,1},{25,9},{2,18},{10... | collective-permute-start | bytes 3145736 | tf_op jit(solution)/shard_map/ppermute | solution.py:25
  98.8 63.7 %collective-permute-start = (bf16[256,2048]{1,0:T(8,128)(2,1)}, bf16[256,2048]{1,0:T(8,128)(2,1)}, u32[]{:S(2)}, u32[]{:S(2)}) collective-permute-start(bf16[256,2048]{1,0:T(8,128)(2,1)} %get-tuple-element.14), channel_id=1, source_target_pairs={{0,24},{8,0},{16,8},{24,16},{1,25},{9,1},{17,9},{25,17},{2,26},{10... | collective-permute-start | bytes 3145736 | tf_op jit(solution)/shard_map/ppermute | solution.py:25
  100.7 37.1 %collective-permute-start.16 = (bf16[4,1024,128]{2,1,0:T(8,128)(2,1)S(1)}, bf16[4,1024,128]{2,1,0:T(8,128)(2,1)}, u32[]{:S(2)}, u32[]{:S(2)}) collective-permute-start(bf16[4,1024,128]{2,1,0:T(8,128)(2,1)S(1)} %pad_maximum_fusion.own_ref), channel_id=1, source_target_pairs={{0,32},{32,0},{1,33},{33,1},{2,34},{34,2},{3,35},{35,3},{4,36},{36... | collective-permute-start | bytes 3145736 | tf_op jit(solution)/shard_map/ppermute | solution.py:29
  102.4 35.3 %all-to-all-start.1 = ((f32[32,8,128]{2,1,0:T(8,128)}), f32[32,8,128]{2,1,0:T(8,128)S(1)}, u32[]{:S(2)}, u32[]{:S(2)}) async-start(f32[32,8,128]{2,1,0:T(8,128)} %broadcast_in_dim.80), calls=%async_computation.1 | async-start | bytes 262144 | tf_op jit(solution)/shard_map/all_to_all | solution.py:42
  146.9 24.5 %all-to-all-start.4 = ((bf16[32,32,128]{2,1,0:T(8,128)(2,1)}), bf16[32,32,128]{2,1,0:T(8,128)(2,1)S(1)}, u32[]{:S(2)}, u32[]{:S(2)}) async-start(bf16[32,32,128]{2,1,0:T(8,128)(2,1)} %bitcast.116), calls=%async_computation.4 | async-start | bytes 524288 | tf_op jit(solution)/shard_map/all_to_all | solution.py:42
  171.4 24.1 %all-to-all-start.3 = ((bf16[8,128,256]{2,1,0:T(8,128)(2,1)}), bf16[8,128,256]{2,1,0:T(8,128)(2,1)S(1)}, u32[]{:S(2)}, u32[]{:S(2)}) async-start(bf16[8,128,256]{2,1,0:T(8,128)(2,1)} %down_product.1), calls=%async_computation.3 | async-start | bytes 1048576 | tf_op jit(solution)/shard_map/all_to_all | solution.py:277
  196.2 16.6 %all-to-all-start.5 = ((bf16[32,32,128]{2,1,0:T(8,128)(2,1)}), bf16[32,32,128]{2,1,0:T(8,128)(2,1)S(1)}, u32[]{:S(2)}, u32[]{:S(2)}) async-start(bf16[32,32,128]{2,1,0:T(8,128)(2,1)} %broadcast_in_dim.83), calls=%async_computation.5 | async-start | bytes 524288 | tf_op jit(solution)/shard_map/all_to_all | solution.py:42
  (19 other events, 206.6 us)

commit v3 on v2

v3 whole, which is shorter than its diff:
```python
import jax
import jax.numpy as jnp
from jax import lax
from jax.experimental import pallas as pl
from jax.experimental.pallas import tpu as pltpu
from jax.sharding import Mesh
from jax.sharding import PartitionSpec as P


HEAD_OUT = 16
TASKS = 6
STEPS = 20
STEP_RATE = 3.0
NX = 4
NC = 2
NY = 4
NZ = 8
SECTIONS = NX * NC
DP = NY * NZ
BF16 = jnp.bfloat16
F32 = jnp.float32


def shift(value, axis, steps):
    count = lax.axis_size(axis)
    return lax.ppermute(value, axis, [(src, (src + steps) % count) for src in range(count)])


def from_later(value, steps):
    return lax.ppermute(value, "x", [(src, src - steps) for src in range(steps, NX)])


def swap_c(value):
    return lax.ppermute(value, "c", [(0, 1), (1, 0)])


def exchange_dp(blocks):
    return lax.all_to_all(blocks, ("y", "z"), 0, 0, tiled=True)


def at(value, index):
    return lax.dynamic_index_in_dim(value, index, 0, keepdims=False)


def rows_at(value, start, size):
    return lax.dynamic_slice_in_dim(value, start, size, 0)


def across(left, right):
    return lax.dot_general(left, right, (((0,), (0,)), ((), ())), preferred_element_type=F32)


VMEM = pl.BlockSpec(memory_space=pltpu.VMEM)
SMEM = pl.BlockSpec(memory_space=pltpu.SMEM)


def local_call(kernel, outs, where, *operands):
    return pl.pallas_call(
        kernel,
        out_shape=tuple(jax.ShapeDtypeStruct(shape, dtype) for shape, dtype in outs),
        in_specs=[SMEM] + [VMEM] * len(operands),
        out_specs=(VMEM,) * len(outs),
    )(where, *operands)


def pack_kernel(
    where_ref, piece_ref, heads_ref, up_ref, own_rep_ref, own_ref, partner_ref,
    got1_ref, got2_ref, got3_ref, sent_ref, factor_ref, rep_ref,
):
    my_x = where_ref[0]
    my_c = where_ref[1]
    my_stage = my_x * NC + my_c
    up_rows = up_ref[...]
    piece = piece_ref[...]
    for d in range(DP):
        sent_ref[d, 0:32, :] = piece
    gots = (None, got1_ref, got2_ref, got3_ref)
    for k in range(NX):
        for r in range(NC):
            stage = ((my_x + k) % NX) * NC + (my_c if r == 0 else 1 - my_c)
            slot = SECTIONS - 1 - stage
            if k == 0:
                rep_rows = own_rep_ref[256 * r : 256 * r + 256, :]
                factor = heads_ref[...] if r == 0 else partner_ref[...]
            else:
                rep_rows = gots[k][256 * r : 256 * r + 256, :]
                factor = gots[k][512 + 256 * r : 768 + 256 * r, :]
            if k or r:
                factor = jnp.where(stage > my_stage, factor, jnp.zeros_like(factor))
            rep_ref[stage] = rep_rows
            factor_ref[slot] = factor
            product = across(factor, up_rows).astype(BF16)
            for i in range(4):
                sent_ref[4 * slot + i, 32:64, :] = product[32 * i : 32 * i + 32]


def heads_kernel(where_ref, got_ref, rep_ref, target_ref, part_ref, cross_ref, head_ref):
    my_stage = where_ref[0] * NC + where_ref[1]
    for z in range(NZ):
        for y in range(NY):
            head_ref[128 * z + 32 * y : 128 * z + 32 * y + 32, :] = got_ref[NZ * y + z, 0:32, :]
    total = None
    square = None
    for z in range(NZ):
        head = head_ref[128 * z : 128 * z + 128, :]
        rep = jnp.concatenate([rep_ref[m, 32 * z : 32 * z + 32, :] for m in range(SECTIONS)], axis=0)
        term = jnp.dot(rep, head, preferred_element_type=F32)
        other = across(head, head)
        total = term if total is None else total + term
        square = other if square is None else square + other
    target = target_ref[...].astype(F32)
    for m in range(SECTIONS):
        rows = total[32 * m : 32 * m + 32]
        part_ref[32 * m : 32 * m + 32, :] = rows - jnp.where(m == my_stage, target, 0.0)
    part_ref[256:384, :] = square
    cross_ref[...] = jnp.sum(got_ref[:, 32:64, :].astype(F32), axis=0).astype(BF16)


def gram_kernel(where_ref, a_ref, b_ref, c_ref, d_ref, mask_ref, cross_ref, sent_ref, residual_ref):
    def value(ref, lo, size):
        return ref[lo : lo + size, :].astype(F32)

    def summed(lo, size):
        pair = value(a_ref, lo, size) + value(c_ref, lo, size)
        return pair + (value(b_ref, lo, size) + value(d_ref, lo, size))

    def squares(ref):
        return value(ref, 256, 128) + value(ref, 384, 128)

    residual = summed(0, 256).astype(BF16)
    residual_ref[...] = residual
    square = (squares(a_ref) + squares(c_ref)) + (squares(b_ref) + squares(d_ref))
    product = square * across(residual, residual)
    mask = mask_ref[...]
    high = lax.Precision.HIGHEST
    half = jnp.dot(mask[0:8], product, precision=high, preferred_element_type=F32)
    part = lax.dot_general(
        half, mask, (((1,), (1,)), ((), ())), precision=high, preferred_element_type=F32
    )
    top = part.astype(BF16)
    tile = jnp.concatenate([part, part - top.astype(F32)], axis=0).astype(BF16)
    cross = cross_ref[...]
    for d in range(DP):
        sent_ref[d, 0:32, :] = cross
        sent_ref[d, 32:48, :] = tile


LATER_ROWS = (1024, 768, 512, 256)
LATER_FROM = (0, 1024, 1792, 2304)
ALL_ROWS = 2560


def chain_kernel(
    where_ref, got_ref, mask_ref, residual_ref, active_ref, own_ref, other_ref,
    slope_own_ref, slope_other_ref,
    keep_ref, send1_ref, send2_ref, send3_ref, inner_ref, mix_ref, middle_ref,
):
    my_x = where_ref[0]
    my_c = where_ref[1]
    my_y = where_ref[2]
    my_stage = my_x * NC + my_c
    tiles = jnp.sum(got_ref[:, 32:48, :].astype(F32), axis=0)
    gram = tiles[0:8] + tiles[8:16]
    rows = lax.broadcasted_iota(jnp.int32, gram.shape, 0)
    lanes = lax.broadcasted_iota(jnp.int32, gram.shape, 1)
    diagonal = jnp.where(rows == lanes, gram, 0.0)
    trace_sum = jnp.sum(jnp.sum(diagonal, axis=1, keepdims=True), axis=0, keepdims=True) + 1e-06
    scaled = gram / trace_sum
    down0 = jnp.where(rows < TASKS, 1.0 / TASKS, 0.0)
    along0 = jnp.where(lanes < TASKS, 1.0 / TASKS, 0.0)

    def advance(counter, carry):
        down, along = carry
        step_down = jnp.sum(scaled * along, axis=1, keepdims=True)
        step_along = jnp.sum(scaled * down, axis=0, keepdims=True)
        total = jnp.sum(down, axis=0, keepdims=True)
        rate = -STEP_RATE / total
        down = down * jnp.exp(rate * step_down)
        along = along * jnp.exp(rate * step_along)
        return down, along

    down, along = lax.fori_loop(0, STEPS, advance, (down0, along0))
    total_along = jnp.sum(along[0:1], axis=1, keepdims=True)
    total_down = jnp.sum(down, axis=0, keepdims=True)
    mix_ref[...] = along / total_along
    column_weight = jnp.sum((down / total_down) * mask_ref[0:8], axis=0, keepdims=True)

    def cross(stage, source):
        away = (stage // NC - my_x) % NX
        start = jnp.where(away == 0, LATER_FROM[0], LATER_FROM[1])
        start = jnp.where(away == 2, LATER_FROM[2], start)
        start = jnp.where(away == 3, LATER_FROM[3], start)
        start = jnp.minimum(start + 128 * (SECTIONS - 1 - source), ALL_ROWS - 128)
        start = pl.multiple_of(start, 128)
        own = own_ref[pl.ds(start, 128), :]
        return jnp.where(my_c == stage % NC, own, other_ref[pl.ds(start, 128), :])

    def slope_of(stage):
        away = (stage // NC - my_x) % NX
        return jnp.where(my_c == stage % NC, slope_own_ref[away], slope_other_ref[away])

    active = active_ref[...]
    weighted = (residual_ref[...].astype(F32) * column_weight).astype(BF16)
    first = across(weighted, active)
    inners = {}
    for stage in range(SECTIONS - 1, -1, -1):
        branch = jnp.dot(weighted, cross(stage, stage), preferred_element_type=F32)
        for s in range(SECTIONS - 1, stage, -1):
            branch = branch + jnp.dot(inners[s], cross(stage, s), preferred_element_type=F32)
        inner = (branch * slope_of(stage).astype(F32)).astype(BF16)
        inners[stage] = inner

        @pl.when(stage == my_stage)
        def _():
            inner_ref[...] = inner
            send1_ref[256:512, :] = inner
            send2_ref[256:512, :] = inner
            send3_ref[256:512, :] = inner

        product = jnp.where(stage > my_stage, across(inner, active), 0.0)
        product = jnp.where(stage == my_stage, first, product)
        lo = 128 * (SECTIONS - 1 - stage)
        middle_ref[lo : lo + 128, :] = product.astype(BF16)

    for k, ref in enumerate((keep_ref, send1_ref, send2_ref, send3_ref)):
        start = pl.multiple_of(((my_y - k) % NY) * 256, 256)
        ref[0:256, :] = middle_ref[pl.ds(start, 256), :]


def down_kernel(
    y_ref, x0_ref, x1_ref, x2a_ref, x2b_ref, x3_ref, inner_ref, keep_ref, got1_ref, got2_ref, got3_ref,
    out_ref,
):
    step = pl.program_id(0)
    x2 = jnp.where(step < 2, x2a_ref[...], x2b_ref[...])
    total = across(inner_ref[...], x0_ref[...])
    total = total + across(got1_ref[256:512, :], x1_ref[...])
    total = total + across(got2_ref[256:512, :], x2)
    total = total + across(got3_ref[256:512, :], x3_ref[...])
    total = total.astype(BF16)
    for j in range(2):
        for h in range(2):
            lo = 256 * j + 128 * h
            out_ref[j, 128 * h : 128 * h + 128, :] = total[:, lo : lo + 128]
        start = pl.multiple_of((2 * step + j) * 32, 32)
        rows = [ref[pl.ds(start, 32), :].astype(F32) for ref in (keep_ref, got1_ref, got2_ref, got3_ref)]
        out_ref[j, 256:288, :] = ((rows[0] + rows[1]) + (rows[2] + rows[3])).astype(BF16)


def run_down(my_y, saved, x1, x2a, x2b, x3, inner, keep, got1, got2, got3):
    cols = 512
    whole = lambda value: pl.BlockSpec(value.shape, lambda i, y: (0, 0))
    block = (256, cols)
    return pl.pallas_call(
        down_kernel,
        grid_spec=pltpu.PrefetchScalarGridSpec(
            num_scalar_prefetch=1,
            grid=(4,),
            in_specs=[
                pl.BlockSpec(block, lambda i, y: (0, 4 * y[0] + i)),
                pl.BlockSpec(block, lambda i, y: (0, i)),
                pl.BlockSpec(block, lambda i, y: (0, jnp.minimum(i, 1))),
                pl.BlockSpec(block, lambda i, y: (0, jnp.maximum(i - 2, 0))),
                pl.BlockSpec(block, lambda i, y: (0, i)),
                whole(inner), whole(keep), whole(got1), whole(got2), whole(got3),
            ],
            out_specs=pl.BlockSpec((2, 288, 128), lambda i, y: (i, 0, 0)),
        ),
        out_shape=jax.ShapeDtypeStruct((NZ, 288, 128), BF16),
        name="down_product",
    )(my_y.reshape(1), saved, x1, x2a, x2b, x3, inner, keep, got1, got2, got3)


def stages(
    section_inputs, adapter_down, adapter_up, representation, head_weights, head_targets, head_task
):
    my_x = lax.axis_index("x")
    my_c = lax.axis_index("c")
    my_y = lax.axis_index("y")
    my_dp = my_y * NZ + lax.axis_index("z")
    where = jnp.stack([my_x, my_c, my_y]).astype(jnp.int32)
    dim_model = section_inputs.shape[3]
    saved = section_inputs[0].reshape(-1, dim_model)
    down_map = adapter_down[0]
    up_map = adapter_up[0]
    heads = head_weights
    share, rank = heads.shape
    tok = representation.shape[1]
    column_task = jnp.repeat(head_task[:, 0], HEAD_OUT)
    mask = (column_task[None, :] == jnp.arange(rank, dtype=jnp.int32)[:, None]).astype(F32)

    piece = rows_at(heads, my_c * 128 + my_x * 32, 32)
    turn = [(a * NY + b, b * NY + a) for a in range(NX) for b in range(NY)]
    piece = lax.ppermute(piece, ("x", "y"), turn)

    blocks = representation[0].reshape(tok, NX, NZ, NC, 128).transpose(3, 1, 2, 0, 4)
    blocks = blocks.reshape(NC, NX, NZ * tok, 128)
    down_rows = rows_at(down_map, my_dp * share, share)
    swapped = swap_c(at(blocks, 1 - my_c))
    partner = swap_c(down_rows)
    pair = jnp.concatenate([at(blocks, my_c), swapped], axis=1)
    gots = []
    for k in range(1, NX):
        sent = jnp.concatenate([at(pair, (my_x - k) % NX), down_rows, partner], axis=0)
        gots.append(shift(sent, "x", -k))

    wide = dim_model // NY

    def cut(index, k, lo, size):
        return lax.dynamic_slice_in_dim(saved, ((index - k) % NY) * wide + lo, size, 1)

    x1 = shift(cut(my_y, 1, 0, wide), "y", -1)
    x3 = shift(cut(my_y, 3, 0, wide), "y", -3)

    up_rows = rows_at(up_map, my_dp * share, share)
    sent, factors, rep = local_call(
        pack_kernel,
        [((DP, 64, rank), BF16), ((SECTIONS, share, rank), BF16), ((SECTIONS, NZ * tok, rank), BF16)],
        where, piece, heads, up_rows, at(pair, my_x), down_rows, partner, *gots,
    )

    preact = jnp.dot(saved, down_map, preferred_element_type=F32)
    logistic = jax.nn.sigmoid(preact)
    active = (preact * logistic).astype(BF16)
    slope = (logistic * (1.0 + preact * (1.0 - logistic))).astype(BF16)
    slope_own = jnp.stack([slope] + [from_later(slope, k) for k in range(1, NX)])
    slope_other = swap_c(slope_own)

    got = exchange_dp(sent)
    part, cross_rows, _ = local_call(
        heads_kernel,
        [((384, rank), F32), ((32, rank), BF16), ((1024, rank), BF16)],
        where, got, rep, head_targets[0],
    )
    part = part + swap_c(part)
    top = part.astype(BF16)
    low = (part[256:] - top[256:].astype(F32)).astype(BF16)
    halves = jnp.concatenate([top, low], axis=0)
    others = [shift(halves, "x", -k) for k in range(1, NX)]
    x2a = shift(cut(my_y, 2, 0, wide // 2), "y", -2)
    sent, residual = local_call(
        gram_kernel,
        [((DP, 48, rank), BF16), ((256, rank), BF16)],
        where, halves, *others, mask, cross_rows,
    )
    got = exchange_dp(sent)
    cross = got[:, :32].reshape(-1, rank)
    kept = [cross]
    for k in range(1, NX):
        kept.append(from_later(cross[: LATER_ROWS[k]], k))
    x2b = shift(cut(my_y, 2, wide // 2, wide // 2), "y", -2)
    cross_own = jnp.concatenate(kept, axis=0)
    cross_other = swap_c(cross_own)
    keep, send1, send2, send3, inner, mix, _ = local_call(
        chain_kernel,
        [((256, rank), BF16)] + [((512, rank), BF16)] * 3
        + [((256, rank), BF16), ((8, rank), F32), ((1024, rank), BF16)],
        where, got, mask, residual, active, cross_own, cross_other, slope_own, slope_other,
    )
    got1 = shift(send1, "y", -1)
    got2 = shift(send2, "y", -2)
    got3 = shift(send3, "y", -3)
    part_down = run_down(my_y, saved, x1, x2a, x2b, x3, inner, keep, got1, got2, got3)
    got = lax.all_to_all(part_down, "z", 0, 0, tiled=True)
    total = jnp.sum(got.astype(F32), axis=0)
    rows = total[256:].astype(BF16)
    middle = exchange_dp(jnp.broadcast_to(rows[None], (DP, 32, rank)))
    middle = middle.reshape(SECTIONS, rank, rank)
    grad_up = lax.dot_general(
        factors, middle, (((0, 2), (0, 1)), ((), ())), preferred_element_type=F32
    )
    grad_down = jnp.concatenate([total[:128].T, total[128:256].T], axis=0)
    return (grad_down[None], grad_up[None], mix[0, :TASKS])


def solution(mesh):
    fine = Mesh(mesh.devices.reshape(NX, NC, NY, NZ), ("x", "c", "y", "z"))
    section = ("x", "c")
    dp = ("y", "z")
    in_specs = (
        P(section, None, dp, None),
        P(section, None, None),
        P(section, None, None),
        P(section, dp, None),
        P(dp, None),
        P(section, dp, None),
        P(),
    )
    out_specs = (P(section, dp, None), P(section, dp, None), P())
    return jax.shard_map(stages, mesh=fine, in_specs=in_specs, out_specs=out_specs, check_vma=False)
```

time: 217 us -> 201 us (0.926)
  blocking collectives: 0 us -> 46 us
  waiting for transfers between devices: 94.2 us -> 56.9 us
  starting transfers between devices: 72.7 us -> 48.7 us
  Pallas kernels: 13 us -> 19.6 us
  matrix products: 8 us -> 5.01 us
    all_to_all x0 -> x2, blocking collectives: none -> 46 us  [the longest x1 25.5 us: exchange_dp(): return lax.all_to_all(blocks, ('y', 'z'), 0, 0, tiled=True)]
    all_to_all x5 -> x2, waiting for transfers between devices: 56.4 us -> 12.7 us  [exchange_dp(): return lax.all_to_all(blocks, ('y', 'z'), 0, 0, tiled=True)]
    all_to_all x5 -> x2, starting transfers between devices: 33.3 us -> 9.54 us  [exchange_dp(): return lax.all_to_all(blocks, ('y', 'z'), 0, 0, tiled=True)]
    all_to_all x1 -> x0, waiting for transfers between devices: 17.2 us -> none  [body(): got_down = lax.all_to_all(part_down, 'z', 0, 0, tiled=True)]
    ppermute x18 -> x13, waiting for transfers between devices: 19.1 us -> 35.4 us  [shift(): lax.ppermute(value, axis, [(src, (src + steps) % count) for src in range(...]
    ppermute x1 -> x7, starting transfers between devices: 5.03 us -> 17.7 us  [the longest x6 13 us: from_later(): lax.ppermute(value, 'x', [(src, src - steps) for src in range(steps, NX)])]
    all_to_all x1 -> x0, starting transfers between devices: 6.8 us -> none  [body(): got_down = lax.all_to_all(part_down, 'z', 0, 0, tiled=True)]
    ppermute x18 -> x13, starting transfers between devices: 26.7 us -> 20.2 us  [shift(): lax.ppermute(value, axis, [(src, (src + steps) % count) for src in range(...]
  transfers between devices with their start and end apart: 30 -> 27, of which waited for: 12 -> 12; matrix products, arithmetic and copies ran while one was open for 12% -> 9% of each run, Pallas kernels for 6% -> 4%
where the time goes in v3:
time: 201 us; the launch traced here: 198 us
  waiting for transfers between devices  56.9 us (28%)
  starting transfers between devices  48.7 us (24%)
  blocking collectives  46 us (23%)
  Pallas kernels  19.6 us (10%)
  local copies, waits for them, and re-layouts  16.2 us (8%)
  matrix products  5.01 us (2%)
  other arithmetic  4.91 us (2%)
    ppermute x13, waiting for transfers between devices, shift(): lax.ppermute(value, axis, [(src, (src + steps) % count) for src in range(...  35.4 us
    all_to_all x1, blocking collectives, exchange_dp(): return lax.all_to_all(blocks, ('y', 'z'), 0, 0, tiled=True)  25.5 us
    all_to_all x1, blocking collectives, stages(): got = lax.all_to_all(part_down, 'z', 0, 0, tiled=True)  20.5 us
    ppermute x13, starting transfers between devices, shift(): lax.ppermute(value, axis, [(src, (src + steps) % count) for src in range(...  20.2 us
    pallas_call x4, Pallas kernels, local_call(): pl.pallas_call(kernel, out_shape=tuple((jax.ShapeDtypeStruct(shape, dtype...  14.9 us
    ppermute x6, starting transfers between devices, from_later(): lax.ppermute(value, 'x', [(src, src - steps) for src in range(steps, NX)])  13 us
    all_to_all x2, waiting for transfers between devices, exchange_dp(): return lax.all_to_all(blocks, ('y', 'z'), 0, 0, tiled=True)  12.7 us
    all_to_all x2, starting transfers between devices, exchange_dp(): return lax.all_to_all(blocks, ('y', 'z'), 0, 0, tiled=True)  9.54 us
  transfers between devices with their start and end apart: 27, of which 12 were waited for; matrix products, arithmetic and copies ran while one was open for 9% of the time, Pallas kernels for 4%

profile of v3, /device:TPU:4, one launch (start us, length us, event | category | flops | bytes accessed | tf_op | source)
XLA Modules:
  0.0 198.5 jit_solution(4135140000971106059)
XLA Ops:
  5.6 2.7 %collective-permute-start.8 = (bf16[1024,128]{1,0:T(8,128)(2,1)S(1)}, bf16[1024,128]{1,0:T(8,128)(2,1)S(1)}, u32[]{:S(2)}, u32[]{:S(2)}) collective-permute-start(bf16[1024,128]{1,0:T(8,128)(2,1)S(1)} %get-tuple-element.49), channel_id=1, source_target_pairs={{0,128},{64,192},{128,0},{192,64},{1,129},{65,193},{129,1},{193,65... | collective-permute-start | bytes 786440 | tf_op jit(solution)/shard_map/ppermute | solution.py:26
  10.6 4.6 %collective-permute-start.4 = (bf16[32,128]{1,0:T(8,128)(2,1)S(1)}, bf16[32,128]{1,0:T(8,128)(2,1)S(1)}, u32[]{:S(2)}, u32[]{:S(2)}) collective-permute-start(bf16[32,128]{1,0:T(8,128)(2,1)S(1)} %constant_dynamic-slice_fusion), channel_id=1, source_target_pairs={{0,0},{8,64},{16,128},{24,192},{64,8},{72,72},{80,136},{88,200},{1... | collective-permute-start | bytes 24584 | tf_op jit(solution)/shard_map/ppermute | solution.py:294
  17.3 6.4 %collective-permute-done.4.piece_ref = bf16[32,128]{1,0:T(8,128)(2,1)S(1)} collective-permute-done((bf16[32,128]{1,0:T(8,128)(2,1)S(1)}, bf16[32,128]{1,0:T(8,128)(2,1)S(1)}, u32[]{:S(2)}, u32[]{:S(2)}) %collective-permute-start.4) | collective-permute-done | bytes 8224 | tf_op jit(solution)/shard_map/ppermute | solution.py:294
  24.7 2.7 %shard_map.94 = (bf16[32,64,128]{2,1,0:T(8,128)(2,1)}, bf16[8,256,128]{2,1,0:T(8,128)(2,1)}, bf16[8,256,128]{2,1,0:T(8,128)(2,1)}) custom-call(s32[3]{0:T(128)} %pad_add_fusion.where_ref, bf16[32,128]{1,0:T(8,128)(2,1)} %copy-done.23, bf16[256,128]{1,0:T(8,128)(2,1)} %heads_ref.1, bf16[256,128]{1,0:T(8,128)(2,1)} %dynamic-slice_bitcast_fusion.3.up_ref, ...), custom_call_target="tpu_custom_call" | custom-call | tf_op jit(solution)/shard_map/pallas_call | solution.py:58
  27.4 25.5 %all_to_all.20.got_ref = bf16[32,64,128]{2,1,0:T(8,128)(2,1)} all-to-all(bf16[32,64,128]{2,1,0:T(8,128)(2,1)} %get-tuple-element.16), channel_id=1, replica_groups=mesh['x'=4,'c'=2,'y'=4,'z'=8] {'y','z'}, dimensions={0} | all-to-all | bytes 1048576 | tf_op jit(solution)/shard_map/all_to_all | solution.py:38
  52.8 2.3 %shard_map.95 = (f32[384,128]{1,0:T(8,128)}, bf16[32,128]{1,0:T(8,128)(2,1)}, bf16[1024,128]{1,0:T(8,128)(2,1)}) custom-call(s32[3]{0:T(128)} %pad_add_fusion.where_ref, bf16[32,64,128]{2,1,0:T(8,128)(2,1)} %all_to_all.20.got_ref, bf16[8,256,128]{2,1,0:T(8,128)(2,1)} %get-tuple-element.17.rep_ref, bf16[32,128]{1,0:T(8,128)(2,1)} %bitcast.67), custom_call_target="tpu_custom_call" | custom-call | tf_op jit(solution)/shard_map/pallas_call | solution.py:58
  58.0 3.3 %collective-permute-start.12 = (bf16[512,128]{1,0:T(8,128)(2,1)S(1)}, bf16[512,128]{1,0:T(8,128)(2,1)S(1)}, u32[]{:S(2)}, u32[]{:S(2)}) collective-permute-start(bf16[512,128]{1,0:T(8,128)(2,1)S(1)} %pad_maximum_fusion.8.a_ref), channel_id=1, source_target_pairs={{0,128},{64,192},{128,0},{192,64},{1,129},{65,193},{129,1},{193,65... | collective-permute-start | bytes 393224 | tf_op jit(solution)/shard_map/ppermute | solution.py:26
  68.5 2.5 %shard_map.96 = (bf16[32,48,128]{2,1,0:T(8,128)(2,1)}, bf16[256,128]{1,0:T(8,128)(2,1)}) custom-call(s32[3]{0:T(128)} %pad_add_fusion.where_ref, bf16[512,128]{1,0:T(8,128)(2,1)} %copy-done.8, bf16[512,128]{1,0:T(8,128)(2,1)} %copy-done.18, bf16[512,128]{1,0:T(8,128)(2,1)} %copy-done.19, bf16[512,128]{1,0:T(8,128)(2,1)} %copy-done.20, ...), custom_call_target="tpu_custom_call" | custom-call | tf_op jit(solution)/shard_map/pallas_call | solution.py:58
  71.0 5.7 %all-to-all-start.1 = ((bf16[32,48,128]{2,1,0:T(8,128)(2,1)}), bf16[32,48,128]{2,1,0:T(8,128)(2,1)S(1)}, u32[]{:S(2)}, u32[]{:S(2)}) async-start(bf16[32,48,128]{2,1,0:T(8,128)(2,1)} %get-tuple-element.20), calls=%async_computation.1 | async-start | bytes 786432 | tf_op jit(solution)/shard_map/all_to_all | solution.py:38
  76.7 4.1 %multiply_convert_fusion = (bf16[256,128]{1,0:T(8,128)(2,1)S(1)}, bf16[256,128]{1,0:T(8,128)(2,1)}) fusion(bf16[256,8192]{1,0:T(8,128)(2,1)} %bitcast.52, bf16[1,8192,128]{2,1,0:T(8,128)(2,1)S(1)} %copy-done), kind=kOutput, calls=%fused_computation.32 | convolution fusion | flops 537198592 | bytes 6422528 | tf_op jit(solution)/shard_map/dot_general | solution.py:322
  80.8 2.5 %collective-permute-start.18 = (bf16[256,128]{1,0:T(8,128)(2,1)S(1)}, bf16[256,128]{1,0:T(8,128)(2,1)S(1)}, u32[]{:S(2)}, u32[]{:S(2)}) collective-permute-start(bf16[256,128]{1,0:T(8,128)(2,1)S(1)} %get-tuple-element.46), channel_id=1, source_target_pairs={{64,0},{128,64},{192,128},{65,1},{129,65},{193,129},{66,2},{130,66... | collective-permute-start | bytes 196616 | tf_op jit(solution)/shard_map/ppermute | solution.py:30
  83.2 3.4 %collective-permute-start.19 = (bf16[256,128]{1,0:T(8,128)(2,1)S(1)}, bf16[256,128]{1,0:T(8,128)(2,1)S(1)}, u32[]{:S(2)}, u32[]{:S(2)}) collective-permute-start(bf16[256,128]{1,0:T(8,128)(2,1)S(1)} %get-tuple-element.46), channel_id=1, source_target_pairs={{128,0},{192,64},{129,1},{193,65},{130,2},{194,66},{131,3},{195,67... | collective-permute-start | bytes 196616 | tf_op jit(solution)/shard_map/ppermute | solution.py:30
  87.4 3.8 %all-to-all-done.1.got_ref = bf16[32,48,128]{2,1,0:T(8,128)(2,1)S(1)} async-done(((bf16[32,48,128]{2,1,0:T(8,128)(2,1)}), bf16[32,48,128]{2,1,0:T(8,128)(2,1)S(1)}, u32[]{:S(2)}, u32[]{:S(2)}) %all-to-all-start.1) | async-done | bytes 393248 | tf_op jit(solution)/shard_map/all_to_all | solution.py:38
  93.2 3.9 %collective-permute-start.15 = (bf16[512,128]{1,0:T(8,128)(2,1)S(1)}, bf16[512,128]{1,0:T(8,128)(2,1)S(1)}, u32[]{:S(2)}, u32[]{:S(2)}) collective-permute-start(bf16[512,128]{1,0:T(8,128)(2,1)S(1)} %bitcast.61), channel_id=1, source_target_pairs={{128,0},{192,64},{129,1},{193,65},{130,2},{194,66},{131,3},{195,67... | collective-permute-start | bytes 393224 | tf_op jit(solution)/shard_map/ppermute | solution.py:30
  97.1 3.2 %constant_dynamic-slice_fusion.1 = (bf16[256,2048]{1,0:T(8,128)(2,1)}, bf16[256,2048]{1,0:T(8,128)(2,1)}) fusion(bf16[256,8192]{1,0:T(8,128)(2,1)} %bitcast.53, s32[]{:T(128)S(6)} %select_n.74, s32[]{:T(128)S(6)} %select_n.69), kind=kLoop, calls=%fused_computation.45 | loop fusion | bytes 4194312 | tf_op jit(solution)/shard_map/dynamic_slice | solution.py:310
  113.1 7.4 %shard_map.97 = (bf16[256,128]{1,0:T(8,128)(2,1)}, bf16[512,128]{1,0:T(8,128)(2,1)}, bf16[512,128]{1,0:T(8,128)(2,1)}, bf16[512,128]{1,0:T(8,128)(2,1)}, bf16[25...) custom-call(s32[3]{0:T(128)} %pad_add_fusion.where_ref, bf16[32,48,128]{2,1,0:T(8,128)(2,1)} %copy-done.1, ...), custom_call_target="tpu_custom_call" | custom-call | tf_op jit(solution)/shard_map/pallas_call | solution.py:58
  120.5 2.9 %collective-permute-start.22 = (bf16[512,128]{1,0:T(8,128)(2,1)}, bf16[512,128]{1,0:T(8,128)(2,1)S(1)}, u32[]{:S(2)}, u32[]{:S(2)}) collective-permute-start(bf16[512,128]{1,0:T(8,128)(2,1)} %get-tuple-element.24), channel_id=1, source_target_pairs={{0,24},{8,0},{16,8},{24,16},{1,25},{9,1},{17,9},{25,17},{2,26},{10... | collective-permute-start | bytes 393224 | tf_op jit(solution)/shard_map/ppermute | solution.py:26
  123.3 16.6 %collective-permute-done.1.x2a_ref = bf16[256,1024]{1,0:T(8,128)(2,1)S(1)} collective-permute-done((bf16[256,1024]{1,0:T(8,128)(2,1)}, bf16[256,1024]{1,0:T(8,128)(2,1)S(1)}, u32[]{:S(2)}, u32[]{:S(2)}) %collective-permute-start.1) | collective-permute-done | bytes 524320 | tf_op jit(solution)/shard_map/ppermute | solution.py:26
  141.4 8.3 %collective-permute-done.2.x2b_ref = bf16[256,1024]{1,0:T(8,128)(2,1)} collective-permute-done((bf16[256,1024]{1,0:T(8,128)(2,1)}, bf16[256,1024]{1,0:T(8,128)(2,1)}, u32[]{:S(2)}, u32[]{:S(2)}) %collective-permute-start.2) | collective-permute-done | bytes 524320 | tf_op jit(solution)/shard_map/ppermute | solution.py:26
  151.0 5.1 %collective-permute-done.24.got3_ref = bf16[512,128]{1,0:T(8,128)(2,1)S(1)} collective-permute-done((bf16[512,128]{1,0:T(8,128)(2,1)}, bf16[512,128]{1,0:T(8,128)(2,1)S(1)}, u32[]{:S(2)}, u32[]{:S(2)}) %collective-permute-start.24) | collective-permute-done | bytes 131104 | tf_op jit(solution)/shard_map/ppermute | solution.py:26
  156.7 4.7 %down_product.1 = bf16[8,288,128]{2,1,0:T(8,128)(2,1)} custom-call(s32[1]{0:T(128)} %bitcast.y_ref, bf16[256,8192]{1,0:T(8,128)(2,1)} %bitcast.55, bf16[256,2048]{1,0:T(8,128)(2,1)} %collective-permute-done.x1_ref, bf16[256,1024]{1,0:T(8,128)(2,1)} %copy-done.6, bf16[256,1024]{1,0:T(8,128)(2,1)} %collective-permute-done.2.x2b_ref, ...), custom_call_target="tpu_custom_call" | custom-call | tf_op jit(solution)/shard_map/down_product/pallas_call | solution.py:254
  161.5 20.5 %all_to_all.21 = bf16[8,288,128]{2,1,0:T(8,128)(2,1)S(1)} all-to-all(bf16[8,288,128]{2,1,0:T(8,128)(2,1)} %down_product.1), channel_id=1, replica_groups=mesh['x'=4,'c'=2,'y'=4,'z'=8] {'z'}, dimensions={0} | all-to-all | bytes 1179648 | tf_op jit(solution)/shard_map/all_to_all | solution.py:364
  182.9 3.9 %all-to-all-start.3 = ((bf16[32,32,128]{2,1,0:T(8,128)(2,1)}), bf16[32,32,128]{2,1,0:T(8,128)(2,1)S(1)}, u32[]{:S(2)}, u32[]{:S(2)}) async-start(bf16[32,32,128]{2,1,0:T(8,128)(2,1)} %broadcast_in_dim.18), calls=%async_computation.3 | async-start | bytes 524288 | tf_op jit(solution)/shard_map/all_to_all | solution.py:38
  188.7 8.8 %all-to-all-done.3 = bf16[32,32,128]{2,1,0:T(8,128)(2,1)S(1)} async-done(((bf16[32,32,128]{2,1,0:T(8,128)(2,1)}), bf16[32,32,128]{2,1,0:T(8,128)(2,1)S(1)}, u32[]{:S(2)}, u32[]{:S(2)}) %all-to-all-start.3) | async-done | bytes 262176 | tf_op jit(solution)/shard_map/all_to_all | solution.py:38
  (119 shorter events, 42.6 us)
Async XLA Ops:
  2.8 2.2 %collective-permute-start.6 = (bf16[256,128]{1,0:T(8,128)(2,1)S(1)}, bf16[256,128]{1,0:T(8,128)(2,1)S(1)}, u32[]{:S(2)}, u32[]{:S(2)}) collective-permute-start(bf16[256,128]{1,0:T(8,128)(2,1)S(1)} %dynamic-slice_bitcast_fusion.2.own_ref), channel_id=1, source_target_pairs={{0,32},{32,0},{1,33},{33,1},{2,34},{34,2},{3,35},{35,3},{4,36},{36... | collective-permute-start | bytes 196616 | tf_op jit(solution)/shard_map/ppermute | solution.py:34
  5.0 18.8 %collective-permute-start.7 = (bf16[1024,128]{1,0:T(8,128)(2,1)S(1)}, bf16[1024,128]{1,0:T(8,128)(2,1)S(1)}, u32[]{:S(2)}, u32[]{:S(2)}) collective-permute-start(bf16[1024,128]{1,0:T(8,128)(2,1)S(1)} %get-tuple-element.50), channel_id=1, source_target_pairs={{0,192},{64,0},{128,64},{192,128},{1,193},{65,1},{129,65},{193,129... | collective-permute-start | bytes 786440 | tf_op jit(solution)/shard_map/ppermute | solution.py:26
  5.6 18.1 %collective-permute-start.8 = (bf16[1024,128]{1,0:T(8,128)(2,1)S(1)}, bf16[1024,128]{1,0:T(8,128)(2,1)S(1)}, u32[]{:S(2)}, u32[]{:S(2)}) collective-permute-start(bf16[1024,128]{1,0:T(8,128)(2,1)S(1)} %get-tuple-element.49), channel_id=1, source_target_pairs={{0,128},{64,192},{128,0},{192,64},{1,129},{65,193},{129,1},{193,65... | collective-permute-start | bytes 786440 | tf_op jit(solution)/shard_map/ppermute | solution.py:26
  8.3 15.4 %collective-permute-start.9 = (bf16[1024,128]{1,0:T(8,128)(2,1)S(1)}, bf16[1024,128]{1,0:T(8,128)(2,1)S(1)}, u32[]{:S(2)}, u32[]{:S(2)}) collective-permute-start(bf16[1024,128]{1,0:T(8,128)(2,1)S(1)} %get-tuple-element.48), channel_id=1, source_target_pairs={{0,64},{64,128},{128,192},{192,0},{1,65},{65,129},{129,193},{193,1... | collective-permute-start | bytes 786440 | tf_op jit(solution)/shard_map/ppermute | solution.py:26
  10.6 13.1 %collective-permute-start.4 = (bf16[32,128]{1,0:T(8,128)(2,1)S(1)}, bf16[32,128]{1,0:T(8,128)(2,1)S(1)}, u32[]{:S(2)}, u32[]{:S(2)}) collective-permute-start(bf16[32,128]{1,0:T(8,128)(2,1)S(1)} %constant_dynamic-slice_fusion), channel_id=1, source_target_pairs={{0,0},{8,64},{16,128},{24,192},{64,8},{72,72},{80,136},{88,200},{1... | collective-permute-start | bytes 24584 | tf_op jit(solution)/shard_map/ppermute | solution.py:294
  57.8 5.9 %collective-permute-start.11 = (bf16[512,128]{1,0:T(8,128)(2,1)S(1)}, bf16[512,128]{1,0:T(8,128)(2,1)S(1)}, u32[]{:S(2)}, u32[]{:S(2)}) collective-permute-start(bf16[512,128]{1,0:T(8,128)(2,1)S(1)} %pad_maximum_fusion.8.a_ref), channel_id=1, source_target_pairs={{0,192},{64,0},{128,64},{192,128},{1,193},{65,1},{129,65},{193,129... | collective-permute-start | bytes 393224 | tf_op jit(solution)/shard_map/ppermute | solution.py:26
  58.0 7.9 %collective-permute-start.12 = (bf16[512,128]{1,0:T(8,128)(2,1)S(1)}, bf16[512,128]{1,0:T(8,128)(2,1)S(1)}, u32[]{:S(2)}, u32[]{:S(2)}) collective-permute-start(bf16[512,128]{1,0:T(8,128)(2,1)S(1)} %pad_maximum_fusion.8.a_ref), channel_id=1, source_target_pairs={{0,128},{64,192},{128,0},{192,64},{1,129},{65,193},{129,1},{193,65... | collective-permute-start | bytes 393224 | tf_op jit(solution)/shard_map/ppermute | solution.py:26
  61.3 6.5 %collective-permute-start.13 = (bf16[512,128]{1,0:T(8,128)(2,1)S(1)}, bf16[512,128]{1,0:T(8,128)(2,1)S(1)}, u32[]{:S(2)}, u32[]{:S(2)}) collective-permute-start(bf16[512,128]{1,0:T(8,128)(2,1)S(1)} %pad_maximum_fusion.8.a_ref), channel_id=1, source_target_pairs={{0,64},{64,128},{128,192},{192,0},{1,65},{65,129},{129,193},{193,1... | collective-permute-start | bytes 393224 | tf_op jit(solution)/shard_map/ppermute | solution.py:26
  71.0 20.2 %all-to-all-start.1 = ((bf16[32,48,128]{2,1,0:T(8,128)(2,1)}), bf16[32,48,128]{2,1,0:T(8,128)(2,1)S(1)}, u32[]{:S(2)}, u32[]{:S(2)}) async-start(bf16[32,48,128]{2,1,0:T(8,128)(2,1)} %get-tuple-element.20), calls=%async_computation.1 | async-start | bytes 786432 | tf_op jit(solution)/shard_map/all_to_all | solution.py:38
  80.8 19.5 %collective-permute-start.18 = (bf16[256,128]{1,0:T(8,128)(2,1)S(1)}, bf16[256,128]{1,0:T(8,128)(2,1)S(1)}, u32[]{:S(2)}, u32[]{:S(2)}) collective-permute-start(bf16[256,128]{1,0:T(8,128)(2,1)S(1)} %get-tuple-element.46), channel_id=1, source_target_pairs={{64,0},{128,64},{192,128},{65,1},{129,65},{193,129},{66,2},{130,66... | collective-permute-start | bytes 196616 | tf_op jit(solution)/shard_map/ppermute | solution.py:30
  83.2 18.7 %collective-permute-start.19 = (bf16[256,128]{1,0:T(8,128)(2,1)S(1)}, bf16[256,128]{1,0:T(8,128)(2,1)S(1)}, u32[]{:S(2)}, u32[]{:S(2)}) collective-permute-start(bf16[256,128]{1,0:T(8,128)(2,1)S(1)} %get-tuple-element.46), channel_id=1, source_target_pairs={{128,0},{192,64},{129,1},{193,65},{130,2},{194,66},{131,3},{195,67... | collective-permute-start | bytes 196616 | tf_op jit(solution)/shard_map/ppermute | solution.py:30
  86.7 15.7 %collective-permute-start.20 = (bf16[256,128]{1,0:T(8,128)(2,1)S(1)}, bf16[256,128]{1,0:T(8,128)(2,1)S(1)}, u32[]{:S(2)}, u32[]{:S(2)}) collective-permute-start(bf16[256,128]{1,0:T(8,128)(2,1)S(1)} %get-tuple-element.46), channel_id=1, source_target_pairs={{192,0},{193,1},{194,2},{195,3},{196,4},{197,5},{198,6},{199,7},{2... | collective-permute-start | bytes 196616 | tf_op jit(solution)/shard_map/ppermute | solution.py:30
  91.2 12.9 %collective-permute-start.14 = (bf16[768,128]{1,0:T(8,128)(2,1)S(1)}, bf16[768,128]{1,0:T(8,128)(2,1)S(1)}, u32[]{:S(2)}, u32[]{:S(2)}) collective-permute-start(bf16[768,128]{1,0:T(8,128)(2,1)S(1)} %bitcast.60), channel_id=1, source_target_pairs={{64,0},{128,64},{192,128},{65,1},{129,65},{193,129},{66,2},{130,66... | collective-permute-start | bytes 589832 | tf_op jit(solution)/shard_map/ppermute | solution.py:30
  93.2 11.0 %collective-permute-start.15 = (bf16[512,128]{1,0:T(8,128)(2,1)S(1)}, bf16[512,128]{1,0:T(8,128)(2,1)S(1)}, u32[]{:S(2)}, u32[]{:S(2)}) collective-permute-start(bf16[512,128]{1,0:T(8,128)(2,1)S(1)} %bitcast.61), channel_id=1, source_target_pairs={{128,0},{192,64},{129,1},{193,65},{130,2},{194,66},{131,3},{195,67... | collective-permute-start | bytes 393224 | tf_op jit(solution)/shard_map/ppermute | solution.py:30
  100.3 49.4 %collective-permute-start = (bf16[256,2048]{1,0:T(8,128)(2,1)}, bf16[256,2048]{1,0:T(8,128)(2,1)}, u32[]{:S(2)}, u32[]{:S(2)}) collective-permute-start(bf16[256,2048]{1,0:T(8,128)(2,1)} %get-tuple-element.35), channel_id=1, source_target_pairs={{0,24},{8,0},{16,8},{24,16},{1,25},{9,1},{17,9},{25,17},{2,26},{10... | collective-permute-start | bytes 3145736 | tf_op jit(solution)/shard_map/ppermute | solution.py:26
  102.0 47.7 %collective-permute-start.3 = (bf16[256,2048]{1,0:T(8,128)(2,1)}, bf16[256,2048]{1,0:T(8,128)(2,1)}, u32[]{:S(2)}, u32[]{:S(2)}) collective-permute-start(bf16[256,2048]{1,0:T(8,128)(2,1)} %get-tuple-element.34), channel_id=1, source_target_pairs={{0,8},{8,16},{16,24},{24,0},{1,9},{9,17},{17,25},{25,1},{2,10},{10... | collective-permute-start | bytes 3145736 | tf_op jit(solution)/shard_map/ppermute | solution.py:26
  104.1 6.6 %collective-permute-start.21 = (bf16[4,256,128]{2,1,0:T(8,128)(2,1)S(1)}, bf16[4,256,128]{2,1,0:T(8,128)(2,1)S(1)}, u32[]{:S(2)}, u32[]{:S(2)}) collective-permute-start(bf16[4,256,128]{2,1,0:T(8,128)(2,1)S(1)} %pad_maximum_fusion.7.slope_own_ref), channel_id=1, source_target_pairs={{0,32},{32,0},{1,33},{33,1},{2,34},{34,2},{3,35},{35,3},{4,36},{36... | collective-permute-start | bytes 786440 | tf_op jit(solution)/shard_map/ppermute | solution.py:34
  105.8 6.4 %collective-permute-start.17 = (bf16[2560,128]{1,0:T(8,128)(2,1)S(1)}, bf16[2560,128]{1,0:T(8,128)(2,1)S(1)}, u32[]{:S(2)}, u32[]{:S(2)}) collective-permute-start(bf16[2560,128]{1,0:T(8,128)(2,1)S(1)} %pad_maximum_fusion.own_ref), channel_id=1, source_target_pairs={{0,32},{32,0},{1,33},{33,1},{2,34},{34,2},{3,35},{35,3},{4,36},{36... | collective-permute-start | bytes 1966088 | tf_op jit(solution)/shard_map/ppermute | solution.py:34
  108.7 31.2 %collective-permute-start.1 = (bf16[256,1024]{1,0:T(8,128)(2,1)}, bf16[256,1024]{1,0:T(8,128)(2,1)S(1)}, u32[]{:S(2)}, u32[]{:S(2)}) collective-permute-start(bf16[256,1024]{1,0:T(8,128)(2,1)} %get-tuple-element.37), channel_id=1, source_target_pairs={{0,16},{8,24},{16,0},{24,8},{1,17},{9,25},{17,1},{25,9},{2,18},{10... | collective-permute-start | bytes 1572872 | tf_op jit(solution)/shard_map/ppermute | solution.py:26
  110.6 39.1 %collective-permute-start.2 = (bf16[256,1024]{1,0:T(8,128)(2,1)}, bf16[256,1024]{1,0:T(8,128)(2,1)}, u32[]{:S(2)}, u32[]{:S(2)}) collective-permute-start(bf16[256,1024]{1,0:T(8,128)(2,1)} %get-tuple-element.36), channel_id=1, source_target_pairs={{0,16},{8,24},{16,0},{24,8},{1,17},{9,25},{17,1},{25,9},{2,18},{10... | collective-permute-start | bytes 1572872 | tf_op jit(solution)/shard_map/ppermute | solution.py:26
  120.5 29.6 %collective-permute-start.22 = (bf16[512,128]{1,0:T(8,128)(2,1)}, bf16[512,128]{1,0:T(8,128)(2,1)S(1)}, u32[]{:S(2)}, u32[]{:S(2)}) collective-permute-start(bf16[512,128]{1,0:T(8,128)(2,1)} %get-tuple-element.24), channel_id=1, source_target_pairs={{0,24},{8,0},{16,8},{24,16},{1,25},{9,1},{17,9},{25,17},{2,26},{10... | collective-permute-start | bytes 393224 | tf_op jit(solution)/shard_map/ppermute | solution.py:26
  139.9 11.1 %collective-permute-start.23 = (bf16[512,128]{1,0:T(8,128)(2,1)}, bf16[512,128]{1,0:T(8,128)(2,1)S(1)}, u32[]{:S(2)}, u32[]{:S(2)}) collective-permute-start(bf16[512,128]{1,0:T(8,128)(2,1)} %get-tuple-element.25), channel_id=1, source_target_pairs={{0,16},{8,24},{16,0},{24,8},{1,17},{9,25},{17,1},{25,9},{2,18},{10... | collective-permute-start | bytes 393224 | tf_op jit(solution)/shard_map/ppermute | solution.py:26
  149.7 6.4 %collective-permute-start.24 = (bf16[512,128]{1,0:T(8,128)(2,1)}, bf16[512,128]{1,0:T(8,128)(2,1)S(1)}, u32[]{:S(2)}, u32[]{:S(2)}) collective-permute-start(bf16[512,128]{1,0:T(8,128)(2,1)} %get-tuple-element.26), channel_id=1, source_target_pairs={{0,8},{8,16},{16,24},{24,0},{1,9},{9,17},{17,25},{25,1},{2,10},{10... | collective-permute-start | bytes 393224 | tf_op jit(solution)/shard_map/ppermute | solution.py:26
  182.9 14.7 %all-to-all-start.3 = ((bf16[32,32,128]{2,1,0:T(8,128)(2,1)}), bf16[32,32,128]{2,1,0:T(8,128)(2,1)S(1)}, u32[]{:S(2)}, u32[]{:S(2)}) async-start(bf16[32,32,128]{2,1,0:T(8,128)(2,1)} %broadcast_in_dim.18), calls=%async_computation.3 | async-start | bytes 524288 | tf_op jit(solution)/shard_map/all_to_all | solution.py:38
  (28 other events, 215.8 us)

commit v4 on v3

--- a/solution.py
+++ b/solution.py
@@ -38,10 +38,6 @@
     return lax.all_to_all(blocks, ("y", "z"), 0, 0, tiled=True)
 
 
-def at(value, index):
-    return lax.dynamic_index_in_dim(value, index, 0, keepdims=False)
-
-
 def rows_at(value, start, size):
     return lax.dynamic_slice_in_dim(value, start, size, 0)
 
@@ -64,73 +60,42 @@
 
 
 def pack_kernel(
-    where_ref, piece_ref, heads_ref, up_ref, own_rep_ref, own_ref, partner_ref,
-    got1_ref, got2_ref, got3_ref, sent_ref, factor_ref, rep_ref,
+    where_ref, heads_ref, up_ref, own_ref, partner_ref, got1_ref, got2_ref, got3_ref,
+    sent_ref, factor_ref,
 ):
     my_x = where_ref[0]
     my_c = where_ref[1]
     my_stage = my_x * NC + my_c
     up_rows = up_ref[...]
-    piece = piece_ref[...]
-    for d in range(DP):
-        sent_ref[d, 0:32, :] = piece
     gots = (None, got1_ref, got2_ref, got3_ref)
     for k in range(NX):
         for r in range(NC):
             stage = ((my_x + k) % NX) * NC + (my_c if r == 0 else 1 - my_c)
             slot = SECTIONS - 1 - stage
             if k == 0:
-                rep_rows = own_rep_ref[256 * r : 256 * r + 256, :]
                 factor = heads_ref[...] if r == 0 else partner_ref[...]
             else:
-                rep_rows = gots[k][256 * r : 256 * r + 256, :]
-                factor = gots[k][512 + 256 * r : 768 + 256 * r, :]
+                factor = gots[k][256 * r : 256 * r + 256, :]
             if k or r:
                 factor = jnp.where(stage > my_stage, factor, jnp.zeros_like(factor))
-            rep_ref[stage] = rep_rows
             factor_ref[slot] = factor
             product = across(factor, up_rows).astype(BF16)
             for i in range(4):
-                sent_ref[4 * slot + i, 32:64, :] = product[32 * i : 32 * i + 32]
-
-
-def heads_kernel(where_ref, got_ref, rep_ref, target_ref, part_ref, cross_ref, head_ref):
-    my_stage = where_ref[0] * NC + where_ref[1]
-    for z in range(NZ):
-        for y in range(NY):
-            head_ref[128 * z + 32 * y : 128 * z + 32 * y + 32, :] = got_ref[NZ * y + z, 0:32, :]
-    total = None
-    square = None
-    for z in range(NZ):
-        head = head_ref[128 * z : 128 * z + 128, :]
-        rep = jnp.concatenate([rep_ref[m, 32 * z : 32 * z + 32, :] for m in range(SECTIONS)], axis=0)
-        term = jnp.dot(rep, head, preferred_element_type=F32)
-        other = across(head, head)
-        total = term if total is None else total + term
-        square = other if square is None else square + other
-    target = target_ref[...].astype(F32)
-    for m in range(SECTIONS):
-        rows = total[32 * m : 32 * m + 32]
-        part_ref[32 * m : 32 * m + 32, :] = rows - jnp.where(m == my_stage, target, 0.0)
-    part_ref[256:384, :] = square
-    cross_ref[...] = jnp.sum(got_ref[:, 32:64, :].astype(F32), axis=0).astype(BF16)
-
-
-def gram_kernel(where_ref, a_ref, b_ref, c_ref, d_ref, mask_ref, cross_ref, sent_ref, residual_ref):
-    def value(ref, lo, size):
-        return ref[lo : lo + size, :].astype(F32)
-
-    def summed(lo, size):
-        pair = value(a_ref, lo, size) + value(c_ref, lo, size)
-        return pair + (value(b_ref, lo, size) + value(d_ref, lo, size))
-
-    def squares(ref):
-        return value(ref, 256, 128) + value(ref, 384, 128)
-
-    residual = summed(0, 256).astype(BF16)
-    residual_ref[...] = residual
-    square = (squares(a_ref) + squares(c_ref)) + (squares(b_ref) + squares(d_ref))
-    product = square * across(residual, residual)
+                sent_ref[4 * slot + i] = product[32 * i : 32 * i + 32]
+
+
+def assemble_kernel(where_ref, own_ref, other_ref, out_ref):
+    my_x = where_ref[0]
+    my_c = where_ref[1]
+    for k in range(NX):
+        base = ((my_x + k) % NX) * NC
+        out_ref[:, base + my_c] = own_ref[k]
+        out_ref[:, base + 1 - my_c] = other_ref[k]
+
+
+def gram_kernel(where_ref, residual_ref, square_ref, mask_ref, cross_ref, sent_ref):
+    residual = residual_ref[...]
+    product = square_ref[...] * across(residual, residual)
     mask = mask_ref[...]
     high = lax.Precision.HIGHEST
     half = jnp.dot(mask[0:8], product, precision=high, preferred_element_type=F32)
@@ -139,28 +104,42 @@
     )
     top = part.astype(BF16)
     tile = jnp.concatenate([part, part - top.astype(F32)], axis=0).astype(BF16)
-    cross = cross_ref[...]
+    cross = jnp.sum(cross_ref[...].astype(F32), axis=0).astype(BF16)
     for d in range(DP):
         sent_ref[d, 0:32, :] = cross
         sent_ref[d, 32:48, :] = tile
 
 
+def merge_kernel(where_ref, residual_ref, got_ref, out_ref):
+    out_ref[0:32, :] = residual_ref[...]
+    tile = jnp.sum(got_ref[:, 32:48, :].astype(F32), axis=0)
+    part = tile[0:8] + tile[8:16]
+    top = part.astype(BF16).astype(F32)
+    out_ref[32:48, :] = jnp.concatenate([part, part - top], axis=0).astype(BF16)
+    for d in range(DP):
+        out_ref[48 + 32 * d : 80 + 32 * d, :] = got_ref[d, 0:32, :]
+
+
+SMALL = 48
 LATER_ROWS = (1024, 768, 512, 256)
-LATER_FROM = (0, 1024, 1792, 2304)
-ALL_ROWS = 2560
+LATER_FROM = (0, 1072, 1888, 2448)
+ALL_ROWS = 2752
 
 
 def chain_kernel(
-    where_ref, got_ref, mask_ref, residual_ref, active_ref, own_ref, other_ref,
-    slope_own_ref, slope_other_ref,
+    where_ref, mask_ref, active_ref, own_ref, other_ref, slope_own_ref, slope_other_ref,
     keep_ref, send1_ref, send2_ref, send3_ref, inner_ref, mix_ref, middle_ref,
 ):
     my_x = where_ref[0]
     my_c = where_ref[1]
     my_y = where_ref[2]
     my_stage = my_x * NC + my_c
-    tiles = jnp.sum(got_ref[:, 32:48, :].astype(F32), axis=0)
-    gram = tiles[0:8] + tiles[8:16]
+    tiles = []
+    for k in range(NX):
+        lo = LATER_FROM[k] + 32
+        tiles.append(own_ref[lo : lo + 16, :].astype(F32) + other_ref[lo : lo + 16, :].astype(F32))
+    tile = (tiles[0] + tiles[2]) + (tiles[1] + tiles[3])
+    gram = tile[0:8] + tile[8:16]
     rows = lax.broadcasted_iota(jnp.int32, gram.shape, 0)
     lanes = lax.broadcasted_iota(jnp.int32, gram.shape, 1)
     diagonal = jnp.where(rows == lanes, gram, 0.0)
@@ -185,22 +164,28 @@
     mix_ref[...] = along / total_along
     column_weight = jnp.sum((down / total_down) * mask_ref[0:8], axis=0, keepdims=True)
 
-    def cross(stage, source):
+    def first_row(stage):
         away = (stage // NC - my_x) % NX
         start = jnp.where(away == 0, LATER_FROM[0], LATER_FROM[1])
         start = jnp.where(away == 2, LATER_FROM[2], start)
-        start = jnp.where(away == 3, LATER_FROM[3], start)
-        start = jnp.minimum(start + 128 * (SECTIONS - 1 - source), ALL_ROWS - 128)
-        start = pl.multiple_of(start, 128)
-        own = own_ref[pl.ds(start, 128), :]
-        return jnp.where(my_c == stage % NC, own, other_ref[pl.ds(start, 128), :])
+        return jnp.where(away == 3, LATER_FROM[3], start)
+
+    def taken(stage, start, size):
+        start = pl.multiple_of(start, 16)
+        own = own_ref[pl.ds(start, size), :]
+        return jnp.where(my_c == stage % NC, own, other_ref[pl.ds(start, size), :])
+
+    def cross(stage, source):
+        start = first_row(stage) + SMALL + 128 * (SECTIONS - 1 - source)
+        return taken(stage, jnp.minimum(start, ALL_ROWS - 128), 128)
 
     def slope_of(stage):
         away = (stage // NC - my_x) % NX
         return jnp.where(my_c == stage % NC, slope_own_ref[away], slope_other_ref[away])
 
     active = active_ref[...]
-    weighted = (residual_ref[...].astype(F32) * column_weight).astype(BF16)
+    residual = jnp.concatenate([taken(m, first_row(m), 32) for m in range(SECTIONS)], axis=0)
+    weighted = (residual.astype(F32) * column_weight).astype(BF16)
     first = across(weighted, active)
     inners = {}
     for stage in range(SECTIONS - 1, -1, -1):
@@ -285,24 +270,19 @@
     up_map = adapter_up[0]
     heads = head_weights
     share, rank = heads.shape
-    tok = representation.shape[1]
     column_task = jnp.repeat(head_task[:, 0], HEAD_OUT)
     mask = (column_task[None, :] == jnp.arange(rank, dtype=jnp.int32)[:, None]).astype(F32)
 
-    piece = rows_at(heads, my_c * 128 + my_x * 32, 32)
-    turn = [(a * NY + b, b * NY + a) for a in range(NX) for b in range(NY)]
-    piece = lax.ppermute(piece, ("x", "y"), turn)
-
-    blocks = representation[0].reshape(tok, NX, NZ, NC, 128).transpose(3, 1, 2, 0, 4)
-    blocks = blocks.reshape(NC, NX, NZ * tok, 128)
     down_rows = rows_at(down_map, my_dp * share, share)
-    swapped = swap_c(at(blocks, 1 - my_c))
     partner = swap_c(down_rows)
-    pair = jnp.concatenate([at(blocks, my_c), swapped], axis=1)
-    gots = []
+    both = jnp.concatenate([down_rows, partner], axis=0)
+    gots = [from_later(both, k) for k in range(1, NX)]
+
+    piece = rows_at(heads, my_x * 64 + my_c * 32, 32)
+    pieces = exchange_dp(jnp.broadcast_to(piece[None], (DP, 32, rank)))
+    near = [pieces]
     for k in range(1, NX):
-        sent = jnp.concatenate([at(pair, (my_x - k) % NX), down_rows, partner], axis=0)
-        gots.append(shift(sent, "x", -k))
+        near.append(shift(pieces, "x", -k))
 
     wide = dim_model // NY
 
@@ -313,41 +293,37 @@
     x3 = shift(cut(my_y, 3, 0, wide), "y", -3)
 
     up_rows = rows_at(up_map, my_dp * share, share)
-    sent, factors, rep = local_call(
+    sent, factors = local_call(
         pack_kernel,
-        [((DP, 64, rank), BF16), ((SECTIONS, share, rank), BF16), ((SECTIONS, NZ * tok, rank), BF16)],
-        where, piece, heads, up_rows, at(pair, my_x), down_rows, partner, *gots,
-    )
-
-    preact = jnp.dot(saved, down_map, preferred_element_type=F32)
+        [((DP, 32, rank), BF16), ((SECTIONS, share, rank), BF16)],
+        where, heads, up_rows, down_rows, partner, *gots,
+    )
+    down_late, sent = lax.optimization_barrier((down_map, sent))
+    got_cross = exchange_dp(sent)
+
+    preact = jnp.dot(saved, down_late, preferred_element_type=F32)
     logistic = jax.nn.sigmoid(preact)
     active = (preact * logistic).astype(BF16)
     slope = (logistic * (1.0 + preact * (1.0 - logistic))).astype(BF16)
     slope_own = jnp.stack([slope] + [from_later(slope, k) for k in range(1, NX)])
     slope_other = swap_c(slope_own)
 
+    near, got_cross = lax.optimization_barrier((jnp.stack(near), got_cross))
+    far = swap_c(near)
+    (weights,) = local_call(assemble_kernel, [((DP, SECTIONS, 32, rank), BF16)], where, near, far)
+    weights = weights.reshape(dim_model, rank)
+    predicted = jnp.dot(representation[0], weights, preferred_element_type=F32)
+    residual = (predicted - head_targets[0].astype(F32)).astype(BF16)
+    x2a = shift(cut(my_y, 2, 0, wide // 2), "y", -2)
+    (sent,) = local_call(
+        gram_kernel, [((DP, SMALL, rank), BF16)],
+        where, residual, across(weights, weights), mask, got_cross,
+    )
     got = exchange_dp(sent)
-    part, cross_rows, _ = local_call(
-        heads_kernel,
-        [((384, rank), F32), ((32, rank), BF16), ((1024, rank), BF16)],
-        where, got, rep, head_targets[0],
-    )
-    part = part + swap_c(part)
-    top = part.astype(BF16)
-    low = (part[256:] - top[256:].astype(F32)).astype(BF16)
-    halves = jnp.concatenate([top, low], axis=0)
-    others = [shift(halves, "x", -k) for k in range(1, NX)]
-    x2a = shift(cut(my_y, 2, 0, wide // 2), "y", -2)
-    sent, residual = local_call(
-        gram_kernel,
-        [((DP, 48, rank), BF16), ((256, rank), BF16)],
-        where, halves, *others, mask, cross_rows,
-    )
-    got = exchange_dp(sent)
-    cross = got[:, :32].reshape(-1, rank)
+    (cross,) = local_call(merge_kernel, [((SMALL + 1024, rank), BF16)], where, residual, got)
     kept = [cross]
     for k in range(1, NX):
-        kept.append(from_later(cross[: LATER_ROWS[k]], k))
+        kept.append(shift(cross[: SMALL + LATER_ROWS[k]], "x", -k))
     x2b = shift(cut(my_y, 2, wide // 2, wide // 2), "y", -2)
     cross_own = jnp.concatenate(kept, axis=0)
     cross_other = swap_c(cross_own)
@@ -355,7 +331,7 @@
         chain_kernel,
         [((256, rank), BF16)] + [((512, rank), BF16)] * 3
         + [((256, rank), BF16), ((8, rank), F32), ((1024, rank), BF16)],
-        where, got, mask, residual, active, cross_own, cross_other, slope_own, slope_other,
+        where, mask, active, cross_own, cross_other, slope_own, slope_other,
     )
     got1 = shift(send1, "y", -1)
     got2 = shift(send2, "y", -2)

time: 201 us -> 205 us (1.020)
  blocking collectives: 46 us -> 21.5 us
  starting transfers between devices: 48.7 us -> 68.2 us
  waiting for transfers between devices: 56.9 us -> 62.5 us
  matrix products: 5.01 us -> 9.81 us
  other arithmetic: 4.91 us -> 2.72 us
    all_to_all x1 -> x0, blocking collectives: 25.5 us -> none  [exchange_dp(): return lax.all_to_all(blocks, ('y', 'z'), 0, 0, tiled=True)]
    all_to_all x2 -> x4, starting transfers between devices: 9.54 us -> 34.8 us  [exchange_dp(): return lax.all_to_all(blocks, ('y', 'z'), 0, 0, tiled=True)]
    ppermute x13, waiting for transfers between devices: 35.4 us -> 45 us  [shift(): lax.ppermute(value, axis, [(src, (src + steps) % count) for src in range(...]
    ppermute x1 -> x0, waiting for transfers between devices: 6.41 us -> none  [stages(): piece = lax.ppermute(piece, ('x', 'y'), turn)]
    dot_general x1 -> x3, matrix products: 4.07 us -> 8.87 us  [the longest x1 4.07 us: stages(): preact = jnp.dot(saved, down_late, preferred_element_type=F32)]
    ppermute x1 -> x0, starting transfers between devices: 4.63 us -> none  [stages(): piece = lax.ppermute(piece, ('x', 'y'), turn)]
    ppermute x6, starting transfers between devices: 13 us -> 10.1 us  [from_later(): lax.ppermute(value, 'x', [(src, src - steps) for src in range(steps, NX)])]
    ppermute x13, starting transfers between devices: 20.2 us -> 22.6 us  [shift(): lax.ppermute(value, axis, [(src, (src + steps) % count) for src in range(...]
  transfers between devices with their start and end apart: 27 -> 27, of which waited for: 12 -> 14; matrix products, arithmetic and copies ran while one was open for 9% -> 9% of each run, Pallas kernels for 4% -> 6%
where the time goes in v4:
time: 205 us; the launch traced here: 203 us
  starting transfers between devices  68.2 us (33%)
  waiting for transfers between devices  62.5 us (30%)
  Pallas kernels  21.5 us (10%)
  blocking collectives  21.5 us (10%)
  local copies, waits for them, and re-layouts  16 us (8%)
  matrix products  9.81 us (5%)
  other arithmetic  2.72 us (1%)
    ppermute x13, waiting for transfers between devices, shift(): lax.ppermute(value, axis, [(src, (src + steps) % count) for src in range(...  45 us
    all_to_all x4, starting transfers between devices, exchange_dp(): return lax.all_to_all(blocks, ('y', 'z'), 0, 0, tiled=True)  34.8 us
    ppermute x13, starting transfers between devices, shift(): lax.ppermute(value, axis, [(src, (src + steps) % count) for src in range(...  22.6 us
    all_to_all x1, blocking collectives, stages(): got = lax.all_to_all(part_down, 'z', 0, 0, tiled=True)  21.5 us
    pallas_call x5, Pallas kernels, local_call(): pl.pallas_call(kernel, out_shape=tuple((jax.ShapeDtypeStruct(shape, dtype...  16.8 us
    all_to_all x4, waiting for transfers between devices, exchange_dp(): return lax.all_to_all(blocks, ('y', 'z'), 0, 0, tiled=True)  13.4 us
    ppermute x6, starting transfers between devices, from_later(): lax.ppermute(value, 'x', [(src, src - steps) for src in range(steps, NX)])  10.1 us
    dynamic_slice x2, local copies, waits for them, and re-layouts, cut(): lax.dynamic_slice_in_dim(saved, (index - k) % NY * wide + lo, size, 1)  5.45 us
  transfers between devices with their start and end apart: 27, of which 14 were waited for; matrix products, arithmetic and copies ran while one was open for 9% of the time, Pallas kernels for 6%

profile of v4, /device:TPU:4, one launch (start us, length us, event | category | flops | bytes accessed | tf_op | source)
XLA Modules:
  0.0 203.4 jit_solution(8075238104991601480)
XLA Ops:
  2.2 11.6 %all-to-all-start = ((bf16[32,32,128]{2,1,0:T(8,128)(2,1)}), bf16[32,32,128]{2,1,0:T(8,128)(2,1)S(1)}, u32[]{:S(2)}, u32[]{:S(2)}) async-start(bf16[32,32,128]{2,1,0:T(8,128)(2,1)} %broadcast_in_dim.11), calls=%async_computation | async-start | bytes 524288 | tf_op jit(solution)/shard_map/all_to_all | solution.py:38
  26.4 9.8 %all-to-all-start.1 = ((bf16[32,32,128]{2,1,0:T(8,128)(2,1)}), bf16[32,32,128]{2,1,0:T(8,128)(2,1)S(1)}, u32[]{:S(2)}, u32[]{:S(2)}) async-start(bf16[32,32,128]{2,1,0:T(8,128)(2,1)} %get-tuple-element.17), calls=%async_computation.1 | async-start | bytes 524288 | tf_op jit(solution)/shard_map/all_to_all | solution.py:38
  36.2 4.2 %collective-permute-start.8 = (bf16[32,32,128]{2,1,0:T(8,128)(2,1)S(1)}, bf16[32,32,128]{2,1,0:T(8,128)(2,1)S(1)}, u32[]{:S(2)}, u32[]{:S(2)}) collective-permute-start(bf16[32,32,128]{2,1,0:T(8,128)(2,1)S(1)} %all-to-all-done), channel_id=1, source_target_pairs={{0,192},{64,0},{128,64},{192,128},{1,193},{65,1},{129,65},{193,129... | collective-permute-start | bytes 786440 | tf_op jit(solution)/shard_map/ppermute | solution.py:26
  41.8 2.5 %collective-permute-start.10 = (bf16[32,32,128]{2,1,0:T(8,128)(2,1)S(1)}, bf16[32,32,128]{2,1,0:T(8,128)(2,1)S(1)}, u32[]{:S(2)}, u32[]{:S(2)}) collective-permute-start(bf16[32,32,128]{2,1,0:T(8,128)(2,1)S(1)} %all-to-all-done), channel_id=1, source_target_pairs={{0,64},{64,128},{128,192},{192,0},{1,65},{65,129},{129,193},{193,1... | collective-permute-start | bytes 786440 | tf_op jit(solution)/shard_map/ppermute | solution.py:26
  44.4 6.3 %collective-permute-done.8 = bf16[32,32,128]{2,1,0:T(8,128)(2,1)S(1)} collective-permute-done((bf16[32,32,128]{2,1,0:T(8,128)(2,1)S(1)}, bf16[32,32,128]{2,1,0:T(8,128)(2,1)S(1)}, u32[]{:S(2)}, u32[]{:S(2)}) %collective-permute-start.8) | collective-permute-done | bytes 262176 | tf_op jit(solution)/shard_map/ppermute | solution.py:26
  51.2 3.0 %collective-permute-done.10 = bf16[32,32,128]{2,1,0:T(8,128)(2,1)S(1)} collective-permute-done((bf16[32,32,128]{2,1,0:T(8,128)(2,1)S(1)}, bf16[32,32,128]{2,1,0:T(8,128)(2,1)S(1)}, u32[]{:S(2)}, u32[]{:S(2)}) %collective-permute-start.10) | collective-permute-done | bytes 262176 | tf_op jit(solution)/shard_map/ppermute | solution.py:26
  58.1 3.1 %shard_map.95 = bf16[32,8,32,128]{3,2,1,0:T(8,128)(2,1)} custom-call(s32[3]{0:T(128)} %pad_add_fusion.where_ref, bf16[4,32,32,128]{3,2,1,0:T(8,128)(2,1)} %copy-done.2, bf16[4,32,32,128]{3,2,1,0:T(8,128)(2,1)} %collective-permute-done.11.other_ref), custom_call_target="tpu_custom_call" | custom-call | tf_op jit(solution)/shard_map/pallas_call | solution.py:54
  61.2 3.8 %convolution_bitcast_fusion.2.square_ref = f32[128,128]{1,0:T(8,128)} fusion(bf16[32,8,32,128]{3,2,1,0:T(8,128)(2,1)} %shard_map.95), kind=kOutput, calls=%fused_computation.3 | convolution fusion | flops 268435456 | bytes 2162688 | tf_op jit(solution)/shard_map/dot_general | solution.py:46
  66.0 2.5 %shard_map.96 = bf16[32,48,128]{2,1,0:T(8,128)(2,1)} custom-call(s32[3]{0:T(128)} %pad_add_fusion.where_ref, bf16[32,128]{1,0:T(8,128)(2,1)} %fusion.1.residual_ref, f32[128,128]{1,0:T(8,128)} %convolution_bitcast_fusion.2.square_ref, f32[128,128]{1,0:T(8,128)} %fusion.3.mask_ref, bf16[32,32,128]{2,1,0:T(8,128)(2,1)} %copy-done.7), custom_call_target="tpu_custom_call" | custom-call | tf_op jit(solution)/shard_map/pallas_call | solution.py:54
  68.5 9.5 %all-to-all-start.2 = ((bf16[32,48,128]{2,1,0:T(8,128)(2,1)}), bf16[32,48,128]{2,1,0:T(8,128)(2,1)S(1)}, u32[]{:S(2)}, u32[]{:S(2)}) async-start(bf16[32,48,128]{2,1,0:T(8,128)(2,1)} %shard_map.96), calls=%async_computation.2 | async-start | bytes 786432 | tf_op jit(solution)/shard_map/all_to_all | solution.py:38
  78.0 4.1 %multiply_convert_fusion = (bf16[256,128]{1,0:T(8,128)(2,1)S(1)}, bf16[256,128]{1,0:T(8,128)(2,1)}) fusion(bf16[256,8192]{1,0:T(8,128)(2,1)} %bitcast.57, bf16[8192,128]{1,0:T(8,128)(2,1)S(1)} %bitcast.56), kind=kOutput, calls=%fused_computation.13 | convolution fusion | flops 537198592 | bytes 6422528 | tf_op jit(solution)/shard_map/dot_general | solution.py:304
  82.1 2.7 %collective-permute-start.16 = (bf16[256,128]{1,0:T(8,128)(2,1)S(1)}, bf16[256,128]{1,0:T(8,128)(2,1)S(1)}, u32[]{:S(2)}, u32[]{:S(2)}) collective-permute-start(bf16[256,128]{1,0:T(8,128)(2,1)S(1)} %get-tuple-element.36), channel_id=1, source_target_pairs={{64,0},{128,64},{192,128},{65,1},{129,65},{193,129},{66,2},{130,66... | collective-permute-start | bytes 196616 | tf_op jit(solution)/shard_map/ppermute | solution.py:30
  87.8 4.6 %all-to-all-done.2.got_ref = bf16[32,48,128]{2,1,0:T(8,128)(2,1)S(1)} async-done(((bf16[32,48,128]{2,1,0:T(8,128)(2,1)}), bf16[32,48,128]{2,1,0:T(8,128)(2,1)S(1)}, u32[]{:S(2)}, u32[]{:S(2)}) %all-to-all-start.2) | async-done | bytes 393248 | tf_op jit(solution)/shard_map/all_to_all | solution.py:38
  99.8 3.1 %constant_dynamic-slice_fusion.1 = (bf16[256,2048]{1,0:T(8,128)(2,1)}, bf16[256,2048]{1,0:T(8,128)(2,1)}) fusion(bf16[256,8192]{1,0:T(8,128)(2,1)} %bitcast.58, s32[]{:T(128)S(6)} %select_n.42, s32[]{:T(128)S(6)} %select_n.37), kind=kLoop, calls=%fused_computation.24 | loop fusion | bytes 4194312 | tf_op jit(solution)/shard_map/dynamic_slice | solution.py:290
  106.7 2.8 %collective-permute-done.14 = bf16[304,128]{1,0:T(8,128)(2,1)S(1)} collective-permute-done((bf16[304,128]{1,0:T(8,128)(2,1)S(1)}, bf16[304,128]{1,0:T(8,128)(2,1)S(1)}, u32[]{:S(2)}, u32[]{:S(2)}) %collective-permute-start.14) | collective-permute-done | bytes 77856 | tf_op jit(solution)/shard_map/ppermute | solution.py:26
  116.0 7.3 %shard_map.98 = (bf16[256,128]{1,0:T(8,128)(2,1)}, bf16[512,128]{1,0:T(8,128)(2,1)}, bf16[512,128]{1,0:T(8,128)(2,1)}, bf16[512,128]{1,0:T(8,128)(2,1)}, bf16[25...) custom-call(s32[3]{0:T(128)} %pad_add_fusion.where_ref, f32[128,128]{1,0:T(8,128)} %fusion.3.mask_ref, ...), custom_call_target="tpu_custom_call" | custom-call | tf_op jit(solution)/shard_map/pallas_call | solution.py:54
  123.3 3.0 %collective-permute-start.20 = (bf16[512,128]{1,0:T(8,128)(2,1)}, bf16[512,128]{1,0:T(8,128)(2,1)S(1)}, u32[]{:S(2)}, u32[]{:S(2)}) collective-permute-start(bf16[512,128]{1,0:T(8,128)(2,1)} %get-tuple-element.22), channel_id=1, source_target_pairs={{0,24},{8,0},{16,8},{24,16},{1,25},{9,1},{17,9},{25,17},{2,26},{10... | collective-permute-start | bytes 393224 | tf_op jit(solution)/shard_map/ppermute | solution.py:26
  126.3 16.5 %collective-permute-done.1.x2a_ref = bf16[256,1024]{1,0:T(8,128)(2,1)} collective-permute-done((bf16[256,1024]{1,0:T(8,128)(2,1)}, bf16[256,1024]{1,0:T(8,128)(2,1)}, u32[]{:S(2)}, u32[]{:S(2)}) %collective-permute-start.1) | collective-permute-done | bytes 524320 | tf_op jit(solution)/shard_map/ppermute | solution.py:26
  144.1 9.5 %collective-permute-done.2.x2b_ref = bf16[256,1024]{1,0:T(8,128)(2,1)} collective-permute-done((bf16[256,1024]{1,0:T(8,128)(2,1)}, bf16[256,1024]{1,0:T(8,128)(2,1)}, u32[]{:S(2)}, u32[]{:S(2)}) %collective-permute-start.2) | collective-permute-done | bytes 524320 | tf_op jit(solution)/shard_map/ppermute | solution.py:26
  155.0 5.1 %collective-permute-done.22.got3_ref = bf16[512,128]{1,0:T(8,128)(2,1)S(1)} collective-permute-done((bf16[512,128]{1,0:T(8,128)(2,1)}, bf16[512,128]{1,0:T(8,128)(2,1)S(1)}, u32[]{:S(2)}, u32[]{:S(2)}) %collective-permute-start.22) | collective-permute-done | bytes 131104 | tf_op jit(solution)/shard_map/ppermute | solution.py:26
  160.7 4.8 %down_product.1 = bf16[8,288,128]{2,1,0:T(8,128)(2,1)} custom-call(s32[1]{0:T(128)} %bitcast.y_ref, bf16[256,8192]{1,0:T(8,128)(2,1)} %bitcast.60, bf16[256,2048]{1,0:T(8,128)(2,1)} %collective-permute-done.x1_ref, bf16[256,1024]{1,0:T(8,128)(2,1)} %collective-permute-done.1.x2a_ref, bf16[256,1024]{1,0:T(8,128)(2,1)} %collective-permute-done.2.x2b_ref, ...), custom_call_target="tpu_custom_call" | custom-call | tf_op jit(solution)/shard_map/down_product/pallas_call | solution.py:239
  165.4 21.5 %all_to_all.25 = bf16[8,288,128]{2,1,0:T(8,128)(2,1)S(1)} all-to-all(bf16[8,288,128]{2,1,0:T(8,128)(2,1)} %down_product.1), channel_id=1, replica_groups=mesh['x'=4,'c'=2,'y'=4,'z'=8] {'z'}, dimensions={0} | all-to-all | bytes 1179648 | tf_op jit(solution)/shard_map/all_to_all | solution.py:340
  187.8 3.9 %all-to-all-start.4 = ((bf16[32,32,128]{2,1,0:T(8,128)(2,1)}), bf16[32,32,128]{2,1,0:T(8,128)(2,1)S(1)}, u32[]{:S(2)}, u32[]{:S(2)}) async-start(bf16[32,32,128]{2,1,0:T(8,128)(2,1)} %broadcast_in_dim.25), calls=%async_computation.4 | async-start | bytes 524288 | tf_op jit(solution)/shard_map/all_to_all | solution.py:38
  193.6 8.8 %all-to-all-done.4 = bf16[32,32,128]{2,1,0:T(8,128)(2,1)S(1)} async-done(((bf16[32,32,128]{2,1,0:T(8,128)(2,1)}), bf16[32,32,128]{2,1,0:T(8,128)(2,1)S(1)}, u32[]{:S(2)}, u32[]{:S(2)}) %all-to-all-start.4) | async-done | bytes 262176 | tf_op jit(solution)/shard_map/all_to_all | solution.py:38
  (109 shorter events, 48.5 us)
Async XLA Ops:
  2.2 24.2 %all-to-all-start = ((bf16[32,32,128]{2,1,0:T(8,128)(2,1)}), bf16[32,32,128]{2,1,0:T(8,128)(2,1)S(1)}, u32[]{:S(2)}, u32[]{:S(2)}) async-start(bf16[32,32,128]{2,1,0:T(8,128)(2,1)} %broadcast_in_dim.11), calls=%async_computation | async-start | bytes 524288 | tf_op jit(solution)/shard_map/all_to_all | solution.py:38
  15.3 7.5 %collective-permute-start.5 = (bf16[512,128]{1,0:T(8,128)(2,1)S(1)}, bf16[512,128]{1,0:T(8,128)(2,1)S(1)}, u32[]{:S(2)}, u32[]{:S(2)}) collective-permute-start(bf16[512,128]{1,0:T(8,128)(2,1)S(1)} %pad_maximum_fusion.3), channel_id=1, source_target_pairs={{64,0},{128,64},{192,128},{65,1},{129,65},{193,129},{66,2},{130,66... | collective-permute-start | bytes 393224 | tf_op jit(solution)/shard_map/ppermute | solution.py:30
  17.7 5.1 %collective-permute-start.6 = (bf16[512,128]{1,0:T(8,128)(2,1)S(1)}, bf16[512,128]{1,0:T(8,128)(2,1)S(1)}, u32[]{:S(2)}, u32[]{:S(2)}) collective-permute-start(bf16[512,128]{1,0:T(8,128)(2,1)S(1)} %pad_maximum_fusion.3), channel_id=1, source_target_pairs={{128,0},{192,64},{129,1},{193,65},{130,2},{194,66},{131,3},{195,67... | collective-permute-start | bytes 393224 | tf_op jit(solution)/shard_map/ppermute | solution.py:30
  26.4 28.8 %all-to-all-start.1 = ((bf16[32,32,128]{2,1,0:T(8,128)(2,1)}), bf16[32,32,128]{2,1,0:T(8,128)(2,1)S(1)}, u32[]{:S(2)}, u32[]{:S(2)}) async-start(bf16[32,32,128]{2,1,0:T(8,128)(2,1)} %get-tuple-element.17), calls=%async_computation.1 | async-start | bytes 524288 | tf_op jit(solution)/shard_map/all_to_all | solution.py:38
  36.2 14.4 %collective-permute-start.8 = (bf16[32,32,128]{2,1,0:T(8,128)(2,1)S(1)}, bf16[32,32,128]{2,1,0:T(8,128)(2,1)S(1)}, u32[]{:S(2)}, u32[]{:S(2)}) collective-permute-start(bf16[32,32,128]{2,1,0:T(8,128)(2,1)S(1)} %all-to-all-done), channel_id=1, source_target_pairs={{0,192},{64,0},{128,64},{192,128},{1,193},{65,1},{129,65},{193,129... | collective-permute-start | bytes 786440 | tf_op jit(solution)/shard_map/ppermute | solution.py:26
  40.5 10.7 %collective-permute-start.9 = (bf16[32,32,128]{2,1,0:T(8,128)(2,1)S(1)}, bf16[32,32,128]{2,1,0:T(8,128)(2,1)S(1)}, u32[]{:S(2)}, u32[]{:S(2)}) collective-permute-start(bf16[32,32,128]{2,1,0:T(8,128)(2,1)S(1)} %all-to-all-done), channel_id=1, source_target_pairs={{0,128},{64,192},{128,0},{192,64},{1,129},{65,193},{129,1},{193,65... | collective-permute-start | bytes 786440 | tf_op jit(solution)/shard_map/ppermute | solution.py:26
  41.8 12.3 %collective-permute-start.10 = (bf16[32,32,128]{2,1,0:T(8,128)(2,1)S(1)}, bf16[32,32,128]{2,1,0:T(8,128)(2,1)S(1)}, u32[]{:S(2)}, u32[]{:S(2)}) collective-permute-start(bf16[32,32,128]{2,1,0:T(8,128)(2,1)S(1)} %all-to-all-done), channel_id=1, source_target_pairs={{0,64},{64,128},{128,192},{192,0},{1,65},{65,129},{129,193},{193,1... | collective-permute-start | bytes 786440 | tf_op jit(solution)/shard_map/ppermute | solution.py:26
  68.5 23.9 %all-to-all-start.2 = ((bf16[32,48,128]{2,1,0:T(8,128)(2,1)}), bf16[32,48,128]{2,1,0:T(8,128)(2,1)S(1)}, u32[]{:S(2)}, u32[]{:S(2)}) async-start(bf16[32,48,128]{2,1,0:T(8,128)(2,1)} %shard_map.96), calls=%async_computation.2 | async-start | bytes 786432 | tf_op jit(solution)/shard_map/all_to_all | solution.py:38
  82.1 20.8 %collective-permute-start.16 = (bf16[256,128]{1,0:T(8,128)(2,1)S(1)}, bf16[256,128]{1,0:T(8,128)(2,1)S(1)}, u32[]{:S(2)}, u32[]{:S(2)}) collective-permute-start(bf16[256,128]{1,0:T(8,128)(2,1)S(1)} %get-tuple-element.36), channel_id=1, source_target_pairs={{64,0},{128,64},{192,128},{65,1},{129,65},{193,129},{66,2},{130,66... | collective-permute-start | bytes 196616 | tf_op jit(solution)/shard_map/ppermute | solution.py:30
  84.8 20.0 %collective-permute-start.17 = (bf16[256,128]{1,0:T(8,128)(2,1)S(1)}, bf16[256,128]{1,0:T(8,128)(2,1)S(1)}, u32[]{:S(2)}, u32[]{:S(2)}) collective-permute-start(bf16[256,128]{1,0:T(8,128)(2,1)S(1)} %get-tuple-element.36), channel_id=1, source_target_pairs={{128,0},{192,64},{129,1},{193,65},{130,2},{194,66},{131,3},{195,67... | collective-permute-start | bytes 196616 | tf_op jit(solution)/shard_map/ppermute | solution.py:30
  87.1 17.9 %collective-permute-start.18 = (bf16[256,128]{1,0:T(8,128)(2,1)S(1)}, bf16[256,128]{1,0:T(8,128)(2,1)S(1)}, u32[]{:S(2)}, u32[]{:S(2)}) collective-permute-start(bf16[256,128]{1,0:T(8,128)(2,1)S(1)} %get-tuple-element.36), channel_id=1, source_target_pairs={{192,0},{193,1},{194,2},{195,3},{196,4},{197,5},{198,6},{199,7},{2... | collective-permute-start | bytes 196616 | tf_op jit(solution)/shard_map/ppermute | solution.py:30
  96.8 12.7 %collective-permute-start.12 = (bf16[816,128]{1,0:T(8,128)(2,1)S(1)}, bf16[816,128]{1,0:T(8,128)(2,1)S(1)}, u32[]{:S(2)}, u32[]{:S(2)}) collective-permute-start(bf16[816,128]{1,0:T(8,128)(2,1)S(1)} %slice.29), channel_id=1, source_target_pairs={{0,192},{64,0},{128,64},{192,128},{1,193},{65,1},{129,65},{193,129... | collective-permute-start | bytes 626696 | tf_op jit(solution)/shard_map/ppermute | solution.py:26
  97.7 11.8 %collective-permute-start.13 = (bf16[560,128]{1,0:T(8,128)(2,1)S(1)}, bf16[560,128]{1,0:T(8,128)(2,1)S(1)}, u32[]{:S(2)}, u32[]{:S(2)}) collective-permute-start(bf16[560,128]{1,0:T(8,128)(2,1)S(1)} %slice.30), channel_id=1, source_target_pairs={{0,128},{64,192},{128,0},{192,64},{1,129},{65,193},{129,1},{193,65... | collective-permute-start | bytes 430088 | tf_op jit(solution)/shard_map/ppermute | solution.py:26
  102.9 50.7 %collective-permute-start = (bf16[256,2048]{1,0:T(8,128)(2,1)}, bf16[256,2048]{1,0:T(8,128)(2,1)}, u32[]{:S(2)}, u32[]{:S(2)}) collective-permute-start(bf16[256,2048]{1,0:T(8,128)(2,1)} %get-tuple-element.31), channel_id=1, source_target_pairs={{0,24},{8,0},{16,8},{24,16},{1,25},{9,1},{17,9},{25,17},{2,26},{10... | collective-permute-start | bytes 3145736 | tf_op jit(solution)/shard_map/ppermute | solution.py:26
  104.9 48.8 %collective-permute-start.3 = (bf16[256,2048]{1,0:T(8,128)(2,1)}, bf16[256,2048]{1,0:T(8,128)(2,1)}, u32[]{:S(2)}, u32[]{:S(2)}) collective-permute-start(bf16[256,2048]{1,0:T(8,128)(2,1)} %get-tuple-element.30), channel_id=1, source_target_pairs={{0,8},{8,16},{16,24},{24,0},{1,9},{9,17},{17,25},{25,1},{2,10},{10... | collective-permute-start | bytes 3145736 | tf_op jit(solution)/shard_map/ppermute | solution.py:26
  105.0 4.5 %collective-permute-start.14 = (bf16[304,128]{1,0:T(8,128)(2,1)S(1)}, bf16[304,128]{1,0:T(8,128)(2,1)S(1)}, u32[]{:S(2)}, u32[]{:S(2)}) collective-permute-start(bf16[304,128]{1,0:T(8,128)(2,1)S(1)} %slice.31), channel_id=1, source_target_pairs={{0,64},{64,128},{128,192},{192,0},{1,65},{65,129},{129,193},{193,1... | collective-permute-start | bytes 233480 | tf_op jit(solution)/shard_map/ppermute | solution.py:26
  109.5 5.0 %collective-permute-start.19 = (bf16[4,256,128]{2,1,0:T(8,128)(2,1)S(1)}, bf16[4,256,128]{2,1,0:T(8,128)(2,1)S(1)}, u32[]{:S(2)}, u32[]{:S(2)}) collective-permute-start(bf16[4,256,128]{2,1,0:T(8,128)(2,1)S(1)} %pad_maximum_fusion.2.slope_own_ref), channel_id=1, source_target_pairs={{0,32},{32,0},{1,33},{33,1},{2,34},{34,2},{3,35},{35,3},{4,36},{36... | collective-permute-start | bytes 786440 | tf_op jit(solution)/shard_map/ppermute | solution.py:34
  109.6 6.4 %collective-permute-start.15 = (bf16[2752,128]{1,0:T(8,128)(2,1)S(1)}, bf16[2752,128]{1,0:T(8,128)(2,1)}, u32[]{:S(2)}, u32[]{:S(2)}) collective-permute-start(bf16[2752,128]{1,0:T(8,128)(2,1)S(1)} %pad_maximum_fusion.1.own_ref), channel_id=1, source_target_pairs={{0,32},{32,0},{1,33},{33,1},{2,34},{34,2},{3,35},{35,3},{4,36},{36... | collective-permute-start | bytes 2113544 | tf_op jit(solution)/shard_map/ppermute | solution.py:34
  112.5 30.3 %collective-permute-start.1 = (bf16[256,1024]{1,0:T(8,128)(2,1)}, bf16[256,1024]{1,0:T(8,128)(2,1)}, u32[]{:S(2)}, u32[]{:S(2)}) collective-permute-start(bf16[256,1024]{1,0:T(8,128)(2,1)} %get-tuple-element.33), channel_id=1, source_target_pairs={{0,16},{8,24},{16,0},{24,8},{1,17},{9,25},{17,1},{25,9},{2,18},{10... | collective-permute-start | bytes 1572872 | tf_op jit(solution)/shard_map/ppermute | solution.py:26
  114.5 39.1 %collective-permute-start.2 = (bf16[256,1024]{1,0:T(8,128)(2,1)}, bf16[256,1024]{1,0:T(8,128)(2,1)}, u32[]{:S(2)}, u32[]{:S(2)}) collective-permute-start(bf16[256,1024]{1,0:T(8,128)(2,1)} %get-tuple-element.32), channel_id=1, source_target_pairs={{0,16},{8,24},{16,0},{24,8},{1,17},{9,25},{17,1},{25,9},{2,18},{10... | collective-permute-start | bytes 1572872 | tf_op jit(solution)/shard_map/ppermute | solution.py:26
  123.3 30.7 %collective-permute-start.20 = (bf16[512,128]{1,0:T(8,128)(2,1)}, bf16[512,128]{1,0:T(8,128)(2,1)S(1)}, u32[]{:S(2)}, u32[]{:S(2)}) collective-permute-start(bf16[512,128]{1,0:T(8,128)(2,1)} %get-tuple-element.22), channel_id=1, source_target_pairs={{0,24},{8,0},{16,8},{24,16},{1,25},{9,1},{17,9},{25,17},{2,26},{10... | collective-permute-start | bytes 393224 | tf_op jit(solution)/shard_map/ppermute | solution.py:26
  142.8 12.2 %collective-permute-start.21 = (bf16[512,128]{1,0:T(8,128)(2,1)}, bf16[512,128]{1,0:T(8,128)(2,1)S(1)}, u32[]{:S(2)}, u32[]{:S(2)}) collective-permute-start(bf16[512,128]{1,0:T(8,128)(2,1)} %get-tuple-element.23), channel_id=1, source_target_pairs={{0,16},{8,24},{16,0},{24,8},{1,17},{9,25},{17,1},{25,9},{2,18},{10... | collective-permute-start | bytes 393224 | tf_op jit(solution)/shard_map/ppermute | solution.py:26
  153.7 6.4 %collective-permute-start.22 = (bf16[512,128]{1,0:T(8,128)(2,1)}, bf16[512,128]{1,0:T(8,128)(2,1)S(1)}, u32[]{:S(2)}, u32[]{:S(2)}) collective-permute-start(bf16[512,128]{1,0:T(8,128)(2,1)} %get-tuple-element.24), channel_id=1, source_target_pairs={{0,8},{8,16},{16,24},{24,0},{1,9},{9,17},{17,25},{25,1},{2,10},{10... | collective-permute-start | bytes 393224 | tf_op jit(solution)/shard_map/ppermute | solution.py:26
  187.8 14.7 %all-to-all-start.4 = ((bf16[32,32,128]{2,1,0:T(8,128)(2,1)}), bf16[32,32,128]{2,1,0:T(8,128)(2,1)S(1)}, u32[]{:S(2)}, u32[]{:S(2)}) async-start(bf16[32,32,128]{2,1,0:T(8,128)(2,1)} %broadcast_in_dim.25), calls=%async_computation.4 | async-start | bytes 524288 | tf_op jit(solution)/shard_map/all_to_all | solution.py:38
  (25 other events, 213.7 us)

commit v5 on v3

--- a/solution.py
+++ b/solution.py
@@ -165,25 +165,30 @@
     lanes = lax.broadcasted_iota(jnp.int32, gram.shape, 1)
     diagonal = jnp.where(rows == lanes, gram, 0.0)
     trace_sum = jnp.sum(jnp.sum(diagonal, axis=1, keepdims=True), axis=0, keepdims=True) + 1e-06
-    scaled = gram / trace_sum
-    down0 = jnp.where(rows < TASKS, 1.0 / TASKS, 0.0)
-    along0 = jnp.where(lanes < TASKS, 1.0 / TASKS, 0.0)
-
-    def advance(counter, carry):
-        down, along = carry
-        step_down = jnp.sum(scaled * along, axis=1, keepdims=True)
-        step_along = jnp.sum(scaled * down, axis=0, keepdims=True)
-        total = jnp.sum(down, axis=0, keepdims=True)
-        rate = -STEP_RATE / total
-        down = down * jnp.exp(rate * step_down)
-        along = along * jnp.exp(rate * step_along)
-        return down, along
-
-    down, along = lax.fori_loop(0, STEPS, advance, (down0, along0))
-    total_along = jnp.sum(along[0:1], axis=1, keepdims=True)
-    total_down = jnp.sum(down, axis=0, keepdims=True)
-    mix_ref[...] = along / total_along
-    column_weight = jnp.sum((down / total_down) * mask_ref[0:8], axis=0, keepdims=True)
+    scaled = gram * (-STEP_RATE / trace_sum)
+    tasks = range(TASKS)
+    entry = [[jnp.broadcast_to(scaled[t : t + 1, u : u + 1], (8, 128)) for u in tasks] for t in tasks]
+
+    def advance(counter, weights):
+        total = ((weights[0] + weights[1]) + (weights[2] + weights[3])) + (weights[4] + weights[5])
+        inverse = 1.0 / total
+        moved = []
+        for t in tasks:
+            terms = [entry[t][u] * weights[u] for u in tasks]
+            step = ((terms[0] + terms[1]) + (terms[2] + terms[3])) + (terms[4] + terms[5])
+            moved.append(weights[t] * jnp.exp(step * inverse))
+        return tuple(moved)
+
+    even = jnp.full((8, 128), 1.0 / TASKS, F32)
+    weights = lax.fori_loop(0, STEPS, advance, (even,) * TASKS)
+    total = ((weights[0] + weights[1]) + (weights[2] + weights[3])) + (weights[4] + weights[5])
+    weights = [weight / total for weight in weights]
+    mix = jnp.zeros((8, 128), F32)
+    column_weight = jnp.zeros((1, 128), F32)
+    for t in tasks:
+        mix = jnp.where(lanes == t, weights[t], mix)
+        column_weight = column_weight + weights[t][0:1] * mask_ref[t : t + 1]
+    mix_ref[...] = mix
 
     def cross(stage, source):
         away = (stage // NC - my_x) % NX
@@ -199,14 +204,21 @@
         away = (stage // NC - my_x) % NX
         return jnp.where(my_c == stage % NC, slope_own_ref[away], slope_other_ref[away])
 
-    active = active_ref[...]
+    active = active_ref[...].T
     weighted = (residual_ref[...].astype(F32) * column_weight).astype(BF16)
-    first = across(weighted, active)
+    first = jnp.dot(active, weighted, preferred_element_type=F32)
     inners = {}
     for stage in range(SECTIONS - 1, -1, -1):
-        branch = jnp.dot(weighted, cross(stage, stage), preferred_element_type=F32)
-        for s in range(SECTIONS - 1, stage, -1):
-            branch = branch + jnp.dot(inners[s], cross(stage, s), preferred_element_type=F32)
+        left = [weighted] + [inners[s] for s in range(SECTIONS - 1, stage, -1)]
+        right = [cross(stage, s) for s in [stage] + list(range(SECTIONS - 1, stage, -1))]
+        branch = None
+        for n in range(0, len(left), 2):
+            term = jnp.dot(
+                jnp.concatenate(left[n : n + 2], axis=1),
+                jnp.concatenate(right[n : n + 2], axis=0),
+                preferred_element_type=F32,
+            )
+            branch = term if branch is None else branch + term
         inner = (branch * slope_of(stage).astype(F32)).astype(BF16)
         inners[stage] = inner
 
@@ -217,7 +229,8 @@
             send2_ref[256:512, :] = inner
             send3_ref[256:512, :] = inner
 
-        product = jnp.where(stage > my_stage, across(inner, active), 0.0)
+        product = jnp.dot(active, inner, preferred_element_type=F32)
+        product = jnp.where(stage > my_stage, product, 0.0)
         product = jnp.where(stage == my_stage, first, product)
         lo = 128 * (SECTIONS - 1 - stage)
         middle_ref[lo : lo + 128, :] = product.astype(BF16)
@@ -326,6 +339,9 @@
     slope_own = jnp.stack([slope] + [from_later(slope, k) for k in range(1, NX)])
     slope_other = swap_c(slope_own)
 
+    late_y, sent = lax.optimization_barrier((my_y, sent))
+    x2a = cut(late_y, 2, 0, wide // 2)
+    x2b = cut(late_y, 2, wide // 2, wide // 2)
     got = exchange_dp(sent)
     part, cross_rows, _ = local_call(
         heads_kernel,
@@ -337,7 +353,7 @@
     low = (part[256:] - top[256:].astype(F32)).astype(BF16)
     halves = jnp.concatenate([top, low], axis=0)
     others = [shift(halves, "x", -k) for k in range(1, NX)]
-    x2a = shift(cut(my_y, 2, 0, wide // 2), "y", -2)
+    x2a = shift(x2a, "y", -2)
     sent, residual = local_call(
         gram_kernel,
         [((DP, 48, rank), BF16), ((256, rank), BF16)],
@@ -348,7 +364,7 @@
     kept = [cross]
     for k in range(1, NX):
         kept.append(from_later(cross[: LATER_ROWS[k]], k))
-    x2b = shift(cut(my_y, 2, wide // 2, wide // 2), "y", -2)
+    x2b = shift(x2b, "y", -2)
     cross_own = jnp.concatenate(kept, axis=0)
     cross_other = swap_c(cross_own)
     keep, send1, send2, send3, inner, mix, _ = local_call(
@@ -367,7 +383,7 @@
     middle = exchange_dp(jnp.broadcast_to(rows[None], (DP, 32, rank)))
     middle = middle.reshape(SECTIONS, rank, rank)
     grad_up = lax.dot_general(
-        factors, middle, (((0, 2), (0, 1)), ((), ())), preferred_element_type=F32
+        factors, middle, (((0, 2), (0, 2)), ((), ())), preferred_element_type=F32
     )
     grad_down = jnp.concatenate([total[:128].T, total[128:256].T], axis=0)
     return (grad_down[None], grad_up[None], mix[0, :TASKS])

time: 201 us -> 197 us (0.980)
    ppermute x13, waiting for transfers between devices: 35.4 us -> 40.1 us  [shift(): lax.ppermute(value, axis, [(src, (src + steps) % count) for src in range(...]
    ppermute x1, waiting for transfers between devices: 6.41 us -> 3.41 us  [stages(): piece = lax.ppermute(piece, ('x', 'y'), turn)]
    unnamed x51 -> x53, local copies, waits for them, and re-layouts: 4.48 us -> 3.87 us
  transfers between devices with their start and end apart: 27 -> 27, of which waited for: 12 -> 12; matrix products, arithmetic and copies ran while one was open for 9% -> 9% of each run, Pallas kernels for 4% -> 3%
where the time goes in v5:
time: 197 us; the launch traced here: 195 us
  waiting for transfers between devices  58 us (29%)
  starting transfers between devices  46.9 us (24%)
  blocking collectives  46.4 us (24%)
  Pallas kernels  17.8 us (9%)
  local copies, waits for them, and re-layouts  15.6 us (8%)
  matrix products  5.03 us (3%)
  other arithmetic  4.01 us (2%)
    ppermute x13, waiting for transfers between devices, shift(): lax.ppermute(value, axis, [(src, (src + steps) % count) for src in range(...  40.1 us
    all_to_all x1, blocking collectives, exchange_dp(): return lax.all_to_all(blocks, ('y', 'z'), 0, 0, tiled=True)  26.8 us
    all_to_all x1, blocking collectives, stages(): got = lax.all_to_all(part_down, 'z', 0, 0, tiled=True)  19.6 us
    ppermute x13, starting transfers between devices, shift(): lax.ppermute(value, axis, [(src, (src + steps) % count) for src in range(...  18.2 us
    pallas_call x4, Pallas kernels, local_call(): pl.pallas_call(kernel, out_shape=tuple((jax.ShapeDtypeStruct(shape, dtype...  13.1 us
    ppermute x6, starting transfers between devices, from_later(): lax.ppermute(value, 'x', [(src, src - steps) for src in range(steps, NX)])  12.3 us
    all_to_all x2, waiting for transfers between devices, exchange_dp(): return lax.all_to_all(blocks, ('y', 'z'), 0, 0, tiled=True)  12.1 us
    all_to_all x2, starting transfers between devices, exchange_dp(): return lax.all_to_all(blocks, ('y', 'z'), 0, 0, tiled=True)  9.17 us
  transfers between devices with their start and end apart: 27, of which 12 were waited for; matrix products, arithmetic and copies ran while one was open for 9% of the time, Pallas kernels for 3%

profile of v5, /device:TPU:4, one launch (start us, length us, event | category | flops | bytes accessed | tf_op | source)
XLA Modules:
  0.0 194.9 jit_solution(3380784122497496504)
XLA Ops:
  7.4 2.5 %collective-permute-start.4 = (bf16[1024,128]{1,0:T(8,128)(2,1)S(1)}, bf16[1024,128]{1,0:T(8,128)(2,1)S(1)}, u32[]{:S(2)}, u32[]{:S(2)}) collective-permute-start(bf16[1024,128]{1,0:T(8,128)(2,1)S(1)} %get-tuple-element.54), channel_id=1, source_target_pairs={{0,192},{64,0},{128,64},{192,128},{1,193},{65,1},{129,65},{193,129... | collective-permute-start | bytes 786440 | tf_op jit(solution)/shard_map/ppermute | solution.py:26
  10.6 5.8 %collective-permute-start.1 = (bf16[32,128]{1,0:T(8,128)(2,1)S(1)}, bf16[32,128]{1,0:T(8,128)(2,1)S(1)}, u32[]{:S(2)}, u32[]{:S(2)}) collective-permute-start(bf16[32,128]{1,0:T(8,128)(2,1)S(1)} %constant_dynamic-slice_fusion.3), channel_id=1, source_target_pairs={{0,0},{8,64},{16,128},{24,192},{64,8},{72,72},{80,136},{88,200},{1... | collective-permute-start | bytes 24584 | tf_op jit(solution)/shard_map/ppermute | solution.py:307
  18.5 3.4 %collective-permute-done.1.piece_ref = bf16[32,128]{1,0:T(8,128)(2,1)S(1)} collective-permute-done((bf16[32,128]{1,0:T(8,128)(2,1)S(1)}, bf16[32,128]{1,0:T(8,128)(2,1)S(1)}, u32[]{:S(2)}, u32[]{:S(2)}) %collective-permute-start.1) | collective-permute-done | bytes 8224 | tf_op jit(solution)/shard_map/ppermute | solution.py:307
  22.8 2.7 %shard_map.94 = (bf16[32,64,128]{2,1,0:T(8,128)(2,1)}, bf16[8,256,128]{2,1,0:T(8,128)(2,1)}, bf16[8,256,128]{2,1,0:T(8,128)(2,1)}) custom-call(s32[3]{0:T(128)} %pad_add_fusion.where_ref, bf16[32,128]{1,0:T(8,128)(2,1)} %copy-done.24, bf16[256,128]{1,0:T(8,128)(2,1)} %heads_ref.1, bf16[256,128]{1,0:T(8,128)(2,1)} %dynamic-slice_bitcast_fusion.3.up_ref, ...), custom_call_target="tpu_custom_call" | custom-call | tf_op jit(solution)/shard_map/pallas_call | solution.py:58
  25.5 26.8 %all_to_all.20.got_ref = bf16[32,64,128]{2,1,0:T(8,128)(2,1)} all-to-all(bf16[32,64,128]{2,1,0:T(8,128)(2,1)} %get-tuple-element.20), channel_id=1, replica_groups=mesh['x'=4,'c'=2,'y'=4,'z'=8] {'y','z'}, dimensions={0} | all-to-all | bytes 1048576 | tf_op jit(solution)/shard_map/all_to_all | solution.py:38
  63.1 4.0 %collective-permute-done.12.c_ref = bf16[512,128]{1,0:T(8,128)(2,1)S(1)} collective-permute-done((bf16[512,128]{1,0:T(8,128)(2,1)S(1)}, bf16[512,128]{1,0:T(8,128)(2,1)S(1)}, u32[]{:S(2)}, u32[]{:S(2)}) %collective-permute-start.12) | collective-permute-done | bytes 131104 | tf_op jit(solution)/shard_map/ppermute | solution.py:26
  68.5 2.6 %shard_map.96 = (bf16[32,48,128]{2,1,0:T(8,128)(2,1)}, bf16[256,128]{1,0:T(8,128)(2,1)}) custom-call(s32[3]{0:T(128)} %pad_add_fusion.where_ref, bf16[512,128]{1,0:T(8,128)(2,1)} %copy-done.8, bf16[512,128]{1,0:T(8,128)(2,1)} %copy-done.19, bf16[512,128]{1,0:T(8,128)(2,1)} %copy-done.18, bf16[512,128]{1,0:T(8,128)(2,1)} %copy-done.17, ...), custom_call_target="tpu_custom_call" | custom-call | tf_op jit(solution)/shard_map/pallas_call | solution.py:58
  71.1 5.3 %all-to-all-start.1 = ((bf16[32,48,128]{2,1,0:T(8,128)(2,1)}), bf16[32,48,128]{2,1,0:T(8,128)(2,1)S(1)}, u32[]{:S(2)}, u32[]{:S(2)}) async-start(bf16[32,48,128]{2,1,0:T(8,128)(2,1)} %get-tuple-element.24), calls=%async_computation.1 | async-start | bytes 786432 | tf_op jit(solution)/shard_map/all_to_all | solution.py:38
  76.4 4.1 %multiply_convert_fusion = (bf16[256,128]{1,0:T(8,128)(2,1)S(1)}, bf16[256,128]{1,0:T(8,128)(2,1)}) fusion(bf16[256,8192]{1,0:T(8,128)(2,1)} %bitcast.52, bf16[1,8192,128]{2,1,0:T(8,128)(2,1)S(1)} %copy-done), kind=kOutput, calls=%fused_computation.32 | convolution fusion | flops 537198592 | bytes 6422528 | tf_op jit(solution)/shard_map/dot_general | solution.py:335
  81.1 3.9 %collective-permute-start.19 = (bf16[256,128]{1,0:T(8,128)(2,1)S(1)}, bf16[256,128]{1,0:T(8,128)(2,1)S(1)}, u32[]{:S(2)}, u32[]{:S(2)}) collective-permute-start(bf16[256,128]{1,0:T(8,128)(2,1)S(1)} %get-tuple-element.50), channel_id=1, source_target_pairs={{128,0},{192,64},{129,1},{193,65},{130,2},{194,66},{131,3},{195,67... | collective-permute-start | bytes 196616 | tf_op jit(solution)/shard_map/ppermute | solution.py:30
  87.0 3.3 %all-to-all-done.1.got_ref = bf16[32,48,128]{2,1,0:T(8,128)(2,1)S(1)} async-done(((bf16[32,48,128]{2,1,0:T(8,128)(2,1)}), bf16[32,48,128]{2,1,0:T(8,128)(2,1)S(1)}, u32[]{:S(2)}, u32[]{:S(2)}) %all-to-all-start.1) | async-done | bytes 393248 | tf_op jit(solution)/shard_map/all_to_all | solution.py:38
  90.3 3.3 %collective-permute-start.15 = (bf16[512,128]{1,0:T(8,128)(2,1)S(1)}, bf16[512,128]{1,0:T(8,128)(2,1)S(1)}, u32[]{:S(2)}, u32[]{:S(2)}) collective-permute-start(bf16[512,128]{1,0:T(8,128)(2,1)S(1)} %bitcast.61), channel_id=1, source_target_pairs={{128,0},{192,64},{129,1},{193,65},{130,2},{194,66},{131,3},{195,67... | collective-permute-start | bytes 393224 | tf_op jit(solution)/shard_map/ppermute | solution.py:30
  95.5 3.2 %constant_dynamic-slice_fusion = (bf16[256,2048]{1,0:T(8,128)(2,1)}, bf16[256,2048]{1,0:T(8,128)(2,1)}) fusion(bf16[256,8192]{1,0:T(8,128)(2,1)} %bitcast.53, s32[]{:T(128)S(6)} %select_n.85, s32[]{:T(128)S(6)} %select_n.69), kind=kLoop, calls=%fused_computation.44 | loop fusion | bytes 4194312 | tf_op jit(solution)/shard_map/dynamic_slice | solution.py:323
  99.4 2.6 %collective-permute-start = (bf16[256,2048]{1,0:T(8,128)(2,1)}, bf16[256,2048]{1,0:T(8,128)(2,1)}, u32[]{:S(2)}, u32[]{:S(2)}) collective-permute-start(bf16[256,2048]{1,0:T(8,128)(2,1)} %get-tuple-element.39), channel_id=1, source_target_pairs={{0,24},{8,0},{16,8},{24,16},{1,25},{9,1},{17,9},{25,17},{2,26},{10... | collective-permute-start | bytes 3145736 | tf_op jit(solution)/shard_map/ppermute | solution.py:26
  104.6 2.3 %constant_dynamic-slice_fusion.1 = (bf16[256,1024]{1,0:T(8,128)(2,1)}, bf16[256,1024]{1,0:T(8,128)(2,1)}) fusion(bf16[256,8192]{1,0:T(8,128)(2,1)} %bitcast.54, s32[]{:T(128)S(6)} %select_n.83, s32[]{:T(128)S(6)} %select_n.82), kind=kLoop, calls=%fused_computation.45 | loop fusion | bytes 2097160 | tf_op jit(solution)/shard_map/dynamic_slice | solution.py:323
  107.4 3.0 %collective-permute-start.7 = (bf16[256,1024]{1,0:T(8,128)(2,1)}, bf16[256,1024]{1,0:T(8,128)(2,1)}, u32[]{:S(2)}, u32[]{:S(2)}) collective-permute-start(bf16[256,1024]{1,0:T(8,128)(2,1)} %get-tuple-element.41), channel_id=1, source_target_pairs={{0,16},{8,24},{16,0},{24,8},{1,17},{9,25},{17,1},{25,9},{2,18},{10... | collective-permute-start | bytes 1572872 | tf_op jit(solution)/shard_map/ppermute | solution.py:26
  111.3 5.5 %shard_map.97 = (bf16[256,128]{1,0:T(8,128)(2,1)}, bf16[512,128]{1,0:T(8,128)(2,1)}, bf16[512,128]{1,0:T(8,128)(2,1)}, bf16[512,128]{1,0:T(8,128)(2,1)}, bf16[25...) custom-call(s32[3]{0:T(128)} %pad_add_fusion.where_ref, bf16[32,48,128]{2,1,0:T(8,128)(2,1)} %copy-done.1, ...), custom_call_target="tpu_custom_call" | custom-call | tf_op jit(solution)/shard_map/pallas_call | solution.py:58
  117.1 20.1 %collective-permute-done.8.x2b_ref = bf16[256,1024]{1,0:T(8,128)(2,1)S(1)} collective-permute-done((bf16[256,1024]{1,0:T(8,128)(2,1)}, bf16[256,1024]{1,0:T(8,128)(2,1)S(1)}, u32[]{:S(2)}, u32[]{:S(2)}) %collective-permute-start.8) | collective-permute-done | bytes 524320 | tf_op jit(solution)/shard_map/ppermute | solution.py:26
  138.4 8.6 %collective-permute-done.7.x2a_ref = bf16[256,1024]{1,0:T(8,128)(2,1)} collective-permute-done((bf16[256,1024]{1,0:T(8,128)(2,1)}, bf16[256,1024]{1,0:T(8,128)(2,1)}, u32[]{:S(2)}, u32[]{:S(2)}) %collective-permute-start.7) | collective-permute-done | bytes 524320 | tf_op jit(solution)/shard_map/ppermute | solution.py:26
  148.5 4.9 %collective-permute-done.24.got3_ref = bf16[512,128]{1,0:T(8,128)(2,1)S(1)} collective-permute-done((bf16[512,128]{1,0:T(8,128)(2,1)}, bf16[512,128]{1,0:T(8,128)(2,1)S(1)}, u32[]{:S(2)}, u32[]{:S(2)}) %collective-permute-start.24) | collective-permute-done | bytes 131104 | tf_op jit(solution)/shard_map/ppermute | solution.py:26
  154.1 4.7 %down_product.1 = bf16[8,288,128]{2,1,0:T(8,128)(2,1)} custom-call(s32[1]{0:T(128)} %bitcast.y_ref, bf16[256,8192]{1,0:T(8,128)(2,1)} %bitcast.55, bf16[256,2048]{1,0:T(8,128)(2,1)} %collective-permute-done.x1_ref, bf16[256,1024]{1,0:T(8,128)(2,1)} %collective-permute-done.7.x2a_ref, bf16[256,1024]{1,0:T(8,128)(2,1)} %copy-done.6, ...), custom_call_target="tpu_custom_call" | custom-call | tf_op jit(solution)/shard_map/down_product/pallas_call | solution.py:267
  158.9 19.6 %all_to_all.21 = bf16[8,288,128]{2,1,0:T(8,128)(2,1)S(1)} all-to-all(bf16[8,288,128]{2,1,0:T(8,128)(2,1)} %down_product.1), channel_id=1, replica_groups=mesh['x'=4,'c'=2,'y'=4,'z'=8] {'z'}, dimensions={0} | all-to-all | bytes 1179648 | tf_op jit(solution)/shard_map/all_to_all | solution.py:380
  179.3 3.9 %all-to-all-start.3 = ((bf16[32,32,128]{2,1,0:T(8,128)(2,1)}), bf16[32,32,128]{2,1,0:T(8,128)(2,1)S(1)}, u32[]{:S(2)}, u32[]{:S(2)}) async-start(bf16[32,32,128]{2,1,0:T(8,128)(2,1)} %broadcast_in_dim.18), calls=%async_computation.3 | async-start | bytes 524288 | tf_op jit(solution)/shard_map/all_to_all | solution.py:38
  185.1 8.8 %all-to-all-done.3 = bf16[32,32,128]{2,1,0:T(8,128)(2,1)S(1)} async-done(((bf16[32,32,128]{2,1,0:T(8,128)(2,1)}), bf16[32,32,128]{2,1,0:T(8,128)(2,1)S(1)}, u32[]{:S(2)}, u32[]{:S(2)}) %all-to-all-start.3) | async-done | bytes 262176 | tf_op jit(solution)/shard_map/all_to_all | solution.py:38
  (121 shorter events, 38.8 us)
Async XLA Ops:
  2.8 2.2 %collective-permute-start.3 = (bf16[256,128]{1,0:T(8,128)(2,1)S(1)}, bf16[256,128]{1,0:T(8,128)(2,1)S(1)}, u32[]{:S(2)}, u32[]{:S(2)}) collective-permute-start(bf16[256,128]{1,0:T(8,128)(2,1)S(1)} %dynamic-slice_bitcast_fusion.2.own_ref), channel_id=1, source_target_pairs={{0,32},{32,0},{1,33},{33,1},{2,34},{34,2},{3,35},{35,3},{4,36},{36... | collective-permute-start | bytes 196616 | tf_op jit(solution)/shard_map/ppermute | solution.py:34
  5.0 16.9 %collective-permute-start.6 = (bf16[1024,128]{1,0:T(8,128)(2,1)S(1)}, bf16[1024,128]{1,0:T(8,128)(2,1)S(1)}, u32[]{:S(2)}, u32[]{:S(2)}) collective-permute-start(bf16[1024,128]{1,0:T(8,128)(2,1)S(1)} %get-tuple-element.52), channel_id=1, source_target_pairs={{0,64},{64,128},{128,192},{192,0},{1,65},{65,129},{129,193},{193,1... | collective-permute-start | bytes 786440 | tf_op jit(solution)/shard_map/ppermute | solution.py:26
  6.3 15.7 %collective-permute-start.5 = (bf16[1024,128]{1,0:T(8,128)(2,1)S(1)}, bf16[1024,128]{1,0:T(8,128)(2,1)S(1)}, u32[]{:S(2)}, u32[]{:S(2)}) collective-permute-start(bf16[1024,128]{1,0:T(8,128)(2,1)S(1)} %get-tuple-element.53), channel_id=1, source_target_pairs={{0,128},{64,192},{128,0},{192,64},{1,129},{65,193},{129,1},{193,65... | collective-permute-start | bytes 786440 | tf_op jit(solution)/shard_map/ppermute | solution.py:26
  7.4 14.6 %collective-permute-start.4 = (bf16[1024,128]{1,0:T(8,128)(2,1)S(1)}, bf16[1024,128]{1,0:T(8,128)(2,1)S(1)}, u32[]{:S(2)}, u32[]{:S(2)}) collective-permute-start(bf16[1024,128]{1,0:T(8,128)(2,1)S(1)} %get-tuple-element.54), channel_id=1, source_target_pairs={{0,192},{64,0},{128,64},{192,128},{1,193},{65,1},{129,65},{193,129... | collective-permute-start | bytes 786440 | tf_op jit(solution)/shard_map/ppermute | solution.py:26
  10.6 11.3 %collective-permute-start.1 = (bf16[32,128]{1,0:T(8,128)(2,1)S(1)}, bf16[32,128]{1,0:T(8,128)(2,1)S(1)}, u32[]{:S(2)}, u32[]{:S(2)}) collective-permute-start(bf16[32,128]{1,0:T(8,128)(2,1)S(1)} %constant_dynamic-slice_fusion.3), channel_id=1, source_target_pairs={{0,0},{8,64},{16,128},{24,192},{64,8},{72,72},{80,136},{88,200},{1... | collective-permute-start | bytes 24584 | tf_op jit(solution)/shard_map/ppermute | solution.py:307
  57.3 5.8 %collective-permute-start.13 = (bf16[512,128]{1,0:T(8,128)(2,1)S(1)}, bf16[512,128]{1,0:T(8,128)(2,1)S(1)}, u32[]{:S(2)}, u32[]{:S(2)}) collective-permute-start(bf16[512,128]{1,0:T(8,128)(2,1)S(1)} %pad_maximum_fusion.8.a_ref), channel_id=1, source_target_pairs={{0,64},{64,128},{128,192},{192,0},{1,65},{65,129},{129,193},{193,1... | collective-permute-start | bytes 393224 | tf_op jit(solution)/shard_map/ppermute | solution.py:26
  59.1 8.0 %collective-permute-start.12 = (bf16[512,128]{1,0:T(8,128)(2,1)S(1)}, bf16[512,128]{1,0:T(8,128)(2,1)S(1)}, u32[]{:S(2)}, u32[]{:S(2)}) collective-permute-start(bf16[512,128]{1,0:T(8,128)(2,1)S(1)} %pad_maximum_fusion.8.a_ref), channel_id=1, source_target_pairs={{0,128},{64,192},{128,0},{192,64},{1,129},{65,193},{129,1},{193,65... | collective-permute-start | bytes 393224 | tf_op jit(solution)/shard_map/ppermute | solution.py:26
  60.8 7.1 %collective-permute-start.11 = (bf16[512,128]{1,0:T(8,128)(2,1)S(1)}, bf16[512,128]{1,0:T(8,128)(2,1)S(1)}, u32[]{:S(2)}, u32[]{:S(2)}) collective-permute-start(bf16[512,128]{1,0:T(8,128)(2,1)S(1)} %pad_maximum_fusion.8.a_ref), channel_id=1, source_target_pairs={{0,192},{64,0},{128,64},{192,128},{1,193},{65,1},{129,65},{193,129... | collective-permute-start | bytes 393224 | tf_op jit(solution)/shard_map/ppermute | solution.py:26
  71.1 19.2 %all-to-all-start.1 = ((bf16[32,48,128]{2,1,0:T(8,128)(2,1)}), bf16[32,48,128]{2,1,0:T(8,128)(2,1)S(1)}, u32[]{:S(2)}, u32[]{:S(2)}) async-start(bf16[32,48,128]{2,1,0:T(8,128)(2,1)} %get-tuple-element.24), calls=%async_computation.1 | async-start | bytes 786432 | tf_op jit(solution)/shard_map/all_to_all | solution.py:38
  80.5 18.2 %collective-permute-start.20 = (bf16[256,128]{1,0:T(8,128)(2,1)S(1)}, bf16[256,128]{1,0:T(8,128)(2,1)S(1)}, u32[]{:S(2)}, u32[]{:S(2)}) collective-permute-start(bf16[256,128]{1,0:T(8,128)(2,1)S(1)} %get-tuple-element.50), channel_id=1, source_target_pairs={{192,0},{193,1},{194,2},{195,3},{196,4},{197,5},{198,6},{199,7},{2... | collective-permute-start | bytes 196616 | tf_op jit(solution)/shard_map/ppermute | solution.py:30
  81.1 18.3 %collective-permute-start.19 = (bf16[256,128]{1,0:T(8,128)(2,1)S(1)}, bf16[256,128]{1,0:T(8,128)(2,1)S(1)}, u32[]{:S(2)}, u32[]{:S(2)}) collective-permute-start(bf16[256,128]{1,0:T(8,128)(2,1)S(1)} %get-tuple-element.50), channel_id=1, source_target_pairs={{128,0},{192,64},{129,1},{193,65},{130,2},{194,66},{131,3},{195,67... | collective-permute-start | bytes 196616 | tf_op jit(solution)/shard_map/ppermute | solution.py:30
  85.0 17.0 %collective-permute-start.18 = (bf16[256,128]{1,0:T(8,128)(2,1)S(1)}, bf16[256,128]{1,0:T(8,128)(2,1)S(1)}, u32[]{:S(2)}, u32[]{:S(2)}) collective-permute-start(bf16[256,128]{1,0:T(8,128)(2,1)S(1)} %get-tuple-element.50), channel_id=1, source_target_pairs={{64,0},{128,64},{192,128},{65,1},{129,65},{193,129},{66,2},{130,66... | collective-permute-start | bytes 196616 | tf_op jit(solution)/shard_map/ppermute | solution.py:30
  90.3 13.6 %collective-permute-start.15 = (bf16[512,128]{1,0:T(8,128)(2,1)S(1)}, bf16[512,128]{1,0:T(8,128)(2,1)S(1)}, u32[]{:S(2)}, u32[]{:S(2)}) collective-permute-start(bf16[512,128]{1,0:T(8,128)(2,1)S(1)} %bitcast.61), channel_id=1, source_target_pairs={{128,0},{192,64},{129,1},{193,65},{130,2},{194,66},{131,3},{195,67... | collective-permute-start | bytes 393224 | tf_op jit(solution)/shard_map/ppermute | solution.py:30
  93.6 10.3 %collective-permute-start.14 = (bf16[768,128]{1,0:T(8,128)(2,1)S(1)}, bf16[768,128]{1,0:T(8,128)(2,1)S(1)}, u32[]{:S(2)}, u32[]{:S(2)}) collective-permute-start(bf16[768,128]{1,0:T(8,128)(2,1)S(1)} %bitcast.60), channel_id=1, source_target_pairs={{64,0},{128,64},{192,128},{65,1},{129,65},{193,129},{66,2},{130,66... | collective-permute-start | bytes 589832 | tf_op jit(solution)/shard_map/ppermute | solution.py:30
  98.7 49.4 %collective-permute-start.9 = (bf16[256,2048]{1,0:T(8,128)(2,1)}, bf16[256,2048]{1,0:T(8,128)(2,1)}, u32[]{:S(2)}, u32[]{:S(2)}) collective-permute-start(bf16[256,2048]{1,0:T(8,128)(2,1)} %get-tuple-element.38), channel_id=1, source_target_pairs={{0,8},{8,16},{16,24},{24,0},{1,9},{9,17},{17,25},{25,1},{2,10},{10... | collective-permute-start | bytes 3145736 | tf_op jit(solution)/shard_map/ppermute | solution.py:26
  99.4 48.8 %collective-permute-start = (bf16[256,2048]{1,0:T(8,128)(2,1)}, bf16[256,2048]{1,0:T(8,128)(2,1)}, u32[]{:S(2)}, u32[]{:S(2)}) collective-permute-start(bf16[256,2048]{1,0:T(8,128)(2,1)} %get-tuple-element.39), channel_id=1, source_target_pairs={{0,24},{8,0},{16,8},{24,16},{1,25},{9,1},{17,9},{25,17},{2,26},{10... | collective-permute-start | bytes 3145736 | tf_op jit(solution)/shard_map/ppermute | solution.py:26
  103.8 3.5 %collective-permute-start.21 = (bf16[4,256,128]{2,1,0:T(8,128)(2,1)S(1)}, bf16[4,256,128]{2,1,0:T(8,128)(2,1)S(1)}, u32[]{:S(2)}, u32[]{:S(2)}) collective-permute-start(bf16[4,256,128]{2,1,0:T(8,128)(2,1)S(1)} %pad_maximum_fusion.7.slope_own_ref), channel_id=1, source_target_pairs={{0,32},{32,0},{1,33},{33,1},{2,34},{34,2},{3,35},{35,3},{4,36},{36... | collective-permute-start | bytes 786440 | tf_op jit(solution)/shard_map/ppermute | solution.py:34
  104.0 6.4 %collective-permute-start.17 = (bf16[2560,128]{1,0:T(8,128)(2,1)S(1)}, bf16[2560,128]{1,0:T(8,128)(2,1)S(1)}, u32[]{:S(2)}, u32[]{:S(2)}) collective-permute-start(bf16[2560,128]{1,0:T(8,128)(2,1)S(1)} %pad_maximum_fusion.own_ref), channel_id=1, source_target_pairs={{0,32},{32,0},{1,33},{33,1},{2,34},{34,2},{3,35},{35,3},{4,36},{36... | collective-permute-start | bytes 1966088 | tf_op jit(solution)/shard_map/ppermute | solution.py:34
  106.9 30.3 %collective-permute-start.8 = (bf16[256,1024]{1,0:T(8,128)(2,1)}, bf16[256,1024]{1,0:T(8,128)(2,1)S(1)}, u32[]{:S(2)}, u32[]{:S(2)}) collective-permute-start(bf16[256,1024]{1,0:T(8,128)(2,1)} %get-tuple-element.40), channel_id=1, source_target_pairs={{0,16},{8,24},{16,0},{24,8},{1,17},{9,25},{17,1},{25,9},{2,18},{10... | collective-permute-start | bytes 1572872 | tf_op jit(solution)/shard_map/ppermute | solution.py:26
  107.4 39.7 %collective-permute-start.7 = (bf16[256,1024]{1,0:T(8,128)(2,1)}, bf16[256,1024]{1,0:T(8,128)(2,1)}, u32[]{:S(2)}, u32[]{:S(2)}) collective-permute-start(bf16[256,1024]{1,0:T(8,128)(2,1)} %get-tuple-element.41), channel_id=1, source_target_pairs={{0,16},{8,24},{16,0},{24,8},{1,17},{9,25},{17,1},{25,9},{2,18},{10... | collective-permute-start | bytes 1572872 | tf_op jit(solution)/shard_map/ppermute | solution.py:26
  116.8 31.7 %collective-permute-start.22 = (bf16[512,128]{1,0:T(8,128)(2,1)}, bf16[512,128]{1,0:T(8,128)(2,1)S(1)}, u32[]{:S(2)}, u32[]{:S(2)}) collective-permute-start(bf16[512,128]{1,0:T(8,128)(2,1)} %get-tuple-element.28), channel_id=1, source_target_pairs={{0,24},{8,0},{16,8},{24,16},{1,25},{9,1},{17,9},{25,17},{2,26},{10... | collective-permute-start | bytes 393224 | tf_op jit(solution)/shard_map/ppermute | solution.py:26
  137.2 11.4 %collective-permute-start.23 = (bf16[512,128]{1,0:T(8,128)(2,1)}, bf16[512,128]{1,0:T(8,128)(2,1)S(1)}, u32[]{:S(2)}, u32[]{:S(2)}) collective-permute-start(bf16[512,128]{1,0:T(8,128)(2,1)} %get-tuple-element.29), channel_id=1, source_target_pairs={{0,16},{8,24},{16,0},{24,8},{1,17},{9,25},{17,1},{25,9},{2,18},{10... | collective-permute-start | bytes 393224 | tf_op jit(solution)/shard_map/ppermute | solution.py:26
  147.1 6.4 %collective-permute-start.24 = (bf16[512,128]{1,0:T(8,128)(2,1)}, bf16[512,128]{1,0:T(8,128)(2,1)S(1)}, u32[]{:S(2)}, u32[]{:S(2)}) collective-permute-start(bf16[512,128]{1,0:T(8,128)(2,1)} %get-tuple-element.30), channel_id=1, source_target_pairs={{0,8},{8,16},{16,24},{24,0},{1,9},{9,17},{17,25},{25,1},{2,10},{10... | collective-permute-start | bytes 393224 | tf_op jit(solution)/shard_map/ppermute | solution.py:26
  179.3 14.7 %all-to-all-start.3 = ((bf16[32,32,128]{2,1,0:T(8,128)(2,1)}), bf16[32,32,128]{2,1,0:T(8,128)(2,1)S(1)}, u32[]{:S(2)}, u32[]{:S(2)}) async-start(bf16[32,32,128]{2,1,0:T(8,128)(2,1)} %broadcast_in_dim.18), calls=%async_computation.3 | async-start | bytes 524288 | tf_op jit(solution)/shard_map/all_to_all | solution.py:38
  (29 other events, 238.2 us)

commit v6 on v5

--- a/solution.py
+++ b/solution.py
@@ -116,7 +116,7 @@
     cross_ref[...] = jnp.sum(got_ref[:, 32:64, :].astype(F32), axis=0).astype(BF16)
 
 
-def gram_kernel(where_ref, a_ref, b_ref, c_ref, d_ref, mask_ref, cross_ref, sent_ref, residual_ref):
+def gram_kernel(where_ref, a_ref, b_ref, c_ref, d_ref, mask_ref, sent_ref, residual_ref):
     def value(ref, lo, size):
         return ref[lo : lo + size, :].astype(F32)
 
@@ -139,10 +139,8 @@
     )
     top = part.astype(BF16)
     tile = jnp.concatenate([part, part - top.astype(F32)], axis=0).astype(BF16)
-    cross = cross_ref[...]
     for d in range(DP):
-        sent_ref[d, 0:32, :] = cross
-        sent_ref[d, 32:48, :] = tile
+        sent_ref[d] = tile
 
 
 LATER_ROWS = (1024, 768, 512, 256)
@@ -159,7 +157,7 @@
     my_c = where_ref[1]
     my_y = where_ref[2]
     my_stage = my_x * NC + my_c
-    tiles = jnp.sum(got_ref[:, 32:48, :].astype(F32), axis=0)
+    tiles = jnp.sum(got_ref[...].astype(F32), axis=0)
     gram = tiles[0:8] + tiles[8:16]
     rows = lax.broadcasted_iota(jnp.int32, gram.shape, 0)
     lanes = lax.broadcasted_iota(jnp.int32, gram.shape, 1)
@@ -332,22 +330,27 @@
         where, piece, heads, up_rows, at(pair, my_x), down_rows, partner, *gots,
     )
 
-    preact = jnp.dot(saved, down_map, preferred_element_type=F32)
+    late_y, down_late, sent = lax.optimization_barrier((my_y, down_map, sent))
+    x2a = cut(late_y, 2, 0, wide // 2)
+    x2b = cut(late_y, 2, wide // 2, wide // 2)
+    preact = jnp.dot(saved, down_late, preferred_element_type=F32)
     logistic = jax.nn.sigmoid(preact)
     active = (preact * logistic).astype(BF16)
     slope = (logistic * (1.0 + preact * (1.0 - logistic))).astype(BF16)
     slope_own = jnp.stack([slope] + [from_later(slope, k) for k in range(1, NX)])
     slope_other = swap_c(slope_own)
 
-    late_y, sent = lax.optimization_barrier((my_y, sent))
-    x2a = cut(late_y, 2, 0, wide // 2)
-    x2b = cut(late_y, 2, wide // 2, wide // 2)
     got = exchange_dp(sent)
     part, cross_rows, _ = local_call(
         heads_kernel,
         [((384, rank), F32), ((32, rank), BF16), ((1024, rank), BF16)],
         where, got, rep, head_targets[0],
     )
+    got = exchange_dp(jnp.broadcast_to(cross_rows[None], (DP, 32, rank)))
+    cross = got.reshape(-1, rank)
+    kept = [cross]
+    for k in range(1, NX):
+        kept.append(from_later(cross[: LATER_ROWS[k]], k))
     part = part + swap_c(part)
     top = part.astype(BF16)
     low = (part[256:] - top[256:].astype(F32)).astype(BF16)
@@ -356,14 +359,10 @@
     x2a = shift(x2a, "y", -2)
     sent, residual = local_call(
         gram_kernel,
-        [((DP, 48, rank), BF16), ((256, rank), BF16)],
-        where, halves, *others, mask, cross_rows,
+        [((DP, 16, rank), BF16), ((256, rank), BF16)],
+        where, halves, *others, mask,
     )
     got = exchange_dp(sent)
-    cross = got[:, :32].reshape(-1, rank)
-    kept = [cross]
-    for k in range(1, NX):
-        kept.append(from_later(cross[: LATER_ROWS[k]], k))
     x2b = shift(x2b, "y", -2)
     cross_own = jnp.concatenate(kept, axis=0)
     cross_other = swap_c(cross_own)

time: 197 us -> 190 us (0.964)
  the two profiles are of different devices: /device:TPU:4 before, /device:TPU:32 now
where the time goes in v6:
time: 190 us; the launch traced here: 189 us
  waiting for transfers between devices  52.7 us (28%)
  starting transfers between devices  51 us (27%)
  blocking collectives  43.1 us (23%)
  Pallas kernels  17.7 us (9%)
  local copies, waits for them, and re-layouts  16.3 us (9%)
  matrix products  5.03 us (3%)
  other arithmetic  2.26 us (1%)
    all_to_all x3, waiting for transfers between devices, exchange_dp(): return lax.all_to_all(blocks, ('y', 'z'), 0, 0, tiled=True)  24.5 us
    all_to_all x1, blocking collectives, exchange_dp(): return lax.all_to_all(blocks, ('y', 'z'), 0, 0, tiled=True)  21.9 us
    all_to_all x1, blocking collectives, stages(): got = lax.all_to_all(part_down, 'z', 0, 0, tiled=True)  21.2 us
    all_to_all x3, starting transfers between devices, exchange_dp(): return lax.all_to_all(blocks, ('y', 'z'), 0, 0, tiled=True)  21.2 us
    ppermute x13, starting transfers between devices, shift(): lax.ppermute(value, axis, [(src, (src + steps) % count) for src in range(...  20.8 us
    ppermute x13, waiting for transfers between devices, shift(): lax.ppermute(value, axis, [(src, (src + steps) % count) for src in range(...  19.5 us
    pallas_call x4, Pallas kernels, local_call(): pl.pallas_call(kernel, out_shape=tuple((jax.ShapeDtypeStruct(shape, dtype...  12.9 us
    ppermute x6, waiting for transfers between devices, from_later(): lax.ppermute(value, 'x', [(src, src - steps) for src in range(steps, NX)])  7.82 us
  transfers between devices with their start and end apart: 28, of which 11 were waited for; matrix products, arithmetic and copies ran while one was open for 9% of the time, Pallas kernels for 5%

profile of v6, /device:TPU:32, one launch (start us, length us, event | category | flops | bytes accessed | tf_op | source)
XLA Modules:
  0.0 189.2 jit_solution(858756222367841027)
XLA Ops:
  6.6 2.7 %collective-permute-start.5 = (bf16[1024,128]{1,0:T(8,128)(2,1)S(1)}, bf16[1024,128]{1,0:T(8,128)(2,1)S(1)}, u32[]{:S(2)}, u32[]{:S(2)}) collective-permute-start(bf16[1024,128]{1,0:T(8,128)(2,1)S(1)} %get-tuple-element.55), channel_id=1, source_target_pairs={{0,128},{64,192},{128,0},{192,64},{1,129},{65,193},{129,1},{193,65... | collective-permute-start | bytes 786440 | tf_op jit(solution)/shard_map/ppermute | solution.py:26
  14.6 6.8 %collective-permute-done.5.got2_ref = bf16[1024,128]{1,0:T(8,128)(2,1)S(1)} collective-permute-done((bf16[1024,128]{1,0:T(8,128)(2,1)S(1)}, bf16[1024,128]{1,0:T(8,128)(2,1)S(1)}, u32[]{:S(2)}, u32[]{:S(2)}) %collective-permute-start.5) | collective-permute-done | bytes 262176 | tf_op jit(solution)/shard_map/ppermute | solution.py:26
  22.2 2.7 %shard_map.94 = (bf16[32,64,128]{2,1,0:T(8,128)(2,1)}, bf16[8,256,128]{2,1,0:T(8,128)(2,1)}, bf16[8,256,128]{2,1,0:T(8,128)(2,1)}) custom-call(s32[3]{0:T(128)} %pad_add_fusion.where_ref, bf16[32,128]{1,0:T(8,128)(2,1)} %copy-done.20, bf16[256,128]{1,0:T(8,128)(2,1)} %heads_ref.1, bf16[256,128]{1,0:T(8,128)(2,1)} %dynamic-slice_bitcast_fusion.3.up_ref, ...), custom_call_target="tpu_custom_call" | custom-call | tf_op jit(solution)/shard_map/pallas_call | solution.py:58
  24.9 11.3 %all-to-all-start = ((bf16[32,64,128]{2,1,0:T(8,128)(2,1)}), bf16[32,64,128]{2,1,0:T(8,128)(2,1)S(1)}, u32[]{:S(2)}, u32[]{:S(2)}) async-start(bf16[32,64,128]{2,1,0:T(8,128)(2,1)} %get-tuple-element.21), calls=%async_computation | async-start | bytes 1048576 | tf_op jit(solution)/shard_map/all_to_all | solution.py:38
  36.3 4.1 %multiply_convert_fusion = (bf16[256,128]{1,0:T(8,128)(2,1)S(1)}, bf16[256,128]{1,0:T(8,128)(2,1)}) fusion(bf16[256,8192]{1,0:T(8,128)(2,1)} %bitcast.52, bf16[8192,128]{1,0:T(8,128)(2,1)S(1)} %bitcast.51), kind=kOutput, calls=%fused_computation.31 | convolution fusion | flops 537198592 | bytes 6422528 | tf_op jit(solution)/shard_map/dot_general | solution.py:336
  44.3 8.9 %all-to-all-done.got_ref = bf16[32,64,128]{2,1,0:T(8,128)(2,1)S(1)} async-done(((bf16[32,64,128]{2,1,0:T(8,128)(2,1)}), bf16[32,64,128]{2,1,0:T(8,128)(2,1)S(1)}, u32[]{:S(2)}, u32[]{:S(2)}) %all-to-all-start) | async-done | bytes 524320 | tf_op jit(solution)/shard_map/all_to_all | solution.py:38
  54.0 2.3 %shard_map.95 = (f32[384,128]{1,0:T(8,128)}, bf16[32,128]{1,0:T(8,128)(2,1)}, bf16[1024,128]{1,0:T(8,128)(2,1)}) custom-call(s32[3]{0:T(128)} %pad_add_fusion.where_ref, bf16[32,64,128]{2,1,0:T(8,128)(2,1)} %copy-done.2, bf16[8,256,128]{2,1,0:T(8,128)(2,1)} %get-tuple-element.22.rep_ref, bf16[32,128]{1,0:T(8,128)(2,1)} %bitcast.67), custom_call_target="tpu_custom_call" | custom-call | tf_op jit(solution)/shard_map/pallas_call | solution.py:58
  57.7 4.9 %all-to-all-start.2 = ((bf16[32,32,128]{2,1,0:T(8,128)(2,1)}), bf16[32,32,128]{2,1,0:T(8,128)(2,1)S(1)}, u32[]{:S(2)}, u32[]{:S(2)}) async-start(bf16[32,32,128]{2,1,0:T(8,128)(2,1)} %broadcast_in_dim.11), calls=%async_computation.2 | async-start | bytes 524288 | tf_op jit(solution)/shard_map/all_to_all | solution.py:38
  62.6 3.2 %constant_dynamic-slice_fusion = (bf16[256,2048]{1,0:T(8,128)(2,1)}, bf16[256,2048]{1,0:T(8,128)(2,1)}) fusion(bf16[256,8192]{1,0:T(8,128)(2,1)} %bitcast.53, s32[]{:T(128)S(6)} %select_n.85, s32[]{:T(128)S(6)} %select_n.69), kind=kLoop, calls=%fused_computation.43 | loop fusion | bytes 4194312 | tf_op jit(solution)/shard_map/dynamic_slice | solution.py:321
  69.2 6.4 %all-to-all-done.2 = bf16[32,32,128]{2,1,0:T(8,128)(2,1)S(1)} async-done(((bf16[32,32,128]{2,1,0:T(8,128)(2,1)}), bf16[32,32,128]{2,1,0:T(8,128)(2,1)S(1)}, u32[]{:S(2)}, u32[]{:S(2)}) %all-to-all-start.2) | async-done | bytes 262176 | tf_op jit(solution)/shard_map/all_to_all | solution.py:38
  79.6 7.8 %collective-permute-done.16 = bf16[256,128]{1,0:T(8,128)(2,1)S(1)} collective-permute-done((bf16[256,128]{1,0:T(8,128)(2,1)S(1)}, bf16[256,128]{1,0:T(8,128)(2,1)S(1)}, u32[]{:S(2)}, u32[]{:S(2)}) %collective-permute-start.16) | collective-permute-done | bytes 65568 | tf_op jit(solution)/shard_map/ppermute | solution.py:30
  87.6 3.0 %collective-permute-start.12 = (bf16[512,128]{1,0:T(8,128)(2,1)S(1)}, bf16[512,128]{1,0:T(8,128)(2,1)S(1)}, u32[]{:S(2)}, u32[]{:S(2)}) collective-permute-start(bf16[512,128]{1,0:T(8,128)(2,1)S(1)} %pad_maximum_fusion.8.a_ref), channel_id=1, source_target_pairs={{0,128},{64,192},{128,0},{192,64},{1,129},{65,193},{129,1},{193,65... | collective-permute-start | bytes 393224 | tf_op jit(solution)/shard_map/ppermute | solution.py:26
  92.7 4.6 %collective-permute-done.13.d_ref = bf16[512,128]{1,0:T(8,128)(2,1)S(1)} collective-permute-done((bf16[512,128]{1,0:T(8,128)(2,1)S(1)}, bf16[512,128]{1,0:T(8,128)(2,1)S(1)}, u32[]{:S(2)}, u32[]{:S(2)}) %collective-permute-start.13) | collective-permute-done | bytes 131104 | tf_op jit(solution)/shard_map/ppermute | solution.py:26
  97.3 2.3 %constant_dynamic-slice_fusion.1 = (bf16[256,1024]{1,0:T(8,128)(2,1)}, bf16[256,1024]{1,0:T(8,128)(2,1)}) fusion(bf16[256,8192]{1,0:T(8,128)(2,1)} %bitcast.54, s32[]{:T(128)S(6)} %select_n.83, s32[]{:T(128)S(6)} %select_n.82), kind=kLoop, calls=%fused_computation.44 | loop fusion | bytes 2097160 | tf_op jit(solution)/shard_map/dynamic_slice | solution.py:321
  101.1 2.2 %collective-permute-start.7 = (bf16[256,1024]{1,0:T(8,128)(2,1)}, bf16[256,1024]{1,0:T(8,128)(2,1)}, u32[]{:S(2)}, u32[]{:S(2)}) collective-permute-start(bf16[256,1024]{1,0:T(8,128)(2,1)} %get-tuple-element.43), channel_id=1, source_target_pairs={{0,16},{8,24},{16,0},{24,8},{1,17},{9,25},{17,1},{25,9},{2,18},{10... | collective-permute-start | bytes 1572872 | tf_op jit(solution)/shard_map/ppermute | solution.py:26
  104.2 2.4 %shard_map.96 = (bf16[32,16,128]{2,1,0:T(8,128)(2,1)}, bf16[256,128]{1,0:T(8,128)(2,1)}) custom-call(s32[3]{0:T(128)} %pad_add_fusion.where_ref, bf16[512,128]{1,0:T(8,128)(2,1)} %copy-done.7, bf16[512,128]{1,0:T(8,128)(2,1)} %copy-done.19, bf16[512,128]{1,0:T(8,128)(2,1)} %copy-done.18, bf16[512,128]{1,0:T(8,128)(2,1)} %copy-done.17, f32[128,128]{1,0:T(8,128)} %fusion.9.mask_ref), custom_call_target="tpu_custom_call" | custom-call | tf_op jit(solution)/shard_map/pallas_call | solution.py:58
  106.6 21.9 %all_to_all.25.got_ref = bf16[32,16,128]{2,1,0:T(8,128)(2,1)} all-to-all(bf16[32,16,128]{2,1,0:T(8,128)(2,1)} %get-tuple-element.24), channel_id=1, replica_groups=mesh['x'=4,'c'=2,'y'=4,'z'=8] {'y','z'}, dimensions={0} | all-to-all | bytes 262144 | tf_op jit(solution)/shard_map/all_to_all | solution.py:38
  128.5 5.5 %shard_map.97 = (bf16[256,128]{1,0:T(8,128)(2,1)}, bf16[512,128]{1,0:T(8,128)(2,1)}, bf16[512,128]{1,0:T(8,128)(2,1)}, bf16[512,128]{1,0:T(8,128)(2,1)}, bf16[25...) custom-call(s32[3]{0:T(128)} %pad_add_fusion.where_ref, bf16[32,16,128]{2,1,0:T(8,128)(2,1)} %all_to_all.25.got_ref, ...), custom_call_target="tpu_custom_call" | custom-call | tf_op jit(solution)/shard_map/pallas_call | solution.py:58
  136.8 3.7 %collective-permute-done.22.got1_ref = bf16[512,128]{1,0:T(8,128)(2,1)S(1)} collective-permute-done((bf16[512,128]{1,0:T(8,128)(2,1)}, bf16[512,128]{1,0:T(8,128)(2,1)S(1)}, u32[]{:S(2)}, u32[]{:S(2)}) %collective-permute-start.22) | collective-permute-done | bytes 131104 | tf_op jit(solution)/shard_map/ppermute | solution.py:26
  140.6 2.6 %collective-permute-done.23.got2_ref = bf16[512,128]{1,0:T(8,128)(2,1)S(1)} collective-permute-done((bf16[512,128]{1,0:T(8,128)(2,1)}, bf16[512,128]{1,0:T(8,128)(2,1)S(1)}, u32[]{:S(2)}, u32[]{:S(2)}) %collective-permute-start.23) | collective-permute-done | bytes 131104 | tf_op jit(solution)/shard_map/ppermute | solution.py:26
  145.2 4.7 %down_product.1 = bf16[8,288,128]{2,1,0:T(8,128)(2,1)} custom-call(s32[1]{0:T(128)} %bitcast.y_ref, bf16[256,8192]{1,0:T(8,128)(2,1)} %bitcast.55, bf16[256,2048]{1,0:T(8,128)(2,1)} %collective-permute-done.x1_ref, bf16[256,1024]{1,0:T(8,128)(2,1)} %collective-permute-done.7.x2a_ref, bf16[256,1024]{1,0:T(8,128)(2,1)} %copy-done.5, ...), custom_call_target="tpu_custom_call" | custom-call | tf_op jit(solution)/shard_map/down_product/pallas_call | solution.py:265
  150.0 21.2 %all_to_all.26 = bf16[8,288,128]{2,1,0:T(8,128)(2,1)S(1)} all-to-all(bf16[8,288,128]{2,1,0:T(8,128)(2,1)} %down_product.1), channel_id=1, replica_groups=mesh['x'=4,'c'=2,'y'=4,'z'=8] {'z'}, dimensions={0} | all-to-all | bytes 1179648 | tf_op jit(solution)/shard_map/all_to_all | solution.py:379
  172.1 5.0 %all-to-all-start.4 = ((bf16[32,32,128]{2,1,0:T(8,128)(2,1)}), bf16[32,32,128]{2,1,0:T(8,128)(2,1)S(1)}, u32[]{:S(2)}, u32[]{:S(2)}) async-start(bf16[32,32,128]{2,1,0:T(8,128)(2,1)} %broadcast_in_dim.25), calls=%async_computation.4 | async-start | bytes 524288 | tf_op jit(solution)/shard_map/all_to_all | solution.py:38
  179.0 9.2 %all-to-all-done.4 = bf16[32,32,128]{2,1,0:T(8,128)(2,1)S(1)} async-done(((bf16[32,32,128]{2,1,0:T(8,128)(2,1)}), bf16[32,32,128]{2,1,0:T(8,128)(2,1)S(1)}, u32[]{:S(2)}, u32[]{:S(2)}) %all-to-all-start.4) | async-done | bytes 262176 | tf_op jit(solution)/shard_map/all_to_all | solution.py:38
  (115 shorter events, 38.6 us)
Async XLA Ops:
  5.0 9.6 %collective-permute-start.6 = (bf16[1024,128]{1,0:T(8,128)(2,1)S(1)}, bf16[1024,128]{1,0:T(8,128)(2,1)S(1)}, u32[]{:S(2)}, u32[]{:S(2)}) collective-permute-start(bf16[1024,128]{1,0:T(8,128)(2,1)S(1)} %get-tuple-element.54), channel_id=1, source_target_pairs={{0,64},{64,128},{128,192},{192,0},{1,65},{65,129},{129,193},{193,1... | collective-permute-start | bytes 786440 | tf_op jit(solution)/shard_map/ppermute | solution.py:26
  6.6 14.9 %collective-permute-start.5 = (bf16[1024,128]{1,0:T(8,128)(2,1)S(1)}, bf16[1024,128]{1,0:T(8,128)(2,1)S(1)}, u32[]{:S(2)}, u32[]{:S(2)}) collective-permute-start(bf16[1024,128]{1,0:T(8,128)(2,1)S(1)} %get-tuple-element.55), channel_id=1, source_target_pairs={{0,128},{64,192},{128,0},{192,64},{1,129},{65,193},{129,1},{193,65... | collective-permute-start | bytes 786440 | tf_op jit(solution)/shard_map/ppermute | solution.py:26
  9.3 12.1 %collective-permute-start.4 = (bf16[1024,128]{1,0:T(8,128)(2,1)S(1)}, bf16[1024,128]{1,0:T(8,128)(2,1)S(1)}, u32[]{:S(2)}, u32[]{:S(2)}) collective-permute-start(bf16[1024,128]{1,0:T(8,128)(2,1)S(1)} %get-tuple-element.56), channel_id=1, source_target_pairs={{0,192},{64,0},{128,64},{192,128},{1,193},{65,1},{129,65},{193,129... | collective-permute-start | bytes 786440 | tf_op jit(solution)/shard_map/ppermute | solution.py:26
  24.9 28.2 %all-to-all-start = ((bf16[32,64,128]{2,1,0:T(8,128)(2,1)}), bf16[32,64,128]{2,1,0:T(8,128)(2,1)S(1)}, u32[]{:S(2)}, u32[]{:S(2)}) async-start(bf16[32,64,128]{2,1,0:T(8,128)(2,1)} %get-tuple-element.21), calls=%async_computation | async-start | bytes 1048576 | tf_op jit(solution)/shard_map/all_to_all | solution.py:38
  40.4 26.9 %collective-permute-start.20 = (bf16[256,128]{1,0:T(8,128)(2,1)S(1)}, bf16[256,128]{1,0:T(8,128)(2,1)S(1)}, u32[]{:S(2)}, u32[]{:S(2)}) collective-permute-start(bf16[256,128]{1,0:T(8,128)(2,1)S(1)} %get-tuple-element.52), channel_id=1, source_target_pairs={{192,0},{193,1},{194,2},{195,3},{196,4},{197,5},{198,6},{199,7},{2... | collective-permute-start | bytes 196616 | tf_op jit(solution)/shard_map/ppermute | solution.py:30
  41.7 27.4 %collective-permute-start.19 = (bf16[256,128]{1,0:T(8,128)(2,1)S(1)}, bf16[256,128]{1,0:T(8,128)(2,1)S(1)}, u32[]{:S(2)}, u32[]{:S(2)}) collective-permute-start(bf16[256,128]{1,0:T(8,128)(2,1)S(1)} %get-tuple-element.52), channel_id=1, source_target_pairs={{128,0},{192,64},{129,1},{193,65},{130,2},{194,66},{131,3},{195,67... | collective-permute-start | bytes 196616 | tf_op jit(solution)/shard_map/ppermute | solution.py:30
  43.0 26.1 %collective-permute-start.18 = (bf16[256,128]{1,0:T(8,128)(2,1)S(1)}, bf16[256,128]{1,0:T(8,128)(2,1)S(1)}, u32[]{:S(2)}, u32[]{:S(2)}) collective-permute-start(bf16[256,128]{1,0:T(8,128)(2,1)S(1)} %get-tuple-element.52), channel_id=1, source_target_pairs={{64,0},{128,64},{192,128},{65,1},{129,65},{193,129},{66,2},{130,66... | collective-permute-start | bytes 196616 | tf_op jit(solution)/shard_map/ppermute | solution.py:30
  56.3 12.8 %collective-permute-start.10 = (f32[384,128]{1,0:T(8,128)}, f32[384,128]{1,0:T(8,128)S(1)}, u32[]{:S(2)}, u32[]{:S(2)}) collective-permute-start(f32[384,128]{1,0:T(8,128)} %get-tuple-element.23), channel_id=1, source_target_pairs={{0,32},{32,0},{1,33},{33,1},{2,34},{34,2},{3,35},{35,3},{4,36},{36... | collective-permute-start | bytes 589832 | tf_op jit(solution)/shard_map/ppermute | solution.py:34
  57.7 17.8 %all-to-all-start.2 = ((bf16[32,32,128]{2,1,0:T(8,128)(2,1)}), bf16[32,32,128]{2,1,0:T(8,128)(2,1)S(1)}, u32[]{:S(2)}, u32[]{:S(2)}) async-start(bf16[32,32,128]{2,1,0:T(8,128)(2,1)} %broadcast_in_dim.11), calls=%async_computation.2 | async-start | bytes 524288 | tf_op jit(solution)/shard_map/all_to_all | solution.py:38
  65.8 71.0 %collective-permute-start.9 = (bf16[256,2048]{1,0:T(8,128)(2,1)}, bf16[256,2048]{1,0:T(8,128)(2,1)}, u32[]{:S(2)}, u32[]{:S(2)}) collective-permute-start(bf16[256,2048]{1,0:T(8,128)(2,1)} %get-tuple-element.40), channel_id=1, source_target_pairs={{0,8},{8,16},{16,24},{24,0},{1,9},{9,17},{17,25},{25,1},{2,10},{10... | collective-permute-start | bytes 3145736 | tf_op jit(solution)/shard_map/ppermute | solution.py:26
  67.3 69.6 %collective-permute-start = (bf16[256,2048]{1,0:T(8,128)(2,1)}, bf16[256,2048]{1,0:T(8,128)(2,1)}, u32[]{:S(2)}, u32[]{:S(2)}) collective-permute-start(bf16[256,2048]{1,0:T(8,128)(2,1)} %get-tuple-element.41), channel_id=1, source_target_pairs={{0,24},{8,0},{16,8},{24,16},{1,25},{9,1},{17,9},{25,17},{2,26},{10... | collective-permute-start | bytes 3145736 | tf_op jit(solution)/shard_map/ppermute | solution.py:26
  75.6 11.8 %collective-permute-start.15 = (bf16[512,128]{1,0:T(8,128)(2,1)S(1)}, bf16[512,128]{1,0:T(8,128)(2,1)S(1)}, u32[]{:S(2)}, u32[]{:S(2)}) collective-permute-start(bf16[512,128]{1,0:T(8,128)(2,1)S(1)} %bitcast.61), channel_id=1, source_target_pairs={{128,0},{192,64},{129,1},{193,65},{130,2},{194,66},{131,3},{195,67... | collective-permute-start | bytes 393224 | tf_op jit(solution)/shard_map/ppermute | solution.py:30
  76.9 10.8 %collective-permute-start.14 = (bf16[768,128]{1,0:T(8,128)(2,1)S(1)}, bf16[768,128]{1,0:T(8,128)(2,1)S(1)}, u32[]{:S(2)}, u32[]{:S(2)}) collective-permute-start(bf16[768,128]{1,0:T(8,128)(2,1)S(1)} %bitcast.60), channel_id=1, source_target_pairs={{64,0},{128,64},{192,128},{65,1},{129,65},{193,129},{66,2},{130,66... | collective-permute-start | bytes 589832 | tf_op jit(solution)/shard_map/ppermute | solution.py:30
  78.2 9.1 %collective-permute-start.16 = (bf16[256,128]{1,0:T(8,128)(2,1)S(1)}, bf16[256,128]{1,0:T(8,128)(2,1)S(1)}, u32[]{:S(2)}, u32[]{:S(2)}) collective-permute-start(bf16[256,128]{1,0:T(8,128)(2,1)S(1)} %bitcast.62), channel_id=1, source_target_pairs={{192,0},{193,1},{194,2},{195,3},{196,4},{197,5},{198,6},{199,7},{2... | collective-permute-start | bytes 196616 | tf_op jit(solution)/shard_map/ppermute | solution.py:30
  87.4 9.9 %collective-permute-start.13 = (bf16[512,128]{1,0:T(8,128)(2,1)S(1)}, bf16[512,128]{1,0:T(8,128)(2,1)S(1)}, u32[]{:S(2)}, u32[]{:S(2)}) collective-permute-start(bf16[512,128]{1,0:T(8,128)(2,1)S(1)} %pad_maximum_fusion.8.a_ref), channel_id=1, source_target_pairs={{0,64},{64,128},{128,192},{192,0},{1,65},{65,129},{129,193},{193,1... | collective-permute-start | bytes 393224 | tf_op jit(solution)/shard_map/ppermute | solution.py:26
  87.6 12.0 %collective-permute-start.12 = (bf16[512,128]{1,0:T(8,128)(2,1)S(1)}, bf16[512,128]{1,0:T(8,128)(2,1)S(1)}, u32[]{:S(2)}, u32[]{:S(2)}) collective-permute-start(bf16[512,128]{1,0:T(8,128)(2,1)S(1)} %pad_maximum_fusion.8.a_ref), channel_id=1, source_target_pairs={{0,128},{64,192},{128,0},{192,64},{1,129},{65,193},{129,1},{193,65... | collective-permute-start | bytes 393224 | tf_op jit(solution)/shard_map/ppermute | solution.py:26
  90.8 10.3 %collective-permute-start.11 = (bf16[512,128]{1,0:T(8,128)(2,1)S(1)}, bf16[512,128]{1,0:T(8,128)(2,1)S(1)}, u32[]{:S(2)}, u32[]{:S(2)}) collective-permute-start(bf16[512,128]{1,0:T(8,128)(2,1)S(1)} %pad_maximum_fusion.8.a_ref), channel_id=1, source_target_pairs={{0,192},{64,0},{128,64},{192,128},{1,193},{65,1},{129,65},{193,129... | collective-permute-start | bytes 393224 | tf_op jit(solution)/shard_map/ppermute | solution.py:26
  97.3 31.2 %collective-permute-start.17 = (bf16[2560,128]{1,0:T(8,128)(2,1)S(1)}, bf16[2560,128]{1,0:T(8,128)(2,1)}, u32[]{:S(2)}, u32[]{:S(2)}) collective-permute-start(bf16[2560,128]{1,0:T(8,128)(2,1)S(1)} %pad_maximum_fusion.own_ref), channel_id=1, source_target_pairs={{0,32},{32,0},{1,33},{33,1},{2,34},{34,2},{3,35},{35,3},{4,36},{36... | collective-permute-start | bytes 1966088 | tf_op jit(solution)/shard_map/ppermute | solution.py:34
  99.6 35.7 %collective-permute-start.8 = (bf16[256,1024]{1,0:T(8,128)(2,1)}, bf16[256,1024]{1,0:T(8,128)(2,1)S(1)}, u32[]{:S(2)}, u32[]{:S(2)}) collective-permute-start(bf16[256,1024]{1,0:T(8,128)(2,1)} %get-tuple-element.42), channel_id=1, source_target_pairs={{0,16},{8,24},{16,0},{24,8},{1,17},{9,25},{17,1},{25,9},{2,18},{10... | collective-permute-start | bytes 1572872 | tf_op jit(solution)/shard_map/ppermute | solution.py:26
  101.1 35.7 %collective-permute-start.7 = (bf16[256,1024]{1,0:T(8,128)(2,1)}, bf16[256,1024]{1,0:T(8,128)(2,1)}, u32[]{:S(2)}, u32[]{:S(2)}) collective-permute-start(bf16[256,1024]{1,0:T(8,128)(2,1)} %get-tuple-element.43), channel_id=1, source_target_pairs={{0,16},{8,24},{16,0},{24,8},{1,17},{9,25},{17,1},{25,9},{2,18},{10... | collective-permute-start | bytes 1572872 | tf_op jit(solution)/shard_map/ppermute | solution.py:26
  134.0 6.6 %collective-permute-start.22 = (bf16[512,128]{1,0:T(8,128)(2,1)}, bf16[512,128]{1,0:T(8,128)(2,1)S(1)}, u32[]{:S(2)}, u32[]{:S(2)}) collective-permute-start(bf16[512,128]{1,0:T(8,128)(2,1)} %get-tuple-element.30), channel_id=1, source_target_pairs={{0,24},{8,0},{16,8},{24,16},{1,25},{9,1},{17,9},{25,17},{2,26},{10... | collective-permute-start | bytes 393224 | tf_op jit(solution)/shard_map/ppermute | solution.py:26
  135.3 7.8 %collective-permute-start.23 = (bf16[512,128]{1,0:T(8,128)(2,1)}, bf16[512,128]{1,0:T(8,128)(2,1)S(1)}, u32[]{:S(2)}, u32[]{:S(2)}) collective-permute-start(bf16[512,128]{1,0:T(8,128)(2,1)} %get-tuple-element.31), channel_id=1, source_target_pairs={{0,16},{8,24},{16,0},{24,8},{1,17},{9,25},{17,1},{25,9},{2,18},{10... | collective-permute-start | bytes 393224 | tf_op jit(solution)/shard_map/ppermute | solution.py:26
  136.8 7.8 %collective-permute-start.24 = (bf16[512,128]{1,0:T(8,128)(2,1)}, bf16[512,128]{1,0:T(8,128)(2,1)S(1)}, u32[]{:S(2)}, u32[]{:S(2)}) collective-permute-start(bf16[512,128]{1,0:T(8,128)(2,1)} %get-tuple-element.32), channel_id=1, source_target_pairs={{0,8},{8,16},{16,24},{24,0},{1,9},{9,17},{17,25},{25,1},{2,10},{10... | collective-permute-start | bytes 393224 | tf_op jit(solution)/shard_map/ppermute | solution.py:26
  172.1 16.2 %all-to-all-start.4 = ((bf16[32,32,128]{2,1,0:T(8,128)(2,1)}), bf16[32,32,128]{2,1,0:T(8,128)(2,1)S(1)}, u32[]{:S(2)}, u32[]{:S(2)}) async-start(bf16[32,32,128]{2,1,0:T(8,128)(2,1)} %broadcast_in_dim.25), calls=%async_computation.4 | async-start | bytes 524288 | tf_op jit(solution)/shard_map/all_to_all | solution.py:38
  (26 other events, 265.4 us)

commit v7 on v6

--- a/solution.py
+++ b/solution.py
@@ -113,7 +113,9 @@
         rows = total[32 * m : 32 * m + 32]
         part_ref[32 * m : 32 * m + 32, :] = rows - jnp.where(m == my_stage, target, 0.0)
     part_ref[256:384, :] = square
-    cross_ref[...] = jnp.sum(got_ref[:, 32:64, :].astype(F32), axis=0).astype(BF16)
+    cross = jnp.sum(got_ref[:, 32:64, :].astype(F32), axis=0).astype(BF16)
+    for d in range(DP):
+        cross_ref[d] = cross
 
 
 def gram_kernel(where_ref, a_ref, b_ref, c_ref, d_ref, mask_ref, sent_ref, residual_ref):
@@ -304,12 +306,16 @@
     turn = [(a * NY + b, b * NY + a) for a in range(NX) for b in range(NY)]
     piece = lax.ppermute(piece, ("x", "y"), turn)
 
-    blocks = representation[0].reshape(tok, NX, NZ, NC, 128).transpose(3, 1, 2, 0, 4)
-    blocks = blocks.reshape(NC, NX, NZ * tok, 128)
+    columns = representation[0].reshape(tok, NX * NZ, NC, 128)
+
+    def half_of(core):
+        taken = lax.dynamic_index_in_dim(columns, core, 2, keepdims=False)
+        return taken.transpose(1, 0, 2).reshape(NX, NZ * tok, 128)
+
     down_rows = rows_at(down_map, my_dp * share, share)
-    swapped = swap_c(at(blocks, 1 - my_c))
+    swapped = swap_c(half_of(1 - my_c))
     partner = swap_c(down_rows)
-    pair = jnp.concatenate([at(blocks, my_c), swapped], axis=1)
+    pair = jnp.concatenate([half_of(my_c), swapped], axis=1)
     gots = []
     for k in range(1, NX):
         sent = jnp.concatenate([at(pair, (my_x - k) % NX), down_rows, partner], axis=0)
@@ -320,8 +326,10 @@
     def cut(index, k, lo, size):
         return lax.dynamic_slice_in_dim(saved, ((index - k) % NY) * wide + lo, size, 1)
 
-    x1 = shift(cut(my_y, 1, 0, wide), "y", -1)
-    x3 = shift(cut(my_y, 3, 0, wide), "y", -3)
+    x1 = cut(my_y, 1, 0, wide)
+    x3 = cut(my_y, 3, 0, wide)
+    x1 = shift(x1, "y", -1)
+    x3 = shift(x3, "y", -3)
 
     up_rows = rows_at(up_map, my_dp * share, share)
     sent, factors, rep = local_call(
@@ -343,10 +351,10 @@
     got = exchange_dp(sent)
     part, cross_rows, _ = local_call(
         heads_kernel,
-        [((384, rank), F32), ((32, rank), BF16), ((1024, rank), BF16)],
+        [((384, rank), F32), ((DP, 32, rank), BF16), ((1024, rank), BF16)],
         where, got, rep, head_targets[0],
     )
-    got = exchange_dp(jnp.broadcast_to(cross_rows[None], (DP, 32, rank)))
+    got = exchange_dp(cross_rows)
     cross = got.reshape(-1, rank)
     kept = [cross]
     for k in range(1, NX):

time: 190 us -> 188 us (0.989)
  transfers between devices with their start and end apart: 28 -> 28, of which waited for: 11 -> 11; matrix products, arithmetic and copies ran while one was open for 9% -> 9% of each run, Pallas kernels for 5% -> 6%
where the time goes in v7:
time: 188 us; the launch traced here: 187 us
  waiting for transfers between devices  52.6 us (28%)
  starting transfers between devices  49.4 us (26%)
  blocking collectives  43 us (23%)
  Pallas kernels  17.8 us (9%)
  local copies, waits for them, and re-layouts  16.2 us (9%)
  matrix products  5.03 us (3%)
  other arithmetic  2.26 us (1%)
    all_to_all x3, waiting for transfers between devices, exchange_dp(): return lax.all_to_all(blocks, ('y', 'z'), 0, 0, tiled=True)  23.3 us
    all_to_all x1, blocking collectives, exchange_dp(): return lax.all_to_all(blocks, ('y', 'z'), 0, 0, tiled=True)  21.9 us
    all_to_all x3, starting transfers between devices, exchange_dp(): return lax.all_to_all(blocks, ('y', 'z'), 0, 0, tiled=True)  21.2 us
    ppermute x13, waiting for transfers between devices, shift(): lax.ppermute(value, axis, [(src, (src + steps) % count) for src in range(...  21.2 us
    all_to_all x1, blocking collectives, stages(): got = lax.all_to_all(part_down, 'z', 0, 0, tiled=True)  21.1 us
    ppermute x13, starting transfers between devices, shift(): lax.ppermute(value, axis, [(src, (src + steps) % count) for src in range(...  19.1 us
    pallas_call x4, Pallas kernels, local_call(): pl.pallas_call(kernel, out_shape=tuple((jax.ShapeDtypeStruct(shape, dtype...  13 us
    ppermute x6, starting transfers between devices, from_later(): lax.ppermute(value, 'x', [(src, src - steps) for src in range(steps, NX)])  7.74 us
  transfers between devices with their start and end apart: 28, of which 11 were waited for; matrix products, arithmetic and copies ran while one was open for 9% of the time, Pallas kernels for 6%

profile of v7, /device:TPU:32, one launch (start us, length us, event | category | flops | bytes accessed | tf_op | source)
XLA Modules:
  0.0 187.4 jit_solution(17833100952729684580)
XLA Ops:
  7.6 2.7 %collective-permute-start.5 = (bf16[1024,128]{1,0:T(8,128)(2,1)S(1)}, bf16[1024,128]{1,0:T(8,128)(2,1)S(1)}, u32[]{:S(2)}, u32[]{:S(2)}) collective-permute-start(bf16[1024,128]{1,0:T(8,128)(2,1)S(1)} %get-tuple-element.55), channel_id=1, source_target_pairs={{0,128},{64,192},{128,0},{192,64},{1,129},{65,193},{129,1},{193,65... | collective-permute-start | bytes 786440 | tf_op jit(solution)/shard_map/ppermute | solution.py:26
  15.7 6.8 %collective-permute-done.5.got2_ref = bf16[1024,128]{1,0:T(8,128)(2,1)S(1)} collective-permute-done((bf16[1024,128]{1,0:T(8,128)(2,1)S(1)}, bf16[1024,128]{1,0:T(8,128)(2,1)S(1)}, u32[]{:S(2)}, u32[]{:S(2)}) %collective-permute-start.5) | collective-permute-done | bytes 262176 | tf_op jit(solution)/shard_map/ppermute | solution.py:26
  23.2 2.7 %shard_map.94 = (bf16[32,64,128]{2,1,0:T(8,128)(2,1)}, bf16[8,256,128]{2,1,0:T(8,128)(2,1)}, bf16[8,256,128]{2,1,0:T(8,128)(2,1)}) custom-call(s32[3]{0:T(128)} %pad_add_fusion.where_ref, bf16[32,128]{1,0:T(8,128)(2,1)} %copy-done.20, bf16[256,128]{1,0:T(8,128)(2,1)} %heads_ref.1, bf16[256,128]{1,0:T(8,128)(2,1)} %dynamic-slice_bitcast_fusion.1.up_ref, ...), custom_call_target="tpu_custom_call" | custom-call | tf_op jit(solution)/shard_map/pallas_call | solution.py:58
  25.9 11.3 %all-to-all-start = ((bf16[32,64,128]{2,1,0:T(8,128)(2,1)}), bf16[32,64,128]{2,1,0:T(8,128)(2,1)S(1)}, u32[]{:S(2)}, u32[]{:S(2)}) async-start(bf16[32,64,128]{2,1,0:T(8,128)(2,1)} %get-tuple-element.21), calls=%async_computation | async-start | bytes 1048576 | tf_op jit(solution)/shard_map/all_to_all | solution.py:38
  37.3 4.1 %multiply_convert_fusion = (bf16[256,128]{1,0:T(8,128)(2,1)S(1)}, bf16[256,128]{1,0:T(8,128)(2,1)}) fusion(bf16[256,8192]{1,0:T(8,128)(2,1)} %bitcast.58, bf16[8192,128]{1,0:T(8,128)(2,1)S(1)} %bitcast.57), kind=kOutput, calls=%fused_computation.29 | convolution fusion | flops 537198592 | bytes 6422528 | tf_op jit(solution)/shard_map/dot_general | solution.py:344
  45.3 8.9 %all-to-all-done.got_ref = bf16[32,64,128]{2,1,0:T(8,128)(2,1)S(1)} async-done(((bf16[32,64,128]{2,1,0:T(8,128)(2,1)}), bf16[32,64,128]{2,1,0:T(8,128)(2,1)S(1)}, u32[]{:S(2)}, u32[]{:S(2)}) %all-to-all-start) | async-done | bytes 524320 | tf_op jit(solution)/shard_map/all_to_all | solution.py:38
  55.0 2.4 %shard_map.95 = (f32[384,128]{1,0:T(8,128)}, bf16[32,32,128]{2,1,0:T(8,128)(2,1)}, bf16[1024,128]{1,0:T(8,128)(2,1)}) custom-call(s32[3]{0:T(128)} %pad_add_fusion.where_ref, bf16[32,64,128]{2,1,0:T(8,128)(2,1)} %copy-done.2, bf16[8,256,128]{2,1,0:T(8,128)(2,1)} %get-tuple-element.22.rep_ref, bf16[32,128]{1,0:T(8,128)(2,1)} %bitcast.73), custom_call_target="tpu_custom_call" | custom-call | tf_op jit(solution)/shard_map/pallas_call | solution.py:58
  57.4 4.9 %all-to-all-start.2 = ((bf16[32,32,128]{2,1,0:T(8,128)(2,1)}), bf16[32,32,128]{2,1,0:T(8,128)(2,1)S(1)}, u32[]{:S(2)}, u32[]{:S(2)}) async-start(bf16[32,32,128]{2,1,0:T(8,128)(2,1)} %get-tuple-element.27), calls=%async_computation.2 | async-start | bytes 524288 | tf_op jit(solution)/shard_map/all_to_all | solution.py:38
  62.4 3.2 %constant_dynamic-slice_fusion = (bf16[256,2048]{1,0:T(8,128)(2,1)}, bf16[256,2048]{1,0:T(8,128)(2,1)}) fusion(bf16[256,8192]{1,0:T(8,128)(2,1)} %bitcast.59, s32[]{:T(128)S(6)} %select_n.85, s32[]{:T(128)S(6)} %select_n.69), kind=kLoop, calls=%fused_computation.41 | loop fusion | bytes 4194312 | tf_op jit(solution)/shard_map/dynamic_slice | solution.py:327
  68.9 4.9 %all-to-all-done.2 = bf16[32,32,128]{2,1,0:T(8,128)(2,1)S(1)} async-done(((bf16[32,32,128]{2,1,0:T(8,128)(2,1)}), bf16[32,32,128]{2,1,0:T(8,128)(2,1)S(1)}, u32[]{:S(2)}, u32[]{:S(2)}) %all-to-all-start.2) | async-done | bytes 262176 | tf_op jit(solution)/shard_map/all_to_all | solution.py:38
  77.8 7.5 %collective-permute-done.16 = bf16[256,128]{1,0:T(8,128)(2,1)S(1)} collective-permute-done((bf16[256,128]{1,0:T(8,128)(2,1)S(1)}, bf16[256,128]{1,0:T(8,128)(2,1)S(1)}, u32[]{:S(2)}, u32[]{:S(2)}) %collective-permute-start.16) | collective-permute-done | bytes 65568 | tf_op jit(solution)/shard_map/ppermute | solution.py:30
  86.9 2.1 %collective-permute-start.11 = (bf16[512,128]{1,0:T(8,128)(2,1)S(1)}, bf16[512,128]{1,0:T(8,128)(2,1)S(1)}, u32[]{:S(2)}, u32[]{:S(2)}) collective-permute-start(bf16[512,128]{1,0:T(8,128)(2,1)S(1)} %pad_maximum_fusion.8.a_ref), channel_id=1, source_target_pairs={{0,192},{64,0},{128,64},{192,128},{1,193},{65,1},{129,65},{193,129... | collective-permute-start | bytes 393224 | tf_op jit(solution)/shard_map/ppermute | solution.py:26
  89.0 6.3 %collective-permute-done.13.d_ref = bf16[512,128]{1,0:T(8,128)(2,1)S(1)} collective-permute-done((bf16[512,128]{1,0:T(8,128)(2,1)S(1)}, bf16[512,128]{1,0:T(8,128)(2,1)S(1)}, u32[]{:S(2)}, u32[]{:S(2)}) %collective-permute-start.13) | collective-permute-done | bytes 131104 | tf_op jit(solution)/shard_map/ppermute | solution.py:26
  95.3 2.3 %constant_dynamic-slice_fusion.1 = (bf16[256,1024]{1,0:T(8,128)(2,1)}, bf16[256,1024]{1,0:T(8,128)(2,1)}) fusion(bf16[256,8192]{1,0:T(8,128)(2,1)} %bitcast.60, s32[]{:T(128)S(6)} %select_n.83, s32[]{:T(128)S(6)} %select_n.82), kind=kLoop, calls=%fused_computation.42 | loop fusion | bytes 2097160 | tf_op jit(solution)/shard_map/dynamic_slice | solution.py:327
  99.1 2.2 %collective-permute-start.7 = (bf16[256,1024]{1,0:T(8,128)(2,1)}, bf16[256,1024]{1,0:T(8,128)(2,1)}, u32[]{:S(2)}, u32[]{:S(2)}) collective-permute-start(bf16[256,1024]{1,0:T(8,128)(2,1)} %get-tuple-element.43), channel_id=1, source_target_pairs={{0,16},{8,24},{16,0},{24,8},{1,17},{9,25},{17,1},{25,9},{2,18},{10... | collective-permute-start | bytes 1572872 | tf_op jit(solution)/shard_map/ppermute | solution.py:26
  102.2 2.4 %shard_map.96 = (bf16[32,16,128]{2,1,0:T(8,128)(2,1)}, bf16[256,128]{1,0:T(8,128)(2,1)}) custom-call(s32[3]{0:T(128)} %pad_add_fusion.where_ref, bf16[512,128]{1,0:T(8,128)(2,1)} %copy-done.7, bf16[512,128]{1,0:T(8,128)(2,1)} %copy-done.19, bf16[512,128]{1,0:T(8,128)(2,1)} %copy-done.18, bf16[512,128]{1,0:T(8,128)(2,1)} %copy-done.17, f32[128,128]{1,0:T(8,128)} %fusion.9.mask_ref), custom_call_target="tpu_custom_call" | custom-call | tf_op jit(solution)/shard_map/pallas_call | solution.py:58
  104.6 21.9 %all_to_all.25.got_ref = bf16[32,16,128]{2,1,0:T(8,128)(2,1)} all-to-all(bf16[32,16,128]{2,1,0:T(8,128)(2,1)} %get-tuple-element.24), channel_id=1, replica_groups=mesh['x'=4,'c'=2,'y'=4,'z'=8] {'y','z'}, dimensions={0} | all-to-all | bytes 262144 | tf_op jit(solution)/shard_map/all_to_all | solution.py:38
  126.5 5.5 %shard_map.97 = (bf16[256,128]{1,0:T(8,128)(2,1)}, bf16[512,128]{1,0:T(8,128)(2,1)}, bf16[512,128]{1,0:T(8,128)(2,1)}, bf16[512,128]{1,0:T(8,128)(2,1)}, bf16[25...) custom-call(s32[3]{0:T(128)} %pad_add_fusion.where_ref, bf16[32,16,128]{2,1,0:T(8,128)(2,1)} %all_to_all.25.got_ref, ...), custom_call_target="tpu_custom_call" | custom-call | tf_op jit(solution)/shard_map/pallas_call | solution.py:58
  134.9 3.7 %collective-permute-done.22.got1_ref = bf16[512,128]{1,0:T(8,128)(2,1)S(1)} collective-permute-done((bf16[512,128]{1,0:T(8,128)(2,1)}, bf16[512,128]{1,0:T(8,128)(2,1)S(1)}, u32[]{:S(2)}, u32[]{:S(2)}) %collective-permute-start.22) | collective-permute-done | bytes 131104 | tf_op jit(solution)/shard_map/ppermute | solution.py:26
  138.6 2.6 %collective-permute-done.23.got2_ref = bf16[512,128]{1,0:T(8,128)(2,1)S(1)} collective-permute-done((bf16[512,128]{1,0:T(8,128)(2,1)}, bf16[512,128]{1,0:T(8,128)(2,1)S(1)}, u32[]{:S(2)}, u32[]{:S(2)}) %collective-permute-start.23) | collective-permute-done | bytes 131104 | tf_op jit(solution)/shard_map/ppermute | solution.py:26
  143.2 4.8 %down_product.1 = bf16[8,288,128]{2,1,0:T(8,128)(2,1)} custom-call(s32[1]{0:T(128)} %bitcast.y_ref, bf16[256,8192]{1,0:T(8,128)(2,1)} %bitcast.61, bf16[256,2048]{1,0:T(8,128)(2,1)} %collective-permute-done.x1_ref, bf16[256,1024]{1,0:T(8,128)(2,1)} %collective-permute-done.7.x2a_ref, bf16[256,1024]{1,0:T(8,128)(2,1)} %copy-done.5, ...), custom_call_target="tpu_custom_call" | custom-call | tf_op jit(solution)/shard_map/down_product/pallas_call | solution.py:267
  148.0 21.1 %all_to_all.26 = bf16[8,288,128]{2,1,0:T(8,128)(2,1)S(1)} all-to-all(bf16[8,288,128]{2,1,0:T(8,128)(2,1)} %down_product.1), channel_id=1, replica_groups=mesh['x'=4,'c'=2,'y'=4,'z'=8] {'z'}, dimensions={0} | all-to-all | bytes 1179648 | tf_op jit(solution)/shard_map/all_to_all | solution.py:387
  169.9 5.0 %all-to-all-start.4 = ((bf16[32,32,128]{2,1,0:T(8,128)(2,1)}), bf16[32,32,128]{2,1,0:T(8,128)(2,1)S(1)}, u32[]{:S(2)}, u32[]{:S(2)}) async-start(bf16[32,32,128]{2,1,0:T(8,128)(2,1)} %broadcast_in_dim.18), calls=%async_computation.4 | async-start | bytes 524288 | tf_op jit(solution)/shard_map/all_to_all | solution.py:38
  176.8 9.6 %all-to-all-done.4 = bf16[32,32,128]{2,1,0:T(8,128)(2,1)S(1)} async-done(((bf16[32,32,128]{2,1,0:T(8,128)(2,1)}), bf16[32,32,128]{2,1,0:T(8,128)(2,1)S(1)}, u32[]{:S(2)}, u32[]{:S(2)}) %all-to-all-start.4) | async-done | bytes 262176 | tf_op jit(solution)/shard_map/all_to_all | solution.py:38
  (115 shorter events, 37.6 us)
Async XLA Ops:
  6.0 9.6 %collective-permute-start.6 = (bf16[1024,128]{1,0:T(8,128)(2,1)S(1)}, bf16[1024,128]{1,0:T(8,128)(2,1)S(1)}, u32[]{:S(2)}, u32[]{:S(2)}) collective-permute-start(bf16[1024,128]{1,0:T(8,128)(2,1)S(1)} %get-tuple-element.54), channel_id=1, source_target_pairs={{0,64},{64,128},{128,192},{192,0},{1,65},{65,129},{129,193},{193,1... | collective-permute-start | bytes 786440 | tf_op jit(solution)/shard_map/ppermute | solution.py:26
  7.6 14.9 %collective-permute-start.5 = (bf16[1024,128]{1,0:T(8,128)(2,1)S(1)}, bf16[1024,128]{1,0:T(8,128)(2,1)S(1)}, u32[]{:S(2)}, u32[]{:S(2)}) collective-permute-start(bf16[1024,128]{1,0:T(8,128)(2,1)S(1)} %get-tuple-element.55), channel_id=1, source_target_pairs={{0,128},{64,192},{128,0},{192,64},{1,129},{65,193},{129,1},{193,65... | collective-permute-start | bytes 786440 | tf_op jit(solution)/shard_map/ppermute | solution.py:26
  10.3 12.1 %collective-permute-start.4 = (bf16[1024,128]{1,0:T(8,128)(2,1)S(1)}, bf16[1024,128]{1,0:T(8,128)(2,1)S(1)}, u32[]{:S(2)}, u32[]{:S(2)}) collective-permute-start(bf16[1024,128]{1,0:T(8,128)(2,1)S(1)} %get-tuple-element.56), channel_id=1, source_target_pairs={{0,192},{64,0},{128,64},{192,128},{1,193},{65,1},{129,65},{193,129... | collective-permute-start | bytes 786440 | tf_op jit(solution)/shard_map/ppermute | solution.py:26
  25.9 28.2 %all-to-all-start = ((bf16[32,64,128]{2,1,0:T(8,128)(2,1)}), bf16[32,64,128]{2,1,0:T(8,128)(2,1)S(1)}, u32[]{:S(2)}, u32[]{:S(2)}) async-start(bf16[32,64,128]{2,1,0:T(8,128)(2,1)} %get-tuple-element.21), calls=%async_computation | async-start | bytes 1048576 | tf_op jit(solution)/shard_map/all_to_all | solution.py:38
  41.4 25.7 %collective-permute-start.20 = (bf16[256,128]{1,0:T(8,128)(2,1)S(1)}, bf16[256,128]{1,0:T(8,128)(2,1)S(1)}, u32[]{:S(2)}, u32[]{:S(2)}) collective-permute-start(bf16[256,128]{1,0:T(8,128)(2,1)S(1)} %get-tuple-element.52), channel_id=1, source_target_pairs={{192,0},{193,1},{194,2},{195,3},{196,4},{197,5},{198,6},{199,7},{2... | collective-permute-start | bytes 196616 | tf_op jit(solution)/shard_map/ppermute | solution.py:30
  42.7 26.1 %collective-permute-start.19 = (bf16[256,128]{1,0:T(8,128)(2,1)S(1)}, bf16[256,128]{1,0:T(8,128)(2,1)S(1)}, u32[]{:S(2)}, u32[]{:S(2)}) collective-permute-start(bf16[256,128]{1,0:T(8,128)(2,1)S(1)} %get-tuple-element.52), channel_id=1, source_target_pairs={{128,0},{192,64},{129,1},{193,65},{130,2},{194,66},{131,3},{195,67... | collective-permute-start | bytes 196616 | tf_op jit(solution)/shard_map/ppermute | solution.py:30
  44.0 24.8 %collective-permute-start.18 = (bf16[256,128]{1,0:T(8,128)(2,1)S(1)}, bf16[256,128]{1,0:T(8,128)(2,1)S(1)}, u32[]{:S(2)}, u32[]{:S(2)}) collective-permute-start(bf16[256,128]{1,0:T(8,128)(2,1)S(1)} %get-tuple-element.52), channel_id=1, source_target_pairs={{64,0},{128,64},{192,128},{65,1},{129,65},{193,129},{66,2},{130,66... | collective-permute-start | bytes 196616 | tf_op jit(solution)/shard_map/ppermute | solution.py:30
  57.4 16.4 %all-to-all-start.2 = ((bf16[32,32,128]{2,1,0:T(8,128)(2,1)}), bf16[32,32,128]{2,1,0:T(8,128)(2,1)S(1)}, u32[]{:S(2)}, u32[]{:S(2)}) async-start(bf16[32,32,128]{2,1,0:T(8,128)(2,1)} %get-tuple-element.27), calls=%async_computation.2 | async-start | bytes 524288 | tf_op jit(solution)/shard_map/all_to_all | solution.py:38
  62.3 6.6 %collective-permute-start.10 = (f32[384,128]{1,0:T(8,128)}, f32[384,128]{1,0:T(8,128)S(1)}, u32[]{:S(2)}, u32[]{:S(2)}) collective-permute-start(f32[384,128]{1,0:T(8,128)} %get-tuple-element.23), channel_id=1, source_target_pairs={{0,32},{32,0},{1,33},{33,1},{2,34},{34,2},{3,35},{35,3},{4,36},{36... | collective-permute-start | bytes 589832 | tf_op jit(solution)/shard_map/ppermute | solution.py:34
  65.6 69.3 %collective-permute-start.9 = (bf16[256,2048]{1,0:T(8,128)(2,1)}, bf16[256,2048]{1,0:T(8,128)(2,1)}, u32[]{:S(2)}, u32[]{:S(2)}) collective-permute-start(bf16[256,2048]{1,0:T(8,128)(2,1)} %get-tuple-element.40), channel_id=1, source_target_pairs={{0,8},{8,16},{16,24},{24,0},{1,9},{9,17},{17,25},{25,1},{2,10},{10... | collective-permute-start | bytes 3145736 | tf_op jit(solution)/shard_map/ppermute | solution.py:26
  67.0 67.8 %collective-permute-start = (bf16[256,2048]{1,0:T(8,128)(2,1)}, bf16[256,2048]{1,0:T(8,128)(2,1)}, u32[]{:S(2)}, u32[]{:S(2)}) collective-permute-start(bf16[256,2048]{1,0:T(8,128)(2,1)} %get-tuple-element.41), channel_id=1, source_target_pairs={{0,24},{8,0},{16,8},{24,16},{1,25},{9,1},{17,9},{25,17},{2,26},{10... | collective-permute-start | bytes 3145736 | tf_op jit(solution)/shard_map/ppermute | solution.py:26
  73.8 11.5 %collective-permute-start.15 = (bf16[512,128]{1,0:T(8,128)(2,1)S(1)}, bf16[512,128]{1,0:T(8,128)(2,1)S(1)}, u32[]{:S(2)}, u32[]{:S(2)}) collective-permute-start(bf16[512,128]{1,0:T(8,128)(2,1)S(1)} %bitcast.67), channel_id=1, source_target_pairs={{128,0},{192,64},{129,1},{193,65},{130,2},{194,66},{131,3},{195,67... | collective-permute-start | bytes 393224 | tf_op jit(solution)/shard_map/ppermute | solution.py:30
  75.1 10.2 %collective-permute-start.14 = (bf16[768,128]{1,0:T(8,128)(2,1)S(1)}, bf16[768,128]{1,0:T(8,128)(2,1)S(1)}, u32[]{:S(2)}, u32[]{:S(2)}) collective-permute-start(bf16[768,128]{1,0:T(8,128)(2,1)S(1)} %bitcast.66), channel_id=1, source_target_pairs={{64,0},{128,64},{192,128},{65,1},{129,65},{193,129},{66,2},{130,66... | collective-permute-start | bytes 589832 | tf_op jit(solution)/shard_map/ppermute | solution.py:30
  76.5 8.9 %collective-permute-start.16 = (bf16[256,128]{1,0:T(8,128)(2,1)S(1)}, bf16[256,128]{1,0:T(8,128)(2,1)S(1)}, u32[]{:S(2)}, u32[]{:S(2)}) collective-permute-start(bf16[256,128]{1,0:T(8,128)(2,1)S(1)} %bitcast.68), channel_id=1, source_target_pairs={{192,0},{193,1},{194,2},{195,3},{196,4},{197,5},{198,6},{199,7},{2... | collective-permute-start | bytes 196616 | tf_op jit(solution)/shard_map/ppermute | solution.py:30
  85.3 9.9 %collective-permute-start.13 = (bf16[512,128]{1,0:T(8,128)(2,1)S(1)}, bf16[512,128]{1,0:T(8,128)(2,1)S(1)}, u32[]{:S(2)}, u32[]{:S(2)}) collective-permute-start(bf16[512,128]{1,0:T(8,128)(2,1)S(1)} %pad_maximum_fusion.8.a_ref), channel_id=1, source_target_pairs={{0,64},{64,128},{128,192},{192,0},{1,65},{65,129},{129,193},{193,1... | collective-permute-start | bytes 393224 | tf_op jit(solution)/shard_map/ppermute | solution.py:26
  85.4 12.3 %collective-permute-start.12 = (bf16[512,128]{1,0:T(8,128)(2,1)S(1)}, bf16[512,128]{1,0:T(8,128)(2,1)S(1)}, u32[]{:S(2)}, u32[]{:S(2)}) collective-permute-start(bf16[512,128]{1,0:T(8,128)(2,1)S(1)} %pad_maximum_fusion.8.a_ref), channel_id=1, source_target_pairs={{0,128},{64,192},{128,0},{192,64},{1,129},{65,193},{129,1},{193,65... | collective-permute-start | bytes 393224 | tf_op jit(solution)/shard_map/ppermute | solution.py:26
  86.9 12.2 %collective-permute-start.11 = (bf16[512,128]{1,0:T(8,128)(2,1)S(1)}, bf16[512,128]{1,0:T(8,128)(2,1)S(1)}, u32[]{:S(2)}, u32[]{:S(2)}) collective-permute-start(bf16[512,128]{1,0:T(8,128)(2,1)S(1)} %pad_maximum_fusion.8.a_ref), channel_id=1, source_target_pairs={{0,192},{64,0},{128,64},{192,128},{1,193},{65,1},{129,65},{193,129... | collective-permute-start | bytes 393224 | tf_op jit(solution)/shard_map/ppermute | solution.py:26
  95.3 31.2 %collective-permute-start.17 = (bf16[2560,128]{1,0:T(8,128)(2,1)S(1)}, bf16[2560,128]{1,0:T(8,128)(2,1)}, u32[]{:S(2)}, u32[]{:S(2)}) collective-permute-start(bf16[2560,128]{1,0:T(8,128)(2,1)S(1)} %pad_maximum_fusion.own_ref), channel_id=1, source_target_pairs={{0,32},{32,0},{1,33},{33,1},{2,34},{34,2},{3,35},{35,3},{4,36},{36... | collective-permute-start | bytes 1966088 | tf_op jit(solution)/shard_map/ppermute | solution.py:34
  97.6 35.7 %collective-permute-start.8 = (bf16[256,1024]{1,0:T(8,128)(2,1)}, bf16[256,1024]{1,0:T(8,128)(2,1)S(1)}, u32[]{:S(2)}, u32[]{:S(2)}) collective-permute-start(bf16[256,1024]{1,0:T(8,128)(2,1)} %get-tuple-element.42), channel_id=1, source_target_pairs={{0,16},{8,24},{16,0},{24,8},{1,17},{9,25},{17,1},{25,9},{2,18},{10... | collective-permute-start | bytes 1572872 | tf_op jit(solution)/shard_map/ppermute | solution.py:26
  99.1 35.6 %collective-permute-start.7 = (bf16[256,1024]{1,0:T(8,128)(2,1)}, bf16[256,1024]{1,0:T(8,128)(2,1)}, u32[]{:S(2)}, u32[]{:S(2)}) collective-permute-start(bf16[256,1024]{1,0:T(8,128)(2,1)} %get-tuple-element.43), channel_id=1, source_target_pairs={{0,16},{8,24},{16,0},{24,8},{1,17},{9,25},{17,1},{25,9},{2,18},{10... | collective-permute-start | bytes 1572872 | tf_op jit(solution)/shard_map/ppermute | solution.py:26
  132.0 6.6 %collective-permute-start.22 = (bf16[512,128]{1,0:T(8,128)(2,1)}, bf16[512,128]{1,0:T(8,128)(2,1)S(1)}, u32[]{:S(2)}, u32[]{:S(2)}) collective-permute-start(bf16[512,128]{1,0:T(8,128)(2,1)} %get-tuple-element.30), channel_id=1, source_target_pairs={{0,24},{8,0},{16,8},{24,16},{1,25},{9,1},{17,9},{25,17},{2,26},{10... | collective-permute-start | bytes 393224 | tf_op jit(solution)/shard_map/ppermute | solution.py:26
  133.3 7.8 %collective-permute-start.23 = (bf16[512,128]{1,0:T(8,128)(2,1)}, bf16[512,128]{1,0:T(8,128)(2,1)S(1)}, u32[]{:S(2)}, u32[]{:S(2)}) collective-permute-start(bf16[512,128]{1,0:T(8,128)(2,1)} %get-tuple-element.31), channel_id=1, source_target_pairs={{0,16},{8,24},{16,0},{24,8},{1,17},{9,25},{17,1},{25,9},{2,18},{10... | collective-permute-start | bytes 393224 | tf_op jit(solution)/shard_map/ppermute | solution.py:26
  134.8 7.8 %collective-permute-start.24 = (bf16[512,128]{1,0:T(8,128)(2,1)}, bf16[512,128]{1,0:T(8,128)(2,1)S(1)}, u32[]{:S(2)}, u32[]{:S(2)}) collective-permute-start(bf16[512,128]{1,0:T(8,128)(2,1)} %get-tuple-element.32), channel_id=1, source_target_pairs={{0,8},{8,16},{16,24},{24,0},{1,9},{9,17},{17,25},{25,1},{2,10},{10... | collective-permute-start | bytes 393224 | tf_op jit(solution)/shard_map/ppermute | solution.py:26
  169.9 16.5 %all-to-all-start.4 = ((bf16[32,32,128]{2,1,0:T(8,128)(2,1)}), bf16[32,32,128]{2,1,0:T(8,128)(2,1)S(1)}, u32[]{:S(2)}, u32[]{:S(2)}) async-start(bf16[32,32,128]{2,1,0:T(8,128)(2,1)} %broadcast_in_dim.18), calls=%async_computation.4 | async-start | bytes 524288 | tf_op jit(solution)/shard_map/all_to_all | solution.py:38
  (26 other events, 266.2 us)

commit v8 on v6

--- a/solution.py
+++ b/solution.py
@@ -239,14 +239,13 @@
 
 
 def down_kernel(
-    y_ref, x0_ref, x1_ref, x2a_ref, x2b_ref, x3_ref, inner_ref, keep_ref, got1_ref, got2_ref, got3_ref,
+    y_ref, x0_ref, x1_ref, x2_ref, x3_ref, inner_ref, keep_ref, got1_ref, got2_ref, got3_ref,
     out_ref,
 ):
     step = pl.program_id(0)
-    x2 = jnp.where(step < 2, x2a_ref[...], x2b_ref[...])
     total = across(inner_ref[...], x0_ref[...])
     total = total + across(got1_ref[256:512, :], x1_ref[...])
-    total = total + across(got2_ref[256:512, :], x2)
+    total = total + across(got2_ref[256:512, :], x2_ref[...])
     total = total + across(got3_ref[256:512, :], x3_ref[...])
     total = total.astype(BF16)
     for j in range(2):
@@ -258,7 +257,7 @@
         out_ref[j, 256:288, :] = ((rows[0] + rows[1]) + (rows[2] + rows[3])).astype(BF16)
 
 
-def run_down(my_y, saved, x1, x2a, x2b, x3, inner, keep, got1, got2, got3):
+def run_down(my_y, saved, x1, x2, x3, inner, keep, got1, got2, got3):
     cols = 512
     whole = lambda value: pl.BlockSpec(value.shape, lambda i, y: (0, 0))
     block = (256, cols)
@@ -270,8 +269,7 @@
             in_specs=[
                 pl.BlockSpec(block, lambda i, y: (0, 4 * y[0] + i)),
                 pl.BlockSpec(block, lambda i, y: (0, i)),
-                pl.BlockSpec(block, lambda i, y: (0, jnp.minimum(i, 1))),
-                pl.BlockSpec(block, lambda i, y: (0, jnp.maximum(i - 2, 0))),
+                pl.BlockSpec(block, lambda i, y: (0, i)),
                 pl.BlockSpec(block, lambda i, y: (0, i)),
                 whole(inner), whole(keep), whole(got1), whole(got2), whole(got3),
             ],
@@ -279,7 +277,7 @@
         ),
         out_shape=jax.ShapeDtypeStruct((NZ, 288, 128), BF16),
         name="down_product",
-    )(my_y.reshape(1), saved, x1, x2a, x2b, x3, inner, keep, got1, got2, got3)
+    )(my_y.reshape(1), saved, x1, x2, x3, inner, keep, got1, got2, got3)
 
 
 def stages(
@@ -320,10 +318,13 @@
     def cut(index, k, lo, size):
         return lax.dynamic_slice_in_dim(saved, ((index - k) % NY) * wide + lo, size, 1)
 
-    x1 = shift(cut(my_y, 1, 0, wide), "y", -1)
-    x3 = shift(cut(my_y, 3, 0, wide), "y", -3)
-
-    up_rows = rows_at(up_map, my_dp * share, share)
+    x1 = cut(my_y, 1, 0, wide)
+    x3 = cut(my_y, 3, 0, wide)
+    x1, x3, tied_dp = lax.optimization_barrier((x1, x3, my_dp))
+    x1 = shift(x1, "y", -1)
+    x3 = shift(x3, "y", -3)
+
+    up_rows = rows_at(up_map, tied_dp * share, share)
     sent, factors, rep = local_call(
         pack_kernel,
         [((DP, 64, rank), BF16), ((SECTIONS, share, rank), BF16), ((SECTIONS, NZ * tok, rank), BF16)],
@@ -331,13 +332,13 @@
     )
 
     late_y, down_late, sent = lax.optimization_barrier((my_y, down_map, sent))
-    x2a = cut(late_y, 2, 0, wide // 2)
-    x2b = cut(late_y, 2, wide // 2, wide // 2)
+    x2 = cut(late_y, 2, 0, wide)
     preact = jnp.dot(saved, down_late, preferred_element_type=F32)
     logistic = jax.nn.sigmoid(preact)
     active = (preact * logistic).astype(BF16)
     slope = (logistic * (1.0 + preact * (1.0 - logistic))).astype(BF16)
-    slope_own = jnp.stack([slope] + [from_later(slope, k) for k in range(1, NX)])
+    slopes = [slope] + [from_later(slope, k) for k in range(1, NX)]
+    slope_own = jnp.stack(slopes)
     slope_other = swap_c(slope_own)
 
     got = exchange_dp(sent)
@@ -356,14 +357,13 @@
     low = (part[256:] - top[256:].astype(F32)).astype(BF16)
     halves = jnp.concatenate([top, low], axis=0)
     others = [shift(halves, "x", -k) for k in range(1, NX)]
-    x2a = shift(x2a, "y", -2)
+    x2 = shift(x2, "y", -2)
     sent, residual = local_call(
         gram_kernel,
         [((DP, 16, rank), BF16), ((256, rank), BF16)],
         where, halves, *others, mask,
     )
     got = exchange_dp(sent)
-    x2b = shift(x2b, "y", -2)
     cross_own = jnp.concatenate(kept, axis=0)
     cross_other = swap_c(cross_own)
     keep, send1, send2, send3, inner, mix, _ = local_call(
@@ -375,7 +375,7 @@
     got1 = shift(send1, "y", -1)
     got2 = shift(send2, "y", -2)
     got3 = shift(send3, "y", -3)
-    part_down = run_down(my_y, saved, x1, x2a, x2b, x3, inner, keep, got1, got2, got3)
+    part_down = run_down(my_y, saved, x1, x2, x3, inner, keep, got1, got2, got3)
     got = lax.all_to_all(part_down, "z", 0, 0, tiled=True)
     total = jnp.sum(got.astype(F32), axis=0)
     rows = total[256:].astype(BF16)

time: 190 us -> 204 us (1.074)
  waiting for transfers between devices: 52.7 us -> 80.9 us
  blocking collectives: 43.1 us -> 23.2 us
  starting transfers between devices: 51 us -> 55 us
    all_to_all x3 -> x4, waiting for transfers between devices: 24.5 us -> 48.5 us  [exchange_dp(): return lax.all_to_all(blocks, ('y', 'z'), 0, 0, tiled=True)]
    all_to_all x1 -> x0, blocking collectives: 21.9 us -> none  [exchange_dp(): return lax.all_to_all(blocks, ('y', 'z'), 0, 0, tiled=True)]
    all_to_all x3 -> x4, starting transfers between devices: 21.2 us -> 27.9 us  [exchange_dp(): return lax.all_to_all(blocks, ('y', 'z'), 0, 0, tiled=True)]
    ppermute x13 -> x12, waiting for transfers between devices: 19.5 us -> 24.4 us  [shift(): lax.ppermute(value, axis, [(src, (src + steps) % count) for src in range(...]
    ppermute x13 -> x12, starting transfers between devices: 20.8 us -> 18 us  [shift(): lax.ppermute(value, axis, [(src, (src + steps) % count) for src in range(...]
  transfers between devices with their start and end apart: 28 -> 28, of which waited for: 11 -> 14; matrix products, arithmetic and copies ran while one was open for 9% -> 9% of each run, Pallas kernels for 5% -> 5%
where the time goes in v8:
time: 204 us; the launch traced here: 203 us
  waiting for transfers between devices  80.9 us (40%)
  starting transfers between devices  55 us (27%)
  blocking collectives  23.2 us (11%)
  Pallas kernels  17.5 us (9%)
  local copies, waits for them, and re-layouts  16.7 us (8%)
  matrix products  5.07 us (2%)
  other arithmetic  3.12 us (2%)
    all_to_all x4, waiting for transfers between devices, exchange_dp(): return lax.all_to_all(blocks, ('y', 'z'), 0, 0, tiled=True)  48.5 us
    all_to_all x4, starting transfers between devices, exchange_dp(): return lax.all_to_all(blocks, ('y', 'z'), 0, 0, tiled=True)  27.9 us
    ppermute x12, waiting for transfers between devices, shift(): lax.ppermute(value, axis, [(src, (src + steps) % count) for src in range(...  24.4 us
    all_to_all x1, blocking collectives, stages(): got = lax.all_to_all(part_down, 'z', 0, 0, tiled=True)  23.2 us
    ppermute x12, starting transfers between devices, shift(): lax.ppermute(value, axis, [(src, (src + steps) % count) for src in range(...  18 us
    pallas_call x4, Pallas kernels, local_call(): pl.pallas_call(kernel, out_shape=tuple((jax.ShapeDtypeStruct(shape, dtype...  12.8 us
    ppermute x6, waiting for transfers between devices, from_later(): lax.ppermute(value, 'x', [(src, src - steps) for src in range(steps, NX)])  8.04 us
    ppermute x6, starting transfers between devices, from_later(): lax.ppermute(value, 'x', [(src, src - steps) for src in range(steps, NX)])  7.73 us
  transfers between devices with their start and end apart: 28, of which 14 were waited for; matrix products, arithmetic and copies ran while one was open for 9% of the time, Pallas kernels for 5%

profile of v8, /device:TPU:32, one launch (start us, length us, event | category | flops | bytes accessed | tf_op | source)
XLA Modules:
  0.0 202.8 jit_solution(16207583900792915119)
XLA Ops:
  5.5 7.0 %collective-permute-start.4 = (bf16[1024,128]{1,0:T(8,128)(2,1)S(1)}, bf16[1024,128]{1,0:T(8,128)(2,1)S(1)}, u32[]{:S(2)}, u32[]{:S(2)}) collective-permute-start(bf16[1024,128]{1,0:T(8,128)(2,1)S(1)} %get-tuple-element.60), channel_id=1, source_target_pairs={{0,192},{64,0},{128,64},{192,128},{1,193},{65,1},{129,65},{193,129... | collective-permute-start | bytes 786440 | tf_op jit(solution)/shard_map/ppermute | solution.py:26
  14.5 3.1 %constant_dynamic-slice_fusion.2 = (bf16[256,2048]{1,0:T(8,128)(2,1)}, bf16[256,2048]{1,0:T(8,128)(2,1)}) fusion(bf16[256,8192]{1,0:T(8,128)(2,1)} %bitcast.52, s32[]{:T(128)S(6)} %select_n.68, s32[]{:T(128)S(6)} %select_n.66), kind=kLoop, calls=%fused_computation.45 | loop fusion | bytes 4194312 | tf_op jit(solution)/shard_map/dynamic_slice | solution.py:319
  19.7 4.0 %collective-permute-done.4.got1_ref = bf16[1024,128]{1,0:T(8,128)(2,1)S(1)} collective-permute-done((bf16[1024,128]{1,0:T(8,128)(2,1)S(1)}, bf16[1024,128]{1,0:T(8,128)(2,1)S(1)}, u32[]{:S(2)}, u32[]{:S(2)}) %collective-permute-start.4) | collective-permute-done | bytes 262176 | tf_op jit(solution)/shard_map/ppermute | solution.py:26
  23.7 3.8 %collective-permute-done.6.got3_ref = bf16[1024,128]{1,0:T(8,128)(2,1)} collective-permute-done((bf16[1024,128]{1,0:T(8,128)(2,1)S(1)}, bf16[1024,128]{1,0:T(8,128)(2,1)}, u32[]{:S(2)}, u32[]{:S(2)}) %collective-permute-start.6) | collective-permute-done | bytes 262176 | tf_op jit(solution)/shard_map/ppermute | solution.py:26
  27.5 2.7 %shard_map.94 = (bf16[32,64,128]{2,1,0:T(8,128)(2,1)}, bf16[8,256,128]{2,1,0:T(8,128)(2,1)}, bf16[8,256,128]{2,1,0:T(8,128)(2,1)}) custom-call(s32[3]{0:T(128)} %pad_add_fusion.where_ref, bf16[32,128]{1,0:T(8,128)(2,1)} %copy-done.20, bf16[256,128]{1,0:T(8,128)(2,1)} %heads_ref.1, bf16[256,128]{1,0:T(8,128)(2,1)} %dynamic-slice_bitcast_fusion.3.up_ref, ...), custom_call_target="tpu_custom_call" | custom-call | tf_op jit(solution)/shard_map/pallas_call | solution.py:58
  30.1 10.0 %all-to-all-start = ((bf16[32,64,128]{2,1,0:T(8,128)(2,1)}), bf16[32,64,128]{2,1,0:T(8,128)(2,1)S(1)}, u32[]{:S(2)}, u32[]{:S(2)}) async-start(bf16[32,64,128]{2,1,0:T(8,128)(2,1)} %get-tuple-element.27), calls=%async_computation | async-start | bytes 1048576 | tf_op jit(solution)/shard_map/all_to_all | solution.py:38
  40.1 2.8 %collective-permute-start = (bf16[256,2048]{1,0:T(8,128)(2,1)}, bf16[256,2048]{1,0:T(8,128)(2,1)}, u32[]{:S(2)}, u32[]{:S(2)}) collective-permute-start(bf16[256,2048]{1,0:T(8,128)(2,1)} %get-tuple-element.22), channel_id=1, source_target_pairs={{0,24},{8,0},{16,8},{24,16},{1,25},{9,1},{17,9},{25,17},{2,26},{10... | collective-permute-start | bytes 3145736 | tf_op jit(solution)/shard_map/ppermute | solution.py:26
  42.9 15.0 %all-to-all-done.got_ref = bf16[32,64,128]{2,1,0:T(8,128)(2,1)S(1)} async-done(((bf16[32,64,128]{2,1,0:T(8,128)(2,1)}), bf16[32,64,128]{2,1,0:T(8,128)(2,1)S(1)}, u32[]{:S(2)}, u32[]{:S(2)}) %all-to-all-start) | async-done | bytes 524320 | tf_op jit(solution)/shard_map/all_to_all | solution.py:38
  58.8 2.3 %shard_map.95 = (f32[384,128]{1,0:T(8,128)}, bf16[32,128]{1,0:T(8,128)(2,1)}, bf16[1024,128]{1,0:T(8,128)(2,1)}) custom-call(s32[3]{0:T(128)} %pad_add_fusion.where_ref, bf16[32,64,128]{2,1,0:T(8,128)(2,1)} %copy-done.2, bf16[8,256,128]{2,1,0:T(8,128)(2,1)} %get-tuple-element.28.rep_ref, bf16[32,128]{1,0:T(8,128)(2,1)} %bitcast.67), custom_call_target="tpu_custom_call" | custom-call | tf_op jit(solution)/shard_map/pallas_call | solution.py:58
  62.5 5.0 %all-to-all-start.2 = ((bf16[32,32,128]{2,1,0:T(8,128)(2,1)}), bf16[32,32,128]{2,1,0:T(8,128)(2,1)S(1)}, u32[]{:S(2)}, u32[]{:S(2)}) async-start(bf16[32,32,128]{2,1,0:T(8,128)(2,1)} %broadcast_in_dim.11), calls=%async_computation.2 | async-start | bytes 524288 | tf_op jit(solution)/shard_map/all_to_all | solution.py:38
  67.5 4.1 %multiply_convert_fusion = (bf16[256,128]{1,0:T(8,128)(2,1)S(1)}, bf16[256,128]{1,0:T(8,128)(2,1)}) fusion(bf16[256,8192]{1,0:T(8,128)(2,1)} %bitcast.53, bf16[8192,128]{1,0:T(8,128)(2,1)S(1)} %bitcast.51), kind=kOutput, calls=%fused_computation.31 | convolution fusion | flops 537198592 | bytes 6422528 | tf_op jit(solution)/shard_map/dot_general | solution.py:336
  74.3 2.3 %constant_dynamic-slice_fusion = bf16[256,2048]{1,0:T(8,128)(2,1)} fusion(bf16[256,8192]{1,0:T(8,128)(2,1)} %bitcast.54, s32[]{:T(128)S(6)} %select_n.82), kind=kLoop, calls=%fused_computation.43 | loop fusion | bytes 2097156 | tf_op jit(solution)/shard_map/dynamic_slice | solution.py:319
  84.9 6.7 %collective-permute-done.19 = bf16[256,128]{1,0:T(8,128)(2,1)S(1)} collective-permute-done((bf16[256,128]{1,0:T(8,128)(2,1)S(1)}, bf16[256,128]{1,0:T(8,128)(2,1)S(1)}, u32[]{:S(2)}, u32[]{:S(2)}) %collective-permute-start.19) | collective-permute-done | bytes 65568 | tf_op jit(solution)/shard_map/ppermute | solution.py:30
  95.3 5.5 %collective-permute-done.10.b_ref = bf16[512,128]{1,0:T(8,128)(2,1)S(1)} collective-permute-done((bf16[512,128]{1,0:T(8,128)(2,1)S(1)}, bf16[512,128]{1,0:T(8,128)(2,1)S(1)}, u32[]{:S(2)}, u32[]{:S(2)}) %collective-permute-start.10) | collective-permute-done | bytes 131104 | tf_op jit(solution)/shard_map/ppermute | solution.py:26
  104.2 3.8 %collective-permute-done.12.d_ref = bf16[512,128]{1,0:T(8,128)(2,1)} collective-permute-done((bf16[512,128]{1,0:T(8,128)(2,1)S(1)}, bf16[512,128]{1,0:T(8,128)(2,1)}, u32[]{:S(2)}, u32[]{:S(2)}) %collective-permute-start.12) | collective-permute-done | bytes 131104 | tf_op jit(solution)/shard_map/ppermute | solution.py:26
  108.7 2.4 %shard_map.96 = (bf16[32,16,128]{2,1,0:T(8,128)(2,1)}, bf16[256,128]{1,0:T(8,128)(2,1)}) custom-call(s32[3]{0:T(128)} %pad_add_fusion.where_ref, bf16[512,128]{1,0:T(8,128)(2,1)} %copy-done.7, bf16[512,128]{1,0:T(8,128)(2,1)} %copy-done.15, bf16[512,128]{1,0:T(8,128)(2,1)} %copy-done.16, bf16[512,128]{1,0:T(8,128)(2,1)} %collective-permute-done.12.d_ref, ...), custom_call_target="tpu_custom_call" | custom-call | tf_op jit(solution)/shard_map/pallas_call | solution.py:58
  111.1 8.0 %all-to-all-start.1 = ((bf16[32,16,128]{2,1,0:T(8,128)(2,1)}), bf16[32,16,128]{2,1,0:T(8,128)(2,1)S(1)}, u32[]{:S(2)}, u32[]{:S(2)}) async-start(bf16[32,16,128]{2,1,0:T(8,128)(2,1)} %get-tuple-element.30), calls=%async_computation.1 | async-start | bytes 262144 | tf_op jit(solution)/shard_map/all_to_all | solution.py:38
  119.1 22.0 %all-to-all-done.1.got_ref = bf16[32,16,128]{2,1,0:T(8,128)(2,1)S(1)} async-done(((bf16[32,16,128]{2,1,0:T(8,128)(2,1)}), bf16[32,16,128]{2,1,0:T(8,128)(2,1)S(1)}, u32[]{:S(2)}, u32[]{:S(2)}) %all-to-all-start.1) | async-done | bytes 131104 | tf_op jit(solution)/shard_map/all_to_all | solution.py:38
  141.8 5.5 %shard_map.97 = (bf16[256,128]{1,0:T(8,128)(2,1)}, bf16[512,128]{1,0:T(8,128)(2,1)}, bf16[512,128]{1,0:T(8,128)(2,1)}, bf16[512,128]{1,0:T(8,128)(2,1)}, bf16[25...) custom-call(s32[3]{0:T(128)} %pad_add_fusion.where_ref, bf16[32,16,128]{2,1,0:T(8,128)(2,1)} %copy-done.6, ...), custom_call_target="tpu_custom_call" | custom-call | tf_op jit(solution)/shard_map/pallas_call | solution.py:58
  149.5 3.8 %collective-permute-done.21.got1_ref = bf16[512,128]{1,0:T(8,128)(2,1)S(1)} collective-permute-done((bf16[512,128]{1,0:T(8,128)(2,1)}, bf16[512,128]{1,0:T(8,128)(2,1)S(1)}, u32[]{:S(2)}, u32[]{:S(2)}) %collective-permute-start.21) | collective-permute-done | bytes 131104 | tf_op jit(solution)/shard_map/ppermute | solution.py:26
  157.0 4.7 %down_product.1 = bf16[8,288,128]{2,1,0:T(8,128)(2,1)} custom-call(s32[1]{0:T(128)} %bitcast.y_ref, bf16[256,8192]{1,0:T(8,128)(2,1)} %bitcast.55, bf16[256,2048]{1,0:T(8,128)(2,1)} %collective-permute-done.x1_ref, bf16[256,2048]{1,0:T(8,128)(2,1)} %collective-permute-done.7.x2_ref, bf16[256,2048]{1,0:T(8,128)(2,1)} %collective-permute-done.8.x3_ref, ...), custom_call_target="tpu_custom_call" | custom-call | tf_op jit(solution)/shard_map/down_product/pallas_call | solution.py:264
  161.6 23.2 %all_to_all.25 = bf16[8,288,128]{2,1,0:T(8,128)(2,1)S(1)} all-to-all(bf16[8,288,128]{2,1,0:T(8,128)(2,1)} %down_product.1), channel_id=1, replica_groups=mesh['x'=4,'c'=2,'y'=4,'z'=8] {'z'}, dimensions={0} | all-to-all | bytes 1179648 | tf_op jit(solution)/shard_map/all_to_all | solution.py:379
  185.7 5.0 %all-to-all-start.4 = ((bf16[32,32,128]{2,1,0:T(8,128)(2,1)}), bf16[32,32,128]{2,1,0:T(8,128)(2,1)S(1)}, u32[]{:S(2)}, u32[]{:S(2)}) async-start(bf16[32,32,128]{2,1,0:T(8,128)(2,1)} %broadcast_in_dim.25), calls=%async_computation.4 | async-start | bytes 524288 | tf_op jit(solution)/shard_map/all_to_all | solution.py:38
  192.7 9.2 %all-to-all-done.4 = bf16[32,32,128]{2,1,0:T(8,128)(2,1)S(1)} async-done(((bf16[32,32,128]{2,1,0:T(8,128)(2,1)}), bf16[32,32,128]{2,1,0:T(8,128)(2,1)S(1)}, u32[]{:S(2)}, u32[]{:S(2)}) %all-to-all-start.4) | async-done | bytes 262176 | tf_op jit(solution)/shard_map/all_to_all | solution.py:38
  (114 shorter events, 39.9 us)
Async XLA Ops:
  4.0 15.7 %collective-permute-start.1 = (bf16[32,128]{1,0:T(8,128)(2,1)S(1)}, bf16[32,128]{1,0:T(8,128)(2,1)S(1)}, u32[]{:S(2)}, u32[]{:S(2)}) collective-permute-start(bf16[32,128]{1,0:T(8,128)(2,1)S(1)} %constant_dynamic-slice_fusion.1), channel_id=1, source_target_pairs={{0,0},{8,64},{16,128},{24,192},{64,8},{72,72},{80,136},{88,200},{1... | collective-permute-start | bytes 24584 | tf_op jit(solution)/shard_map/ppermute | solution.py:303
  5.5 18.1 %collective-permute-start.4 = (bf16[1024,128]{1,0:T(8,128)(2,1)S(1)}, bf16[1024,128]{1,0:T(8,128)(2,1)S(1)}, u32[]{:S(2)}, u32[]{:S(2)}) collective-permute-start(bf16[1024,128]{1,0:T(8,128)(2,1)S(1)} %get-tuple-element.60), channel_id=1, source_target_pairs={{0,192},{64,0},{128,64},{192,128},{1,193},{65,1},{129,65},{193,129... | collective-permute-start | bytes 786440 | tf_op jit(solution)/shard_map/ppermute | solution.py:26
  12.6 11.1 %collective-permute-start.5 = (bf16[1024,128]{1,0:T(8,128)(2,1)S(1)}, bf16[1024,128]{1,0:T(8,128)(2,1)}, u32[]{:S(2)}, u32[]{:S(2)}) collective-permute-start(bf16[1024,128]{1,0:T(8,128)(2,1)S(1)} %get-tuple-element.59), channel_id=1, source_target_pairs={{0,128},{64,192},{128,0},{192,64},{1,129},{65,193},{129,1},{193,65... | collective-permute-start | bytes 786440 | tf_op jit(solution)/shard_map/ppermute | solution.py:26
  13.1 14.3 %collective-permute-start.6 = (bf16[1024,128]{1,0:T(8,128)(2,1)S(1)}, bf16[1024,128]{1,0:T(8,128)(2,1)}, u32[]{:S(2)}, u32[]{:S(2)}) collective-permute-start(bf16[1024,128]{1,0:T(8,128)(2,1)S(1)} %get-tuple-element.58), channel_id=1, source_target_pairs={{0,64},{64,128},{128,192},{192,0},{1,65},{65,129},{129,193},{193,1... | collective-permute-start | bytes 786440 | tf_op jit(solution)/shard_map/ppermute | solution.py:26
  30.1 27.8 %all-to-all-start = ((bf16[32,64,128]{2,1,0:T(8,128)(2,1)}), bf16[32,64,128]{2,1,0:T(8,128)(2,1)S(1)}, u32[]{:S(2)}, u32[]{:S(2)}) async-start(bf16[32,64,128]{2,1,0:T(8,128)(2,1)} %get-tuple-element.27), calls=%async_computation | async-start | bytes 1048576 | tf_op jit(solution)/shard_map/all_to_all | solution.py:38
  40.1 108.1 %collective-permute-start = (bf16[256,2048]{1,0:T(8,128)(2,1)}, bf16[256,2048]{1,0:T(8,128)(2,1)}, u32[]{:S(2)}, u32[]{:S(2)}) collective-permute-start(bf16[256,2048]{1,0:T(8,128)(2,1)} %get-tuple-element.22), channel_id=1, source_target_pairs={{0,24},{8,0},{16,8},{24,16},{1,25},{9,1},{17,9},{25,17},{2,26},{10... | collective-permute-start | bytes 3145736 | tf_op jit(solution)/shard_map/ppermute | solution.py:26
  62.5 16.4 %all-to-all-start.2 = ((bf16[32,32,128]{2,1,0:T(8,128)(2,1)}), bf16[32,32,128]{2,1,0:T(8,128)(2,1)S(1)}, u32[]{:S(2)}, u32[]{:S(2)}) async-start(bf16[32,32,128]{2,1,0:T(8,128)(2,1)} %broadcast_in_dim.11), calls=%async_computation.2 | async-start | bytes 524288 | tf_op jit(solution)/shard_map/all_to_all | solution.py:38
  71.6 10.0 %collective-permute-start.17 = (bf16[256,128]{1,0:T(8,128)(2,1)S(1)}, bf16[256,128]{1,0:T(8,128)(2,1)S(1)}, u32[]{:S(2)}, u32[]{:S(2)}) collective-permute-start(bf16[256,128]{1,0:T(8,128)(2,1)S(1)} %get-tuple-element.56), channel_id=1, source_target_pairs={{64,0},{128,64},{192,128},{65,1},{129,65},{193,129},{66,2},{130,66... | collective-permute-start | bytes 196616 | tf_op jit(solution)/shard_map/ppermute | solution.py:30
  72.9 10.1 %collective-permute-start.18 = (bf16[256,128]{1,0:T(8,128)(2,1)S(1)}, bf16[256,128]{1,0:T(8,128)(2,1)S(1)}, u32[]{:S(2)}, u32[]{:S(2)}) collective-permute-start(bf16[256,128]{1,0:T(8,128)(2,1)S(1)} %get-tuple-element.56), channel_id=1, source_target_pairs={{128,0},{192,64},{129,1},{193,65},{130,2},{194,66},{131,3},{195,67... | collective-permute-start | bytes 196616 | tf_op jit(solution)/shard_map/ppermute | solution.py:30
  79.0 15.7 %collective-permute-start.13 = (bf16[768,128]{1,0:T(8,128)(2,1)S(1)}, bf16[768,128]{1,0:T(8,128)(2,1)S(1)}, u32[]{:S(2)}, u32[]{:S(2)}) collective-permute-start(bf16[768,128]{1,0:T(8,128)(2,1)S(1)} %bitcast.60), channel_id=1, source_target_pairs={{64,0},{128,64},{192,128},{65,1},{129,65},{193,129},{66,2},{130,66... | collective-permute-start | bytes 589832 | tf_op jit(solution)/shard_map/ppermute | solution.py:30
  80.3 14.3 %collective-permute-start.14 = (bf16[512,128]{1,0:T(8,128)(2,1)S(1)}, bf16[512,128]{1,0:T(8,128)(2,1)S(1)}, u32[]{:S(2)}, u32[]{:S(2)}) collective-permute-start(bf16[512,128]{1,0:T(8,128)(2,1)S(1)} %bitcast.61), channel_id=1, source_target_pairs={{128,0},{192,64},{129,1},{193,65},{130,2},{194,66},{131,3},{195,67... | collective-permute-start | bytes 393224 | tf_op jit(solution)/shard_map/ppermute | solution.py:30
  81.6 10.0 %collective-permute-start.19 = (bf16[256,128]{1,0:T(8,128)(2,1)S(1)}, bf16[256,128]{1,0:T(8,128)(2,1)S(1)}, u32[]{:S(2)}, u32[]{:S(2)}) collective-permute-start(bf16[256,128]{1,0:T(8,128)(2,1)S(1)} %get-tuple-element.56), channel_id=1, source_target_pairs={{192,0},{193,1},{194,2},{195,3},{196,4},{197,5},{198,6},{199,7},{2... | collective-permute-start | bytes 196616 | tf_op jit(solution)/shard_map/ppermute | solution.py:30
  83.6 9.4 %collective-permute-start.15 = (bf16[256,128]{1,0:T(8,128)(2,1)S(1)}, bf16[256,128]{1,0:T(8,128)(2,1)S(1)}, u32[]{:S(2)}, u32[]{:S(2)}) collective-permute-start(bf16[256,128]{1,0:T(8,128)(2,1)S(1)} %bitcast.62), channel_id=1, source_target_pairs={{192,0},{193,1},{194,2},{195,3},{196,4},{197,5},{198,6},{199,7},{2... | collective-permute-start | bytes 196616 | tf_op jit(solution)/shard_map/ppermute | solution.py:30
  91.6 57.9 %collective-permute-start.8 = (bf16[256,2048]{1,0:T(8,128)(2,1)}, bf16[256,2048]{1,0:T(8,128)(2,1)}, u32[]{:S(2)}, u32[]{:S(2)}) collective-permute-start(bf16[256,2048]{1,0:T(8,128)(2,1)} %get-tuple-element.26), channel_id=1, source_target_pairs={{0,8},{8,16},{16,24},{24,0},{1,9},{9,17},{17,25},{25,1},{2,10},{10... | collective-permute-start | bytes 3145736 | tf_op jit(solution)/shard_map/ppermute | solution.py:26
  93.0 56.5 %collective-permute-start.7 = (bf16[256,2048]{1,0:T(8,128)(2,1)}, bf16[256,2048]{1,0:T(8,128)(2,1)}, u32[]{:S(2)}, u32[]{:S(2)}) collective-permute-start(bf16[256,2048]{1,0:T(8,128)(2,1)} %constant_dynamic-slice_fusion), channel_id=1, source_target_pairs={{0,16},{8,24},{16,0},{24,8},{1,17},{9,25},{17,1},{25,9},{2,18},{10... | collective-permute-start | bytes 3145736 | tf_op jit(solution)/shard_map/ppermute | solution.py:26
  94.6 6.2 %collective-permute-start.10 = (bf16[512,128]{1,0:T(8,128)(2,1)S(1)}, bf16[512,128]{1,0:T(8,128)(2,1)S(1)}, u32[]{:S(2)}, u32[]{:S(2)}) collective-permute-start(bf16[512,128]{1,0:T(8,128)(2,1)S(1)} %pad_maximum_fusion.8.a_ref), channel_id=1, source_target_pairs={{0,192},{64,0},{128,64},{192,128},{1,193},{65,1},{129,65},{193,129... | collective-permute-start | bytes 393224 | tf_op jit(solution)/shard_map/ppermute | solution.py:26
  94.6 6.7 %collective-permute-start.11 = (bf16[512,128]{1,0:T(8,128)(2,1)S(1)}, bf16[512,128]{1,0:T(8,128)(2,1)S(1)}, u32[]{:S(2)}, u32[]{:S(2)}) collective-permute-start(bf16[512,128]{1,0:T(8,128)(2,1)S(1)} %pad_maximum_fusion.8.a_ref), channel_id=1, source_target_pairs={{0,128},{64,192},{128,0},{192,64},{1,129},{65,193},{129,1},{193,65... | collective-permute-start | bytes 393224 | tf_op jit(solution)/shard_map/ppermute | solution.py:26
  100.8 40.3 %collective-permute-start.16 = (bf16[2560,128]{1,0:T(8,128)(2,1)S(1)}, bf16[2560,128]{1,0:T(8,128)(2,1)}, u32[]{:S(2)}, u32[]{:S(2)}) collective-permute-start(bf16[2560,128]{1,0:T(8,128)(2,1)S(1)} %pad_maximum_fusion.own_ref), channel_id=1, source_target_pairs={{0,32},{32,0},{1,33},{33,1},{2,34},{34,2},{3,35},{35,3},{4,36},{36... | collective-permute-start | bytes 1966088 | tf_op jit(solution)/shard_map/ppermute | solution.py:34
  101.4 6.6 %collective-permute-start.12 = (bf16[512,128]{1,0:T(8,128)(2,1)S(1)}, bf16[512,128]{1,0:T(8,128)(2,1)}, u32[]{:S(2)}, u32[]{:S(2)}) collective-permute-start(bf16[512,128]{1,0:T(8,128)(2,1)S(1)} %pad_maximum_fusion.8.a_ref), channel_id=1, source_target_pairs={{0,64},{64,128},{128,192},{192,0},{1,65},{65,129},{129,193},{193,1... | collective-permute-start | bytes 393224 | tf_op jit(solution)/shard_map/ppermute | solution.py:26
  108.0 11.1 %collective-permute-start.20 = (bf16[4,256,128]{2,1,0:T(8,128)(2,1)S(1)}, bf16[4,256,128]{2,1,0:T(8,128)(2,1)S(1)}, u32[]{:S(2)}, u32[]{:S(2)}) collective-permute-start(bf16[4,256,128]{2,1,0:T(8,128)(2,1)S(1)} %pad_maximum_fusion.7.slope_own_ref), channel_id=1, source_target_pairs={{0,32},{32,0},{1,33},{33,1},{2,34},{34,2},{3,35},{35,3},{4,36},{36... | collective-permute-start | bytes 786440 | tf_op jit(solution)/shard_map/ppermute | solution.py:34
  111.1 30.0 %all-to-all-start.1 = ((bf16[32,16,128]{2,1,0:T(8,128)(2,1)}), bf16[32,16,128]{2,1,0:T(8,128)(2,1)S(1)}, u32[]{:S(2)}, u32[]{:S(2)}) async-start(bf16[32,16,128]{2,1,0:T(8,128)(2,1)} %get-tuple-element.30), calls=%async_computation.1 | async-start | bytes 262144 | tf_op jit(solution)/shard_map/all_to_all | solution.py:38
  147.7 7.7 %collective-permute-start.22 = (bf16[512,128]{1,0:T(8,128)(2,1)}, bf16[512,128]{1,0:T(8,128)(2,1)S(1)}, u32[]{:S(2)}, u32[]{:S(2)}) collective-permute-start(bf16[512,128]{1,0:T(8,128)(2,1)} %get-tuple-element.37), channel_id=1, source_target_pairs={{0,16},{8,24},{16,0},{24,8},{1,17},{9,25},{17,1},{25,9},{2,18},{10... | collective-permute-start | bytes 393224 | tf_op jit(solution)/shard_map/ppermute | solution.py:26
  148.2 8.1 %collective-permute-start.23 = (bf16[512,128]{1,0:T(8,128)(2,1)}, bf16[512,128]{1,0:T(8,128)(2,1)S(1)}, u32[]{:S(2)}, u32[]{:S(2)}) collective-permute-start(bf16[512,128]{1,0:T(8,128)(2,1)} %get-tuple-element.38), channel_id=1, source_target_pairs={{0,8},{8,16},{16,24},{24,0},{1,9},{9,17},{17,25},{25,1},{2,10},{10... | collective-permute-start | bytes 393224 | tf_op jit(solution)/shard_map/ppermute | solution.py:26
  185.7 16.1 %all-to-all-start.4 = ((bf16[32,32,128]{2,1,0:T(8,128)(2,1)}), bf16[32,32,128]{2,1,0:T(8,128)(2,1)S(1)}, u32[]{:S(2)}, u32[]{:S(2)}) async-start(bf16[32,32,128]{2,1,0:T(8,128)(2,1)} %broadcast_in_dim.25), calls=%async_computation.4 | async-start | bytes 524288 | tf_op jit(solution)/shard_map/all_to_all | solution.py:38
  (26 other events, 277.7 us)

commit v9 on v8

--- a/solution.py
+++ b/solution.py
@@ -113,7 +113,9 @@
         rows = total[32 * m : 32 * m + 32]
         part_ref[32 * m : 32 * m + 32, :] = rows - jnp.where(m == my_stage, target, 0.0)
     part_ref[256:384, :] = square
-    cross_ref[...] = jnp.sum(got_ref[:, 32:64, :].astype(F32), axis=0).astype(BF16)
+    cross = jnp.sum(got_ref[:, 32:64, :].astype(F32), axis=0).astype(BF16)
+    for d in range(DP):
+        cross_ref[d] = cross
 
 
 def gram_kernel(where_ref, a_ref, b_ref, c_ref, d_ref, mask_ref, sent_ref, residual_ref):
@@ -344,10 +346,10 @@
     got = exchange_dp(sent)
     part, cross_rows, _ = local_call(
         heads_kernel,
-        [((384, rank), F32), ((32, rank), BF16), ((1024, rank), BF16)],
+        [((384, rank), F32), ((DP, 32, rank), BF16), ((1024, rank), BF16)],
         where, got, rep, head_targets[0],
     )
-    got = exchange_dp(jnp.broadcast_to(cross_rows[None], (DP, 32, rank)))
+    got = exchange_dp(cross_rows)
     cross = got.reshape(-1, rank)
     kept = [cross]
     for k in range(1, NX):

time: 204 us -> 203 us (level)
  transfers between devices with their start and end apart: 28 -> 28, of which waited for: 14 -> 14; matrix products, arithmetic and copies ran while one was open for 9% -> 8% of each run, Pallas kernels for 5% -> 5%
where the time goes in v9:
time: 203 us; the launch traced here: 201 us
  waiting for transfers between devices  80.9 us (40%)
  starting transfers between devices  55 us (27%)
  blocking collectives  23.2 us (11%)
  Pallas kernels  17.6 us (9%)
  local copies, waits for them, and re-layouts  15.3 us (8%)
  matrix products  5.07 us (2%)
  other arithmetic  3.12 us (2%)
    all_to_all x4, waiting for transfers between devices, exchange_dp(): return lax.all_to_all(blocks, ('y', 'z'), 0, 0, tiled=True)  48.4 us
    all_to_all x4, starting transfers between devices, exchange_dp(): return lax.all_to_all(blocks, ('y', 'z'), 0, 0, tiled=True)  27.9 us
    ppermute x12, waiting for transfers between devices, shift(): lax.ppermute(value, axis, [(src, (src + steps) % count) for src in range(...  24.4 us
    all_to_all x1, blocking collectives, stages(): got = lax.all_to_all(part_down, 'z', 0, 0, tiled=True)  23.2 us
    ppermute x12, starting transfers between devices, shift(): lax.ppermute(value, axis, [(src, (src + steps) % count) for src in range(...  18 us
    pallas_call x4, Pallas kernels, local_call(): pl.pallas_call(kernel, out_shape=tuple((jax.ShapeDtypeStruct(shape, dtype...  13 us
    ppermute x6, waiting for transfers between devices, from_later(): lax.ppermute(value, 'x', [(src, src - steps) for src in range(steps, NX)])  8.03 us
    ppermute x6, starting transfers between devices, from_later(): lax.ppermute(value, 'x', [(src, src - steps) for src in range(steps, NX)])  7.73 us
  transfers between devices with their start and end apart: 28, of which 14 were waited for; matrix products, arithmetic and copies ran while one was open for 8% of the time, Pallas kernels for 5%

profile of v9, /device:TPU:32, one launch (start us, length us, event | category | flops | bytes accessed | tf_op | source)
XLA Modules:
  0.0 201.4 jit_solution(11984822368296461055)
XLA Ops:
  5.5 7.0 %collective-permute-start.4 = (bf16[1024,128]{1,0:T(8,128)(2,1)S(1)}, bf16[1024,128]{1,0:T(8,128)(2,1)S(1)}, u32[]{:S(2)}, u32[]{:S(2)}) collective-permute-start(bf16[1024,128]{1,0:T(8,128)(2,1)S(1)} %get-tuple-element.60), channel_id=1, source_target_pairs={{0,192},{64,0},{128,64},{192,128},{1,193},{65,1},{129,65},{193,129... | collective-permute-start | bytes 786440 | tf_op jit(solution)/shard_map/ppermute | solution.py:26
  14.5 3.1 %constant_dynamic-slice_fusion.2 = (bf16[256,2048]{1,0:T(8,128)(2,1)}, bf16[256,2048]{1,0:T(8,128)(2,1)}) fusion(bf16[256,8192]{1,0:T(8,128)(2,1)} %bitcast.52, s32[]{:T(128)S(6)} %select_n.68, s32[]{:T(128)S(6)} %select_n.66), kind=kLoop, calls=%fused_computation.45 | loop fusion | bytes 4194312 | tf_op jit(solution)/shard_map/dynamic_slice | solution.py:321
  19.7 4.0 %collective-permute-done.4.got1_ref = bf16[1024,128]{1,0:T(8,128)(2,1)S(1)} collective-permute-done((bf16[1024,128]{1,0:T(8,128)(2,1)S(1)}, bf16[1024,128]{1,0:T(8,128)(2,1)S(1)}, u32[]{:S(2)}, u32[]{:S(2)}) %collective-permute-start.4) | collective-permute-done | bytes 262176 | tf_op jit(solution)/shard_map/ppermute | solution.py:26
  23.7 3.8 %collective-permute-done.6.got3_ref = bf16[1024,128]{1,0:T(8,128)(2,1)} collective-permute-done((bf16[1024,128]{1,0:T(8,128)(2,1)S(1)}, bf16[1024,128]{1,0:T(8,128)(2,1)}, u32[]{:S(2)}, u32[]{:S(2)}) %collective-permute-start.6) | collective-permute-done | bytes 262176 | tf_op jit(solution)/shard_map/ppermute | solution.py:26
  27.5 2.7 %shard_map.94 = (bf16[32,64,128]{2,1,0:T(8,128)(2,1)}, bf16[8,256,128]{2,1,0:T(8,128)(2,1)}, bf16[8,256,128]{2,1,0:T(8,128)(2,1)}) custom-call(s32[3]{0:T(128)} %pad_add_fusion.where_ref, bf16[32,128]{1,0:T(8,128)(2,1)} %copy-done.20, bf16[256,128]{1,0:T(8,128)(2,1)} %heads_ref.1, bf16[256,128]{1,0:T(8,128)(2,1)} %dynamic-slice_bitcast_fusion.3.up_ref, ...), custom_call_target="tpu_custom_call" | custom-call | tf_op jit(solution)/shard_map/pallas_call | solution.py:58
  30.1 10.0 %all-to-all-start = ((bf16[32,64,128]{2,1,0:T(8,128)(2,1)}), bf16[32,64,128]{2,1,0:T(8,128)(2,1)S(1)}, u32[]{:S(2)}, u32[]{:S(2)}) async-start(bf16[32,64,128]{2,1,0:T(8,128)(2,1)} %get-tuple-element.27), calls=%async_computation | async-start | bytes 1048576 | tf_op jit(solution)/shard_map/all_to_all | solution.py:38
  40.1 2.8 %collective-permute-start = (bf16[256,2048]{1,0:T(8,128)(2,1)}, bf16[256,2048]{1,0:T(8,128)(2,1)}, u32[]{:S(2)}, u32[]{:S(2)}) collective-permute-start(bf16[256,2048]{1,0:T(8,128)(2,1)} %get-tuple-element.22), channel_id=1, source_target_pairs={{0,24},{8,0},{16,8},{24,16},{1,25},{9,1},{17,9},{25,17},{2,26},{10... | collective-permute-start | bytes 3145736 | tf_op jit(solution)/shard_map/ppermute | solution.py:26
  42.9 15.0 %all-to-all-done.got_ref = bf16[32,64,128]{2,1,0:T(8,128)(2,1)S(1)} async-done(((bf16[32,64,128]{2,1,0:T(8,128)(2,1)}), bf16[32,64,128]{2,1,0:T(8,128)(2,1)S(1)}, u32[]{:S(2)}, u32[]{:S(2)}) %all-to-all-start) | async-done | bytes 524320 | tf_op jit(solution)/shard_map/all_to_all | solution.py:38
  58.8 2.4 %shard_map.95 = (f32[384,128]{1,0:T(8,128)}, bf16[32,32,128]{2,1,0:T(8,128)(2,1)}, bf16[1024,128]{1,0:T(8,128)(2,1)}) custom-call(s32[3]{0:T(128)} %pad_add_fusion.where_ref, bf16[32,64,128]{2,1,0:T(8,128)(2,1)} %copy-done.2, bf16[8,256,128]{2,1,0:T(8,128)(2,1)} %get-tuple-element.28.rep_ref, bf16[32,128]{1,0:T(8,128)(2,1)} %bitcast.67), custom_call_target="tpu_custom_call" | custom-call | tf_op jit(solution)/shard_map/pallas_call | solution.py:58
  61.2 4.9 %all-to-all-start.2 = ((bf16[32,32,128]{2,1,0:T(8,128)(2,1)}), bf16[32,32,128]{2,1,0:T(8,128)(2,1)S(1)}, u32[]{:S(2)}, u32[]{:S(2)}) async-start(bf16[32,32,128]{2,1,0:T(8,128)(2,1)} %get-tuple-element.33), calls=%async_computation.2 | async-start | bytes 524288 | tf_op jit(solution)/shard_map/all_to_all | solution.py:38
  66.2 4.1 %multiply_convert_fusion = (bf16[256,128]{1,0:T(8,128)(2,1)S(1)}, bf16[256,128]{1,0:T(8,128)(2,1)}) fusion(bf16[256,8192]{1,0:T(8,128)(2,1)} %bitcast.53, bf16[8192,128]{1,0:T(8,128)(2,1)S(1)} %bitcast.51), kind=kOutput, calls=%fused_computation.31 | convolution fusion | flops 537198592 | bytes 6422528 | tf_op jit(solution)/shard_map/dot_general | solution.py:338
  73.0 2.3 %constant_dynamic-slice_fusion = bf16[256,2048]{1,0:T(8,128)(2,1)} fusion(bf16[256,8192]{1,0:T(8,128)(2,1)} %bitcast.54, s32[]{:T(128)S(6)} %select_n.82), kind=kLoop, calls=%fused_computation.43 | loop fusion | bytes 2097156 | tf_op jit(solution)/shard_map/dynamic_slice | solution.py:321
  83.6 6.7 %collective-permute-done.19 = bf16[256,128]{1,0:T(8,128)(2,1)S(1)} collective-permute-done((bf16[256,128]{1,0:T(8,128)(2,1)S(1)}, bf16[256,128]{1,0:T(8,128)(2,1)S(1)}, u32[]{:S(2)}, u32[]{:S(2)}) %collective-permute-start.19) | collective-permute-done | bytes 65568 | tf_op jit(solution)/shard_map/ppermute | solution.py:30
  94.0 5.5 %collective-permute-done.10.b_ref = bf16[512,128]{1,0:T(8,128)(2,1)S(1)} collective-permute-done((bf16[512,128]{1,0:T(8,128)(2,1)S(1)}, bf16[512,128]{1,0:T(8,128)(2,1)S(1)}, u32[]{:S(2)}, u32[]{:S(2)}) %collective-permute-start.10) | collective-permute-done | bytes 131104 | tf_op jit(solution)/shard_map/ppermute | solution.py:26
  102.9 3.8 %collective-permute-done.12.d_ref = bf16[512,128]{1,0:T(8,128)(2,1)} collective-permute-done((bf16[512,128]{1,0:T(8,128)(2,1)S(1)}, bf16[512,128]{1,0:T(8,128)(2,1)}, u32[]{:S(2)}, u32[]{:S(2)}) %collective-permute-start.12) | collective-permute-done | bytes 131104 | tf_op jit(solution)/shard_map/ppermute | solution.py:26
  107.3 2.4 %shard_map.96 = (bf16[32,16,128]{2,1,0:T(8,128)(2,1)}, bf16[256,128]{1,0:T(8,128)(2,1)}) custom-call(s32[3]{0:T(128)} %pad_add_fusion.where_ref, bf16[512,128]{1,0:T(8,128)(2,1)} %copy-done.7, bf16[512,128]{1,0:T(8,128)(2,1)} %copy-done.15, bf16[512,128]{1,0:T(8,128)(2,1)} %copy-done.16, bf16[512,128]{1,0:T(8,128)(2,1)} %collective-permute-done.12.d_ref, ...), custom_call_target="tpu_custom_call" | custom-call | tf_op jit(solution)/shard_map/pallas_call | solution.py:58
  109.8 8.0 %all-to-all-start.1 = ((bf16[32,16,128]{2,1,0:T(8,128)(2,1)}), bf16[32,16,128]{2,1,0:T(8,128)(2,1)S(1)}, u32[]{:S(2)}, u32[]{:S(2)}) async-start(bf16[32,16,128]{2,1,0:T(8,128)(2,1)} %get-tuple-element.30), calls=%async_computation.1 | async-start | bytes 262144 | tf_op jit(solution)/shard_map/all_to_all | solution.py:38
  117.8 22.0 %all-to-all-done.1.got_ref = bf16[32,16,128]{2,1,0:T(8,128)(2,1)S(1)} async-done(((bf16[32,16,128]{2,1,0:T(8,128)(2,1)}), bf16[32,16,128]{2,1,0:T(8,128)(2,1)S(1)}, u32[]{:S(2)}, u32[]{:S(2)}) %all-to-all-start.1) | async-done | bytes 131104 | tf_op jit(solution)/shard_map/all_to_all | solution.py:38
  140.4 5.5 %shard_map.97 = (bf16[256,128]{1,0:T(8,128)(2,1)}, bf16[512,128]{1,0:T(8,128)(2,1)}, bf16[512,128]{1,0:T(8,128)(2,1)}, bf16[512,128]{1,0:T(8,128)(2,1)}, bf16[25...) custom-call(s32[3]{0:T(128)} %pad_add_fusion.where_ref, bf16[32,16,128]{2,1,0:T(8,128)(2,1)} %copy-done.6, ...), custom_call_target="tpu_custom_call" | custom-call | tf_op jit(solution)/shard_map/pallas_call | solution.py:58
  148.2 3.8 %collective-permute-done.21.got1_ref = bf16[512,128]{1,0:T(8,128)(2,1)S(1)} collective-permute-done((bf16[512,128]{1,0:T(8,128)(2,1)}, bf16[512,128]{1,0:T(8,128)(2,1)S(1)}, u32[]{:S(2)}, u32[]{:S(2)}) %collective-permute-start.21) | collective-permute-done | bytes 131104 | tf_op jit(solution)/shard_map/ppermute | solution.py:26
  155.6 4.7 %down_product.1 = bf16[8,288,128]{2,1,0:T(8,128)(2,1)} custom-call(s32[1]{0:T(128)} %bitcast.y_ref, bf16[256,8192]{1,0:T(8,128)(2,1)} %bitcast.55, bf16[256,2048]{1,0:T(8,128)(2,1)} %collective-permute-done.x1_ref, bf16[256,2048]{1,0:T(8,128)(2,1)} %collective-permute-done.7.x2_ref, bf16[256,2048]{1,0:T(8,128)(2,1)} %collective-permute-done.8.x3_ref, ...), custom_call_target="tpu_custom_call" | custom-call | tf_op jit(solution)/shard_map/down_product/pallas_call | solution.py:266
  160.3 23.2 %all_to_all.25 = bf16[8,288,128]{2,1,0:T(8,128)(2,1)S(1)} all-to-all(bf16[8,288,128]{2,1,0:T(8,128)(2,1)} %down_product.1), channel_id=1, replica_groups=mesh['x'=4,'c'=2,'y'=4,'z'=8] {'z'}, dimensions={0} | all-to-all | bytes 1179648 | tf_op jit(solution)/shard_map/all_to_all | solution.py:381
  184.3 5.0 %all-to-all-start.4 = ((bf16[32,32,128]{2,1,0:T(8,128)(2,1)}), bf16[32,32,128]{2,1,0:T(8,128)(2,1)S(1)}, u32[]{:S(2)}, u32[]{:S(2)}) async-start(bf16[32,32,128]{2,1,0:T(8,128)(2,1)} %broadcast_in_dim.18), calls=%async_computation.4 | async-start | bytes 524288 | tf_op jit(solution)/shard_map/all_to_all | solution.py:38
  191.3 9.2 %all-to-all-done.4 = bf16[32,32,128]{2,1,0:T(8,128)(2,1)S(1)} async-done(((bf16[32,32,128]{2,1,0:T(8,128)(2,1)}), bf16[32,32,128]{2,1,0:T(8,128)(2,1)S(1)}, u32[]{:S(2)}, u32[]{:S(2)}) %all-to-all-start.4) | async-done | bytes 262176 | tf_op jit(solution)/shard_map/all_to_all | solution.py:38
  (113 shorter events, 38.4 us)
Async XLA Ops:
  4.0 15.7 %collective-permute-start.1 = (bf16[32,128]{1,0:T(8,128)(2,1)S(1)}, bf16[32,128]{1,0:T(8,128)(2,1)S(1)}, u32[]{:S(2)}, u32[]{:S(2)}) collective-permute-start(bf16[32,128]{1,0:T(8,128)(2,1)S(1)} %constant_dynamic-slice_fusion.1), channel_id=1, source_target_pairs={{0,0},{8,64},{16,128},{24,192},{64,8},{72,72},{80,136},{88,200},{1... | collective-permute-start | bytes 24584 | tf_op jit(solution)/shard_map/ppermute | solution.py:305
  5.5 18.1 %collective-permute-start.4 = (bf16[1024,128]{1,0:T(8,128)(2,1)S(1)}, bf16[1024,128]{1,0:T(8,128)(2,1)S(1)}, u32[]{:S(2)}, u32[]{:S(2)}) collective-permute-start(bf16[1024,128]{1,0:T(8,128)(2,1)S(1)} %get-tuple-element.60), channel_id=1, source_target_pairs={{0,192},{64,0},{128,64},{192,128},{1,193},{65,1},{129,65},{193,129... | collective-permute-start | bytes 786440 | tf_op jit(solution)/shard_map/ppermute | solution.py:26
  12.6 11.1 %collective-permute-start.5 = (bf16[1024,128]{1,0:T(8,128)(2,1)S(1)}, bf16[1024,128]{1,0:T(8,128)(2,1)}, u32[]{:S(2)}, u32[]{:S(2)}) collective-permute-start(bf16[1024,128]{1,0:T(8,128)(2,1)S(1)} %get-tuple-element.59), channel_id=1, source_target_pairs={{0,128},{64,192},{128,0},{192,64},{1,129},{65,193},{129,1},{193,65... | collective-permute-start | bytes 786440 | tf_op jit(solution)/shard_map/ppermute | solution.py:26
  13.1 14.3 %collective-permute-start.6 = (bf16[1024,128]{1,0:T(8,128)(2,1)S(1)}, bf16[1024,128]{1,0:T(8,128)(2,1)}, u32[]{:S(2)}, u32[]{:S(2)}) collective-permute-start(bf16[1024,128]{1,0:T(8,128)(2,1)S(1)} %get-tuple-element.58), channel_id=1, source_target_pairs={{0,64},{64,128},{128,192},{192,0},{1,65},{65,129},{129,193},{193,1... | collective-permute-start | bytes 786440 | tf_op jit(solution)/shard_map/ppermute | solution.py:26
  30.1 27.8 %all-to-all-start = ((bf16[32,64,128]{2,1,0:T(8,128)(2,1)}), bf16[32,64,128]{2,1,0:T(8,128)(2,1)S(1)}, u32[]{:S(2)}, u32[]{:S(2)}) async-start(bf16[32,64,128]{2,1,0:T(8,128)(2,1)} %get-tuple-element.27), calls=%async_computation | async-start | bytes 1048576 | tf_op jit(solution)/shard_map/all_to_all | solution.py:38
  40.1 106.8 %collective-permute-start = (bf16[256,2048]{1,0:T(8,128)(2,1)}, bf16[256,2048]{1,0:T(8,128)(2,1)}, u32[]{:S(2)}, u32[]{:S(2)}) collective-permute-start(bf16[256,2048]{1,0:T(8,128)(2,1)} %get-tuple-element.22), channel_id=1, source_target_pairs={{0,24},{8,0},{16,8},{24,16},{1,25},{9,1},{17,9},{25,17},{2,26},{10... | collective-permute-start | bytes 3145736 | tf_op jit(solution)/shard_map/ppermute | solution.py:26
  61.2 16.4 %all-to-all-start.2 = ((bf16[32,32,128]{2,1,0:T(8,128)(2,1)}), bf16[32,32,128]{2,1,0:T(8,128)(2,1)S(1)}, u32[]{:S(2)}, u32[]{:S(2)}) async-start(bf16[32,32,128]{2,1,0:T(8,128)(2,1)} %get-tuple-element.33), calls=%async_computation.2 | async-start | bytes 524288 | tf_op jit(solution)/shard_map/all_to_all | solution.py:38
  70.3 10.0 %collective-permute-start.17 = (bf16[256,128]{1,0:T(8,128)(2,1)S(1)}, bf16[256,128]{1,0:T(8,128)(2,1)S(1)}, u32[]{:S(2)}, u32[]{:S(2)}) collective-permute-start(bf16[256,128]{1,0:T(8,128)(2,1)S(1)} %get-tuple-element.56), channel_id=1, source_target_pairs={{64,0},{128,64},{192,128},{65,1},{129,65},{193,129},{66,2},{130,66... | collective-permute-start | bytes 196616 | tf_op jit(solution)/shard_map/ppermute | solution.py:30
  71.6 10.1 %collective-permute-start.18 = (bf16[256,128]{1,0:T(8,128)(2,1)S(1)}, bf16[256,128]{1,0:T(8,128)(2,1)S(1)}, u32[]{:S(2)}, u32[]{:S(2)}) collective-permute-start(bf16[256,128]{1,0:T(8,128)(2,1)S(1)} %get-tuple-element.56), channel_id=1, source_target_pairs={{128,0},{192,64},{129,1},{193,65},{130,2},{194,66},{131,3},{195,67... | collective-permute-start | bytes 196616 | tf_op jit(solution)/shard_map/ppermute | solution.py:30
  77.6 15.7 %collective-permute-start.13 = (bf16[768,128]{1,0:T(8,128)(2,1)S(1)}, bf16[768,128]{1,0:T(8,128)(2,1)S(1)}, u32[]{:S(2)}, u32[]{:S(2)}) collective-permute-start(bf16[768,128]{1,0:T(8,128)(2,1)S(1)} %bitcast.60), channel_id=1, source_target_pairs={{64,0},{128,64},{192,128},{65,1},{129,65},{193,129},{66,2},{130,66... | collective-permute-start | bytes 589832 | tf_op jit(solution)/shard_map/ppermute | solution.py:30
  79.0 14.3 %collective-permute-start.14 = (bf16[512,128]{1,0:T(8,128)(2,1)S(1)}, bf16[512,128]{1,0:T(8,128)(2,1)S(1)}, u32[]{:S(2)}, u32[]{:S(2)}) collective-permute-start(bf16[512,128]{1,0:T(8,128)(2,1)S(1)} %bitcast.61), channel_id=1, source_target_pairs={{128,0},{192,64},{129,1},{193,65},{130,2},{194,66},{131,3},{195,67... | collective-permute-start | bytes 393224 | tf_op jit(solution)/shard_map/ppermute | solution.py:30
  80.3 10.0 %collective-permute-start.19 = (bf16[256,128]{1,0:T(8,128)(2,1)S(1)}, bf16[256,128]{1,0:T(8,128)(2,1)S(1)}, u32[]{:S(2)}, u32[]{:S(2)}) collective-permute-start(bf16[256,128]{1,0:T(8,128)(2,1)S(1)} %get-tuple-element.56), channel_id=1, source_target_pairs={{192,0},{193,1},{194,2},{195,3},{196,4},{197,5},{198,6},{199,7},{2... | collective-permute-start | bytes 196616 | tf_op jit(solution)/shard_map/ppermute | solution.py:30
  82.3 9.4 %collective-permute-start.15 = (bf16[256,128]{1,0:T(8,128)(2,1)S(1)}, bf16[256,128]{1,0:T(8,128)(2,1)S(1)}, u32[]{:S(2)}, u32[]{:S(2)}) collective-permute-start(bf16[256,128]{1,0:T(8,128)(2,1)S(1)} %bitcast.62), channel_id=1, source_target_pairs={{192,0},{193,1},{194,2},{195,3},{196,4},{197,5},{198,6},{199,7},{2... | collective-permute-start | bytes 196616 | tf_op jit(solution)/shard_map/ppermute | solution.py:30
  90.3 57.9 %collective-permute-start.8 = (bf16[256,2048]{1,0:T(8,128)(2,1)}, bf16[256,2048]{1,0:T(8,128)(2,1)}, u32[]{:S(2)}, u32[]{:S(2)}) collective-permute-start(bf16[256,2048]{1,0:T(8,128)(2,1)} %get-tuple-element.26), channel_id=1, source_target_pairs={{0,8},{8,16},{16,24},{24,0},{1,9},{9,17},{17,25},{25,1},{2,10},{10... | collective-permute-start | bytes 3145736 | tf_op jit(solution)/shard_map/ppermute | solution.py:26
  91.7 56.5 %collective-permute-start.7 = (bf16[256,2048]{1,0:T(8,128)(2,1)}, bf16[256,2048]{1,0:T(8,128)(2,1)}, u32[]{:S(2)}, u32[]{:S(2)}) collective-permute-start(bf16[256,2048]{1,0:T(8,128)(2,1)} %constant_dynamic-slice_fusion), channel_id=1, source_target_pairs={{0,16},{8,24},{16,0},{24,8},{1,17},{9,25},{17,1},{25,9},{2,18},{10... | collective-permute-start | bytes 3145736 | tf_op jit(solution)/shard_map/ppermute | solution.py:26
  93.3 6.2 %collective-permute-start.10 = (bf16[512,128]{1,0:T(8,128)(2,1)S(1)}, bf16[512,128]{1,0:T(8,128)(2,1)S(1)}, u32[]{:S(2)}, u32[]{:S(2)}) collective-permute-start(bf16[512,128]{1,0:T(8,128)(2,1)S(1)} %pad_maximum_fusion.8.a_ref), channel_id=1, source_target_pairs={{0,192},{64,0},{128,64},{192,128},{1,193},{65,1},{129,65},{193,129... | collective-permute-start | bytes 393224 | tf_op jit(solution)/shard_map/ppermute | solution.py:26
  93.3 6.7 %collective-permute-start.11 = (bf16[512,128]{1,0:T(8,128)(2,1)S(1)}, bf16[512,128]{1,0:T(8,128)(2,1)S(1)}, u32[]{:S(2)}, u32[]{:S(2)}) collective-permute-start(bf16[512,128]{1,0:T(8,128)(2,1)S(1)} %pad_maximum_fusion.8.a_ref), channel_id=1, source_target_pairs={{0,128},{64,192},{128,0},{192,64},{1,129},{65,193},{129,1},{193,65... | collective-permute-start | bytes 393224 | tf_op jit(solution)/shard_map/ppermute | solution.py:26
  99.4 40.3 %collective-permute-start.16 = (bf16[2560,128]{1,0:T(8,128)(2,1)S(1)}, bf16[2560,128]{1,0:T(8,128)(2,1)}, u32[]{:S(2)}, u32[]{:S(2)}) collective-permute-start(bf16[2560,128]{1,0:T(8,128)(2,1)S(1)} %pad_maximum_fusion.own_ref), channel_id=1, source_target_pairs={{0,32},{32,0},{1,33},{33,1},{2,34},{34,2},{3,35},{35,3},{4,36},{36... | collective-permute-start | bytes 1966088 | tf_op jit(solution)/shard_map/ppermute | solution.py:34
  100.0 6.6 %collective-permute-start.12 = (bf16[512,128]{1,0:T(8,128)(2,1)S(1)}, bf16[512,128]{1,0:T(8,128)(2,1)}, u32[]{:S(2)}, u32[]{:S(2)}) collective-permute-start(bf16[512,128]{1,0:T(8,128)(2,1)S(1)} %pad_maximum_fusion.8.a_ref), channel_id=1, source_target_pairs={{0,64},{64,128},{128,192},{192,0},{1,65},{65,129},{129,193},{193,1... | collective-permute-start | bytes 393224 | tf_op jit(solution)/shard_map/ppermute | solution.py:26
  106.7 11.1 %collective-permute-start.20 = (bf16[4,256,128]{2,1,0:T(8,128)(2,1)S(1)}, bf16[4,256,128]{2,1,0:T(8,128)(2,1)S(1)}, u32[]{:S(2)}, u32[]{:S(2)}) collective-permute-start(bf16[4,256,128]{2,1,0:T(8,128)(2,1)S(1)} %pad_maximum_fusion.7.slope_own_ref), channel_id=1, source_target_pairs={{0,32},{32,0},{1,33},{33,1},{2,34},{34,2},{3,35},{35,3},{4,36},{36... | collective-permute-start | bytes 786440 | tf_op jit(solution)/shard_map/ppermute | solution.py:34
  109.8 30.0 %all-to-all-start.1 = ((bf16[32,16,128]{2,1,0:T(8,128)(2,1)}), bf16[32,16,128]{2,1,0:T(8,128)(2,1)S(1)}, u32[]{:S(2)}, u32[]{:S(2)}) async-start(bf16[32,16,128]{2,1,0:T(8,128)(2,1)} %get-tuple-element.30), calls=%async_computation.1 | async-start | bytes 262144 | tf_op jit(solution)/shard_map/all_to_all | solution.py:38
  146.4 7.7 %collective-permute-start.22 = (bf16[512,128]{1,0:T(8,128)(2,1)}, bf16[512,128]{1,0:T(8,128)(2,1)S(1)}, u32[]{:S(2)}, u32[]{:S(2)}) collective-permute-start(bf16[512,128]{1,0:T(8,128)(2,1)} %get-tuple-element.37), channel_id=1, source_target_pairs={{0,16},{8,24},{16,0},{24,8},{1,17},{9,25},{17,1},{25,9},{2,18},{10... | collective-permute-start | bytes 393224 | tf_op jit(solution)/shard_map/ppermute | solution.py:26
  146.9 8.1 %collective-permute-start.23 = (bf16[512,128]{1,0:T(8,128)(2,1)}, bf16[512,128]{1,0:T(8,128)(2,1)S(1)}, u32[]{:S(2)}, u32[]{:S(2)}) collective-permute-start(bf16[512,128]{1,0:T(8,128)(2,1)} %get-tuple-element.38), channel_id=1, source_target_pairs={{0,8},{8,16},{16,24},{24,0},{1,9},{9,17},{17,25},{25,1},{2,10},{10... | collective-permute-start | bytes 393224 | tf_op jit(solution)/shard_map/ppermute | solution.py:26
  184.3 16.1 %all-to-all-start.4 = ((bf16[32,32,128]{2,1,0:T(8,128)(2,1)}), bf16[32,32,128]{2,1,0:T(8,128)(2,1)S(1)}, u32[]{:S(2)}, u32[]{:S(2)}) async-start(bf16[32,32,128]{2,1,0:T(8,128)(2,1)} %broadcast_in_dim.18), calls=%async_computation.4 | async-start | bytes 524288 | tf_op jit(solution)/shard_map/all_to_all | solution.py:38
  (26 other events, 277.7 us)
